TPU v7x, 32 devices: a whole 2x2x4 slice. The times are simulated.
32 devices in a mesh: dp: 4 (over y, x), row: 4 (over z), col: 2 (over core).
Axes of the slice: x: 2, y: 2, z: 4, core: 2. Of those that a mesh axis runs over, the one named last changes fastest.
Arguments:
- tokens: bfloat16 [32768, 1024], P(('dp', 'row'), 'col')
- cotangent: bfloat16 [32768, 1024], P(('dp', 'row'), 'col'), may hold values from -6 to 6
- seq_lens: int32 [4, 2], replicated, may hold values from 2200 to 4096, as said below
- norm1_gain: bfloat16 [1024], P('col'), may hold values from 0.25 to 1.75
- in_weight: bfloat16 [3, 1024, 1024], P(None, 'col', 'row'), may hold values from -0.1875 to 0.1875
- conv_weight: bfloat16 [3, 1024], P(None, 'row'), may hold values from -3.5 to 3.5
- out_weight: bfloat16 [1024, 1024], P('row', 'col'), may hold values from -0.1875 to 0.1875
- norm2_gain: bfloat16 [1024], P('col'), may hold values from 0.25 to 1.75
- gate_up_weight: bfloat16 [2, 1024, 4608], P(None, 'col', 'row'), may hold values from -0.1875 to 0.1875
- down_weight: bfloat16 [4608, 1024], P('row', 'col'), may hold values from -0.09375 to 0.09375
Outputs:
- output: bfloat16 [32768, 1024], P(('dp', 'row'), 'col')
- input_grad: bfloat16 [32768, 1024], P(('dp', 'row'), 'col')
- norm1_gain_grad: float32 [1024], P('col')
- in_weight_grad: float32 [3, 1024, 1024], P(None, 'col', 'row')
- conv_weight_grad: float32 [3, 1024], P(None, 'row')
- out_weight_grad: float32 [1024, 1024], P('row', 'col')
- norm2_gain_grad: float32 [1024], P('col')
- gate_up_weight_grad: float32 [2, 1024, 4608], P(None, 'col', 'row')
- down_weight_grad: float32 [4608, 1024], P('row', 'col')
Inputs may be any that keep to these rules, and one draw needn't show every extreme that they name: Each packed row of 8192 slots holds two sequences back to back from its first slot, of lengths seq_lens[q, 0] and seq_lens[q, 1], then padding; some row holds a sequence of 4096 tokens.
All inputs are finite; a program needn't handle non-finite values.
Results may differ from a plain program's by a relative error of at most 0.0085.
Values may be sent and summed in bfloat16 or wider, within the bound.
No kernel may reach another device: no remote copies, remote signals or barrier semaphores. Data moves between devices by JAX's collectives and lax.ppermute only.
A program may use at most 320 MiB of HBM per device.

v0:
```python
import jax
import jax.numpy as jnp
from jax import lax
from jax.sharding import PartitionSpec as P

KCONV = 3
ROW_LEN = 8192


eps = 1e-05


def from_behind(value, axis, steps):
    count = lax.axis_size(axis)
    leading, last = (max(0, -steps), min(count, count - steps))
    return lax.ppermute(value, axis, [(source, source + steps) for source in range(leading, last)])


def token_index(count, extra):
    flat_rank = (
        lax.axis_index("dp") * lax.axis_size("row") + lax.axis_index("row")
    ) * lax.axis_size("col") + lax.axis_index("col")
    return flat_rank * count + jnp.arange(count + extra, dtype=jnp.int32)


def slot_masks(seq_lens, count, extra):
    position = token_index(count, extra)
    packed = position // ROW_LEN
    place = position - packed * ROW_LEN
    table = (packed[:, None] == jnp.arange(seq_lens.shape[0], dtype=jnp.int32)[None, :]).astype(
        jnp.int32
    )
    first = jnp.sum(table * seq_lens[None, :, 0], axis=1)
    second = jnp.sum(table * seq_lens[None, :, 1], axis=1)
    start = jnp.where(place < first, 0, first)
    valid_slot = (place < first + second).astype(jnp.float32)
    keep_masks = jnp.stack([(place - lag >= start).astype(jnp.float32) for lag in range(KCONV)])
    return (valid_slot[:count], keep_masks)


def collect(
    norm1_gain, in_weight, conv_weight, out_weight, norm2_gain, gate_up_weight, down_weight
):
    in_rows, conv_full, out_rows, gate_rows, down_rows = (
        lax.all_gather(in_weight, "row", axis=2, tiled=True),
        lax.all_gather(conv_weight, "row", axis=1, tiled=True),
        lax.all_gather(out_weight, "row", axis=0, tiled=True),
        lax.all_gather(gate_up_weight, "row", axis=2, tiled=True),
        lax.all_gather(down_weight, "row", axis=0, tiled=True),
    )
    gain_first, in_full, out_full, gain_second, gate_full, down_full = (
        lax.all_gather(norm1_gain, "col", axis=0, tiled=True),
        lax.all_gather(in_rows, "col", axis=1, tiled=True),
        lax.all_gather(out_rows, "col", axis=1, tiled=True),
        lax.all_gather(norm2_gain, "col", axis=0, tiled=True),
        lax.all_gather(gate_rows, "col", axis=1, tiled=True),
        lax.all_gather(down_rows, "col", axis=1, tiled=True),
    )
    return (gain_first, in_full, conv_full, out_full, gain_second, gate_full, down_full)


def norm_backward(values, rstd, gain, grad_normed):
    scaled = grad_normed * gain
    gain_grad = jnp.sum(grad_normed * values * rstd, axis=0)
    grad_values = rstd * scaled - values * (rstd * rstd * rstd) * jnp.mean(
        scaled * values, axis=1, keepdims=True
    )
    return (grad_values, gain_grad)


def project(left, right):
    return jnp.dot(left, right, preferred_element_type=jnp.float32)


def weight_grad(left, right):
    return jnp.einsum("td,te->de", left, right, preferred_element_type=jnp.float32)


def back_project(grad, matrix):
    return jnp.einsum("te,de->td", grad, matrix, preferred_element_type=jnp.float32)


def shards(
    tokens,
    cotangent,
    seq_lens,
    norm1_gain,
    in_weight,
    conv_weight,
    out_weight,
    norm2_gain,
    gate_up_weight,
    down_weight,
):
    own_tokens, own_cotangent = (
        lax.all_to_all(tokens, "col", split_axis=0, concat_axis=1, tiled=True),
        lax.all_to_all(cotangent, "col", split_axis=0, concat_axis=1, tiled=True),
    )
    gain_first, in_full, conv_full, out_full, gain_second, gate_full, down_full = collect(
        norm1_gain, in_weight, conv_weight, out_weight, norm2_gain, gate_up_weight, down_weight
    )
    count, width = own_tokens.shape
    reach = KCONV - 1
    valid_slot, keep_masks = slot_masks(seq_lens, count, reach)
    conv_taps = conv_full.astype(jnp.float32)
    gain_one_f = gain_first.astype(jnp.float32)
    gain_two_f = gain_second.astype(jnp.float32)
    inputs = own_tokens.astype(jnp.float32)
    rstd_first = lax.rsqrt(jnp.mean(inputs * inputs, axis=1, keepdims=True) + eps)
    normed = (inputs * rstd_first * gain_one_f).astype(jnp.bfloat16)
    gate_b = project(normed, in_full[0])
    gate_c = project(normed, in_full[1])
    value_part = project(normed, in_full[2])
    product = gate_b * value_part
    earlier = from_behind(product[count - reach :], ("row", "col"), 1)
    extended = jnp.concatenate([earlier, product], axis=0)
    conv = jnp.zeros((count, width), jnp.float32)
    for lag in range(KCONV):
        conv = (
            conv
            + conv_taps[lag]
            * keep_masks[lag, :count, None]
            * extended[reach - lag : reach - lag + count]
        )
    carried = (gate_c * conv).astype(jnp.bfloat16)
    hidden = inputs + project(carried, out_full)
    rstd_second = lax.rsqrt(jnp.mean(hidden * hidden, axis=1, keepdims=True) + eps)
    normed_two = (hidden * rstd_second * gain_two_f).astype(jnp.bfloat16)
    gate = project(normed_two, gate_full[0])
    up_part = project(normed_two, gate_full[1])
    sigmoid_gate = jax.nn.sigmoid(gate)
    silu_gate = gate * sigmoid_gate
    active = (silu_gate * up_part).astype(jnp.bfloat16)
    output = hidden + project(active, down_full)
    grad_out = own_cotangent.astype(jnp.float32) * valid_slot[:, None]
    grad_low = grad_out.astype(jnp.bfloat16)
    down_grad = weight_grad(active, grad_low)
    grad_active = back_project(grad_low, down_full)
    grad_gate = (grad_active * up_part * sigmoid_gate * (1.0 + gate * (1.0 - sigmoid_gate))).astype(
        jnp.bfloat16
    )
    grad_up = (grad_active * silu_gate).astype(jnp.bfloat16)
    gate_grad = jnp.stack([weight_grad(normed_two, grad_gate), weight_grad(normed_two, grad_up)])
    grad_normed_two = back_project(grad_gate, gate_full[0]) + back_project(grad_up, gate_full[1])
    grad_second, gain_second_part = norm_backward(hidden, rstd_second, gain_two_f, grad_normed_two)
    grad_hidden = grad_out + grad_second
    grad_o = grad_hidden.astype(jnp.bfloat16)
    out_grad = weight_grad(carried, grad_o)
    grad_carried = back_project(grad_o, out_full)
    grad_gate_c = (grad_carried * conv).astype(jnp.bfloat16)
    grad_conv = grad_carried * gate_c
    later = from_behind(grad_conv[:reach], ("row", "col"), -1)
    grad_extended = jnp.concatenate([grad_conv, later], axis=0)
    grad_product = jnp.zeros((count, width), jnp.float32)
    conv_rows = []
    for lag in range(KCONV):
        masked = keep_masks[lag, :, None] * grad_extended
        grad_product = grad_product + conv_taps[lag] * masked[lag : lag + count]
        conv_rows.append(
            jnp.sum(masked[:count] * extended[reach - lag : reach - lag + count], axis=0)
        )
    conv_grad = jnp.stack(conv_rows)
    grad_gate_b = (grad_product * value_part).astype(jnp.bfloat16)
    grad_value = (grad_product * gate_b).astype(jnp.bfloat16)
    in_grad = jnp.stack(
        [
            weight_grad(normed, grad_gate_b),
            weight_grad(normed, grad_gate_c),
            weight_grad(normed, grad_value),
        ]
    )
    grad_normed = (
        back_project(grad_gate_b, in_full[0])
        + back_project(grad_gate_c, in_full[1])
        + back_project(grad_value, in_full[2])
    )
    grad_first, gain_first_part = norm_backward(inputs, rstd_first, gain_one_f, grad_normed)
    input_grad = (grad_hidden + grad_first).astype(jnp.bfloat16)
    output_back, input_back = (
        lax.all_to_all(output.astype(jnp.bfloat16), "col", split_axis=1, concat_axis=0, tiled=True),
        lax.all_to_all(input_grad, "col", split_axis=1, concat_axis=0, tiled=True),
    )
    in_cols, out_cols, gate_cols, down_cols = (
        lax.psum_scatter(in_grad, "col", scatter_dimension=1, tiled=True),
        lax.psum_scatter(out_grad, "col", scatter_dimension=1, tiled=True),
        lax.psum_scatter(gate_grad, "col", scatter_dimension=1, tiled=True),
        lax.psum_scatter(down_grad, "col", scatter_dimension=1, tiled=True),
    )
    in_part, out_part, gate_part, down_part = (
        lax.psum_scatter(in_cols, "row", scatter_dimension=2, tiled=True),
        lax.psum_scatter(out_cols, "row", scatter_dimension=0, tiled=True),
        lax.psum_scatter(gate_cols, "row", scatter_dimension=2, tiled=True),
        lax.psum_scatter(down_cols, "row", scatter_dimension=0, tiled=True),
    )
    in_sum, out_sum, gate_sum, down_sum = lax.psum((in_part, out_part, gate_part, down_part), "dp")
    gain_one_sum, gain_two_sum, conv_sum = lax.psum(
        (gain_first_part, gain_second_part, conv_grad), ("dp", "row", "col")
    )
    col_width = width // lax.axis_size("col")
    row_width = width // lax.axis_size("row")
    gain_first_grad = lax.dynamic_slice_in_dim(
        gain_one_sum, lax.axis_index("col") * col_width, col_width
    )
    gain_second_grad = lax.dynamic_slice_in_dim(
        gain_two_sum, lax.axis_index("col") * col_width, col_width
    )
    conv_weight_grad = lax.dynamic_slice_in_dim(
        conv_sum, lax.axis_index("row") * row_width, row_width, axis=1
    )
    return (
        output_back,
        input_back,
        gain_first_grad,
        in_sum,
        conv_weight_grad,
        out_sum,
        gain_second_grad,
        gate_sum,
        down_sum,
    )


def solution(mesh):
    return jax.shard_map(
        shards,
        mesh=mesh,
        in_specs=(
            P(("dp", "row"), "col"),
            P(("dp", "row"), "col"),
            P(),
            P("col"),
            P(None, "col", "row"),
            P(None, "row"),
            P("row", "col"),
            P("col"),
            P(None, "col", "row"),
            P("row", "col"),
        ),
        out_specs=(
            P(("dp", "row"), "col"),
            P(("dp", "row"), "col"),
            P("col"),
            P(None, "col", "row"),
            P(None, "row"),
            P("row", "col"),
            P("col"),
            P(None, "col", "row"),
            P("row", "col"),
        ),
        check_vma=False,
    )
```

profile of v0, /device:TPU:0, one launch (start us, length us, event | category | flops | bytes accessed | tf_op | source)
XLA Modules:
  0.0 1570.2 jit_solution(612322937045015688)
XLA Ops:
  10.0 65.7 %all-gather.11.cloned.1.call-done = bf16[3,512,1024]{2,1,0:T(8,128)(2,1)} async-done(((bf16[3,512,256]{2,1,0:T(8,128)(2,1)}), bf16[3,512,1024]{2,1,0:T(8,128)(2,1)}) %all-gather.11.cloned.1.call-update) | async-done | bytes 3145744 | tf_op jit(solution)/shard_map/all_gather | solution.py:45
  75.8 27.6 %all-gather.15.cloned.1.call-done = bf16[1024,512]{1,0:T(8,128)(2,1)} async-done(((bf16[256,512]{1,0:T(8,128)(2,1)}), bf16[1024,512]{1,0:T(8,128)(2,1)}) %all-gather.15.cloned.1.call-update) | async-done | bytes 1048592 | tf_op jit(solution)/shard_map/all_gather | solution.py:47
  103.5 167.8 %all-gather.19.cloned.1.call-done = bf16[2,512,4608]{2,1,0:T(8,128)(2,1)} async-done(((bf16[2,512,1152]{2,1,0:T(8,128)(2,1)}), bf16[2,512,4608]{2,1,0:T(8,128)(2,1)}) %all-gather.19.cloned.1.call-update) | async-done | bytes 9437200 | tf_op jit(solution)/shard_map/all_gather | solution.py:48
  285.9 12.2 all_gather.36
  306.9 53.7 %all-gather.23.cloned.1.call-done = bf16[4608,512]{1,0:T(8,128)(2,1)} async-done(((bf16[1152,512]{1,0:T(8,128)(2,1)}), bf16[4608,512]{1,0:T(8,128)(2,1)}) %all-gather.23.cloned.1.call-update) | async-done | bytes 4718608 | tf_op jit(solution)/shard_map/all_gather | solution.py:49
  364.1 13.0 all-gather.13.cloned.1.call-done
  393.8 6.3 multiply_convert_fusion.7
  400.1 5.6 multiply_reduce_fusion.3
  409.2 18.4 %all-gather.21.cloned.1.call-done = bf16[2,1024,4608]{2,1,0:T(8,128)(2,1)} async-done(((bf16[2,512,4608]{2,1,0:T(8,128)(2,1)}), bf16[2,1024,4608]{2,1,0:T(8,128)(2,1)}) %all-gather.21.cloned.1.call-update) | async-done | bytes 18874384 | tf_op jit(solution)/shard_map/all_gather | solution.py:56
  427.6 17.2 %fusion.2 = f32[1024,4608]{1,0:T(8,128)} fusion(bf16[1024,1024]{0,1:T(8,128)(2,1)S(1)} %multiply_convert_fusion.6, bf16[2,1024,4608]{2,1,0:T(8,128)(2,1)} %all-gather.21.cloned.1.call-done), kind=kOutput, calls=%fused_computation.12 | convolution fusion | flops 9663676416 | bytes 30408704 | tf_op jit(solution)/shard_map/dot_general | solution.py:72
  444.8 18.8 %fusion.4 = f32[1024,4608]{1,0:T(8,128)} fusion(bf16[1024,1024]{0,1:T(8,128)(2,1)} %copy-done.18, bf16[2,1024,4608]{2,1,0:T(8,128)(2,1)} %all-gather.21.cloned.1.call-done), kind=kOutput, calls=%fused_computation.14 | convolution fusion | flops 9663676416 | bytes 30408704 | tf_op jit(solution)/shard_map/dot_general | solution.py:72
  463.6 31.2 %multiply_convert_fusion = (bf16[1024,4608]{1,0:T(8,128)(2,1)}, bf16[1024,4608]{1,0:T(8,128)(2,1)}, bf16[1024,4608]{1,0:T(8,128)(2,1)}) fusion(f32[1024,4608]{1,0:T(8,128)} %fusion.2, f32[1024,4608]{1,0:T(8,128)} %fusion.4, bf16[1024,1024]{0,1:T(8,128)(2,1)S(1)} %copy-done.15, bf16[4608,1024]{1,0:T(8,128)(2,1)} %all-gather.25.cloned.1.call-done), kind=kOutput, calls=%fused_computation.1 | convolution fusion | flops 9734455296 | bytes 77594624 | tf_op jit(solution)/shard_map/te,de->td/dot_general | solution.py:80
  494.9 16.0 %fusion.1 = f32[1024,1024]{0,1:T(8,128)} fusion(bf16[1024,4608]{1,0:T(8,128)(2,1)} %get-tuple-element.30, bf16[2,1024,4608]{2,1,0:T(8,128)(2,1)} %all-gather.21.cloned.1.call-done), kind=kOutput, calls=%fused_computation.11 | convolution fusion | flops 9663676416 | bytes 23068672 | tf_op jit(solution)/shard_map/te,de->td/dot_general | solution.py:80
  510.9 17.2 %multiply_reduce_fusion = (f32[1024]{0:T(1024)}, f32[1024]{0:T(1024)S(1)}, f32[1024,1024]{0,1:T(8,128)S(1)}) fusion(f32[1024,1024]{0,1:T(8,128)S(1)} %copy-done.8, f32[1024]{0:T(1024)S(1)} %get-tuple-element.51, f32[1024]{0:T(1024)S(1)} %bitcast.145, f32[1024,1024]{0,1:T(8,128)} %fusion.1, bf16[1024,4608]{1,0:T(8,128)(2,1)} %get-tuple-element.29, ...), kind=kOutput, calls=%fused_computation.51 | convolution fusion | flops 9671014400 | bytes 31473664 | tf_op jit(solution)/shard_map/te,de->td/dot_general | solution.py:80
  547.1 6.5 fusion.28
  557.1 7.3 fusion.9
  572.9 7.7 fusion.21
  594.0 18.6 %fusion.46 = f32[4608,1024]{1,0:T(8,128)} fusion(bf16[1024,4608]{1,0:T(8,128)(2,1)} %get-tuple-element.31, bf16[1024,1024]{0,1:T(8,128)(2,1)S(1)} %copy-done.16), kind=kOutput, calls=%fused_computation.127 | convolution fusion | flops 9663676416 | bytes 30408704 | tf_op jit(solution)/shard_map/td,te->de/dot_general | solution.py:76
  614.4 12.7 convolution_bitcast_fusion
  627.1 19.4 %convolution_bitcast_fusion.1 = f32[1,1024,4608]{2,1,0:T(8,128)} fusion(bf16[1024,1024]{0,1:T(8,128)(2,1)S(1)} %copy-done.19, bf16[1024,4608]{1,0:T(8,128)(2,1)} %get-tuple-element.30), kind=kOutput, calls=%fused_computation.8 | convolution fusion | flops 9663676416 | bytes 30408704 | tf_op jit(solution)/shard_map/td,te->de/dot_general | solution.py:76
  646.5 21.1 %pad_maximum_fusion = f32[2,1024,4608]{2,1,0:T(8,128)} fusion(f32[1,1024,4608]{2,1,0:T(8,128)S(1)} %convolution_bitcast_fusion, f32[1,1024,4608]{2,1,0:T(8,128)} %convolution_bitcast_fusion.1), kind=kLoop, calls=%fused_computation | loop fusion | flops 9437184 | bytes 75497472 | tf_op jit(solution)/shard_map/stack | solution.py:143
  669.6 48.9 %reduce-scatter.17.cloned.1.call-done = f32[2,512,4608]{2,1,0:T(8,128)} async-done(((f32[2,1024,4608]{2,1,0:T(8,128)}), f32[2,512,4608]{2,1,0:T(8,128)}) %reduce-scatter.17.cloned.1.call-update) | async-done | bytes 18874384 | tf_op jit(solution)/shard_map/reduce_scatter | solution.py:186
  718.5 47.5 %reduce-scatter.15.cloned.1.call-done = f32[256,512]{1,0:T(8,128)} async-done(((f32[1024,512]{1,0:T(8,128)}), f32[256,512]{1,0:T(8,128)}) %reduce-scatter.15.cloned.1.call-update) | async-done | bytes 524304 | tf_op jit(solution)/shard_map/reduce_scatter | solution.py:191
  766.1 112.3 %reduce-scatter.11.cloned.1.call-done = f32[3,512,256]{2,1,0:T(8,128)} async-done(((f32[3,512,1024]{2,1,0:T(8,128)}), f32[3,512,256]{2,1,0:T(8,128)}) %reduce-scatter.11.cloned.1.call-update) | async-done | bytes 1572880 | tf_op jit(solution)/shard_map/reduce_scatter | solution.py:190
  878.3 164.1 %reduce-scatter.23.cloned.1.call-done = f32[1152,512]{1,0:T(8,128)} async-done(((f32[4608,512]{1,0:T(8,128)}), f32[1152,512]{1,0:T(8,128)}) %reduce-scatter.23.cloned.1.call-update) | async-done | bytes 2359312 | tf_op jit(solution)/shard_map/reduce_scatter | solution.py:193
  1042.4 316.9 %reduce-scatter.19.cloned.1.call-done = f32[2,512,1152]{2,1,0:T(8,128)} async-done(((f32[2,512,4608]{2,1,0:T(8,128)}), f32[2,512,1152]{2,1,0:T(8,128)}) %reduce-scatter.19.cloned.1.call-update) | async-done | bytes 4718608 | tf_op jit(solution)/shard_map/reduce_scatter | solution.py:192
  1359.3 17.1 %add_convert_fusion = bf16[1024,1024]{0,1:T(8,128)(2,1)} fusion(f32[1024,1024]{0,1:T(8,128)} %copy-done.7, bf16[1024,4608]{1,0:T(8,128)(2,1)} %get-tuple-element.31, bf16[4608,1024]{1,0:T(8,128)(2,1)} %all-gather.25.cloned.1.call-done), kind=kOutput, calls=%fused_computation.59 | convolution fusion | flops 9665773568 | bytes 25165824 | tf_op jit(solution)/shard_map/dot_general | solution.py:72
  1376.4 8.7 all_to_all.64
  1394.1 5.4 all_to_all.65
  1402.1 41.6 %all-reduce = (f32[1024]{0:T(1024)S(1)}, f32[3,1024]{1,0:T(4,128)S(1)}, f32[1024]{0:T(1024)S(1)}) all-reduce(f32[1024]{0:T(1024)S(1)} %copy-done.43, f32[3,1024]{1,0:T(4,128)S(1)} %pad_maximum_fusion.4, f32[1024]{0:T(1024)S(1)} %copy-done.42), channel_id=1, replica_groups=mesh['dp'=4,'row'=4,'col'=2] {'dp','row','col'}, use_global_device_ids=true, to_apply=%region_7.8 | all-reduce | flops 5120 | bytes 40960 | tf_op jit(solution)/shard_map/psum | solution.py:196
  1445.7 106.8 %all-reduce.4.cloned.1.call-done = (f32[3,512,256]{2,1,0:T(8,128)}, f32[256,512]{1,0:T(8,128)}, f32[2,512,1152]{2,1,0:T(8,128)}, f32[1152,512]{1,0:T(8,128)}) async-done(((f32[3,512,256]{2,1,0:T(8,128)}, f32[256,512]{1,0:T(8,128)}, f32[2,512,1152]{2,1,0:T(8,128)}, f32[1152,512]{1,0:T(8,128)}), (f32[3,512,256]{2,1,0:T(8,128)}, f32[256,512]{1,0:T(8,128)}, f32[2,512,1152]{2,1,0:T(8,128)}, ...) | async-done | bytes 9175056 | tf_op jit(solution)/shard_map/psum | solution.py:195
  1557.0 5.0 copy.40
  (201 shorter events, 116.7 us)
Async XLA Ops:
  7.2 68.6 %all-gather.11.cloned.1.call-start = ((), (), s32[]{:S(2)}) async-start(), calls=%async_computation.12 | async-start | bytes 3932160 | tf_op jit(solution)/shard_map/all_gather | solution.py:45
  7.9 95.5 %all-gather.15.cloned.1.call-start = ((), (), s32[]{:S(2)}) async-start(), calls=%async_computation.14 | async-start | bytes 1310720 | tf_op jit(solution)/shard_map/all_gather | solution.py:47
  8.7 262.7 %all-gather.19.cloned.1.call-start = ((), (), s32[]{:S(2)}) async-start(), calls=%async_computation.16 | async-start | bytes 11796480 | tf_op jit(solution)/shard_map/all_gather | solution.py:48
  9.4 351.2 %all-gather.23.cloned.1.call-start = ((), (), s32[]{:S(2)}) async-start(), calls=%async_computation.18 | async-start | bytes 5898240 | tf_op jit(solution)/shard_map/all_gather | solution.py:49
  10.0 367.2 %all-gather.13.cloned.1.call-start = ((), (), s32[]{:S(2)}) async-start(), calls=%async_computation.13 | async-start | bytes 9437184 | tf_op jit(solution)/shard_map/all_gather | solution.py:53
  75.8 324.4 %all-gather.17.cloned.1.call-start = ((), (), s32[]{:S(2)}) async-start(), calls=%async_computation.15 | async-start | bytes 3145728 | tf_op jit(solution)/shard_map/all_gather | solution.py:54
  103.5 324.1 %all-gather.21.cloned.1.call-start = ((), (), s32[]{:S(2)}) async-start(), calls=%async_computation.17 | async-start | bytes 28311552 | tf_op jit(solution)/shard_map/all_gather | solution.py:56
  275.3 22.8 %copy-start.47 = (s32[4,2]{0,1:T(2,128)S(1)}, s32[4,2]{0,1:T(2,128)}, u32[]{:S(2)}) copy-start(s32[4,2]{0,1:T(2,128)} %param.12) | copy-start | bytes 100
  275.3 23.0 %all-to-all-start = ((bf16[2,1024,512]{1,2,0:T(8,128)(2,1)}), bf16[2,1024,512]{1,2,0:T(8,128)(2,1)S(1)}, u32[]{:S(2)}, u32[]{:S(2)}) async-start(bf16[2,1024,512]{1,2,0:T(8,128)(2,1)} %copy.27), calls=%async_computation | async-start | bytes 4194304 | tf_op jit(solution)/shard_map/all_to_all | solution.py:96
  298.3 101.8 %copy-start = (bf16[2,1024,512]{1,2,0:T(8,128)(2,1)}, bf16[2,1024,512]{1,2,0:T(8,128)(2,1)S(1)}, u32[]{:S(2)}) copy-start(bf16[2,1024,512]{1,2,0:T(8,128)(2,1)S(1)} %all-to-all-done) | copy-start | bytes 6291460
  298.3 62.3 %all-to-all-start.2 = ((bf16[2,1024,512]{1,2,0:T(8,128)(2,1)}), bf16[2,1024,512]{1,2,0:T(8,128)(2,1)}, u32[]{:S(2)}, u32[]{:S(2)}) async-start(bf16[2,1024,512]{1,2,0:T(8,128)(2,1)} %copy.29), calls=%async_computation.2 | async-start | bytes 4194304 | tf_op jit(solution)/shard_map/all_to_all | solution.py:97
  303.2 160.4 %all-gather.25.cloned.1.call-start = ((), (), s32[]{:S(2)}) async-start(), calls=%async_computation.19 | async-start | bytes 14155776 | tf_op jit(solution)/shard_map/all_gather | solution.py:57
  304.4 88.8 %copy-start.33 = (f32[1,1024]{1,0:T(1,128)}, f32[1,1024]{1,0:T(1,128)S(1)}, u32[]{:S(2)}) copy-start(f32[1,1024]{1,0:T(1,128)S(1)} %get-tuple-element.45) | copy-start | bytes 12292
  304.4 88.8 %copy-start.35 = (f32[1,1024]{1,0:T(1,128)}, f32[1,1024]{1,0:T(1,128)S(1)}, u32[]{:S(2)}) copy-start(f32[1,1024]{1,0:T(1,128)S(1)} %get-tuple-element.46) | copy-start | bytes 12292
  304.4 88.8 %copy-start.37 = (f32[1,1024]{1,0:T(1,128)}, f32[1,1024]{1,0:T(1,128)S(1)}, u32[]{:S(2)}) copy-start(f32[1,1024]{1,0:T(1,128)S(1)} %get-tuple-element.47) | copy-start | bytes 12292
  360.6 307.1 %reduce-scatter.13.cloned.1.call-start = ((), (), s32[]{:S(2)}) async-start(), calls=%async_computation.22 | async-start | bytes 6291456 | tf_op jit(solution)/shard_map/reduce_scatter | solution.py:185
  386.6 6.6 collective-permute-start
  409.2 18.4 %copy-start.18 = (bf16[1024,1024]{0,1:T(8,128)(2,1)}, bf16[1024,1024]{0,1:T(8,128)(2,1)S(1)}, u32[]{:S(2)}) copy-start(bf16[1024,1024]{0,1:T(8,128)(2,1)S(1)} %multiply_convert_fusion.6) | copy-start | bytes 6291460
  444.8 18.8 %copy-start.15 = (bf16[1024,1024]{0,1:T(8,128)(2,1)S(1)}, bf16[1024,1024]{0,1:T(8,128)(2,1)}, u32[]{:S(2)}) copy-start(bf16[1024,1024]{0,1:T(8,128)(2,1)} %fusion.24) | copy-start | bytes 6291460
  494.9 16.1 %copy-start.8 = (f32[1024,1024]{0,1:T(8,128)S(1)}, f32[1024,1024]{0,1:T(8,128)}, u32[]{:S(2)}) copy-start(f32[1024,1024]{0,1:T(8,128)} %copy-done.7) | copy-start | bytes 12582916
  537.3 131.1 %reduce-scatter.9.cloned.1.call-start = ((), (), s32[]{:S(2)}) async-start(), calls=%async_computation.20 | async-start | bytes 18874368 | tf_op jit(solution)/shard_map/reduce_scatter | solution.py:184
  545.8 7.8 collective-permute-start.1
  592.5 76.5 %reduce-scatter.21.cloned.1.call-start = ((), (), s32[]{:S(2)}) async-start(), calls=%async_computation.26 | async-start | bytes 28311552 | tf_op jit(solution)/shard_map/reduce_scatter | solution.py:187
  612.7 105.7 %reduce-scatter.17.cloned.1.call-start = ((), (), s32[]{:S(2)}) async-start(), calls=%async_computation.24 | async-start | bytes 56623104 | tf_op jit(solution)/shard_map/reduce_scatter | solution.py:186
  667.6 98.5 %reduce-scatter.15.cloned.1.call-start = ((), (), s32[]{:S(2)}) async-start(), calls=%async_computation.23 | async-start | bytes 2621440 | tf_op jit(solution)/shard_map/reduce_scatter | solution.py:191
  668.4 210.0 %reduce-scatter.11.cloned.1.call-start = ((), (), s32[]{:S(2)}) async-start(), calls=%async_computation.21 | async-start | bytes 7864320 | tf_op jit(solution)/shard_map/reduce_scatter | solution.py:190
  668.9 373.4 %reduce-scatter.23.cloned.1.call-start = ((), (), s32[]{:S(2)}) async-start(), calls=%async_computation.27 | async-start | bytes 11796480 | tf_op jit(solution)/shard_map/reduce_scatter | solution.py:193
  669.5 689.7 %reduce-scatter.19.cloned.1.call-start = ((), (), s32[]{:S(2)}) async-start(), calls=%async_computation.25 | async-start | bytes 23592960 | tf_op jit(solution)/shard_map/reduce_scatter | solution.py:192
  718.5 834.1 %all-reduce.4.cloned.1.call-start = ((), (), s32[]{:S(2)}) async-start(), calls=%async_computation.28 | async-start | bytes 18350080 | tf_op jit(solution)/shard_map/psum | solution.py:195
  1376.4 12.7 copy-start.23
  1376.4 12.7 copy-start.26
  1376.4 12.7 copy-start.31
  (40 other events, 199.6 us)
Sparse Core Ops, SparseCore 0:
  9.6 66.1 all-gather.10
  77.3 26.1 all-gather.14
  105.0 166.2 all-gather.18
  272.8 87.7 all-gather.22
  361.9 15.1 all-gather.12
  378.5 11.7 all-gather.16
  391.9 35.6 all-gather.20
  429.2 23.0 all-gather.24
  537.4 13.2 reduce-scatter.12
  592.6 23.3 reduce-scatter.8
  618.4 29.4 reduce-scatter.20
  667.7 50.6 reduce-scatter.16
  720.8 45.1 reduce-scatter.14
  768.2 110.0 reduce-scatter.10
  880.5 161.8 reduce-scatter.22
  1044.6 314.6 reduce-scatter.18
  1363.6 188.8 all-reduce.3
where the time goes:
time: 1580 us; the launch traced here: 1570 us
  waiting for transfers between devices  1150 us (73%)
  matrix products  224 us (14%)
  blocking collectives  73.9 us (5%)
  other arithmetic  56.2 us (4%)
  local copies, waits for them, and re-layouts  41 us (3%)
    reduce_scatter x1, waiting for transfers between devices, shards(): lax.psum_scatter(gate_cols, 'row', scatter_dimension=2, tiled=True)  317 us
    all_gather x1, waiting for transfers between devices, collect(): lax.all_gather(gate_up_weight, 'row', axis=2, tiled=True)  168 us
    reduce_scatter x1, waiting for transfers between devices, shards(): lax.psum_scatter(down_cols, 'row', scatter_dimension=0, tiled=True)  164 us
    reduce_scatter x1, waiting for transfers between devices, shards(): lax.psum_scatter(in_cols, 'row', scatter_dimension=2, tiled=True)  112 us
    psum x1, waiting for transfers between devices, shards(): lax.psum((in_part, out_part, gate_part, down_part), 'dp')  107 us
    dot_general x7, matrix products, back_project(): jnp.einsum('te,de->td', grad, matrix, preferred_element_type=jnp.float32)  87.5 us
    dot_general x7, matrix products, project(): return jnp.dot(left, right, preferred_element_type=jnp.float32)  74.4 us
    all_gather x1, waiting for transfers between devices, collect(): lax.all_gather(in_weight, 'row', axis=2, tiled=True)  65.7 us
  transfers between devices with their start and end apart: 21, of which 12 were waited for; matrix products, arithmetic and copies ran while one was open for 14% of the time, Pallas kernels for 0%

commit v1 on v0

v1 whole, which is shorter than its diff:
```python
import jax
import jax.numpy as jnp
from jax import lax
from jax.sharding import PartitionSpec as P

KCONV = 3
ROW_LEN = 8192
BLOCKS = 4


eps = 1e-05
bf16 = jnp.bfloat16
f32 = jnp.float32


def dot(left, right):
    return jnp.dot(left, right, preferred_element_type=f32)


def dot_nt(left, right):
    return lax.dot_general(left, right, (((1,), (1,)), ((), ())), preferred_element_type=f32)


def dot_tn(left, right):
    return lax.dot_general(left, right, (((0,), (0,)), ((), ())), preferred_element_type=f32)


def swap_cores(value):
    return lax.ppermute(value, "col", [(0, 1), (1, 0)])


def slot_masks(seq_lens, count):
    flat_rank = (
        lax.axis_index("dp") * lax.axis_size("row") + lax.axis_index("row")
    ) * lax.axis_size("col") + lax.axis_index("col")
    position = flat_rank * count + jnp.arange(count + KCONV - 1, dtype=jnp.int32)
    packed = position // ROW_LEN
    place = position - packed * ROW_LEN
    table = (packed[:, None] == jnp.arange(seq_lens.shape[0], dtype=jnp.int32)[None, :]).astype(
        jnp.int32
    )
    first = jnp.sum(table * seq_lens[None, :, 0], axis=1)
    second = jnp.sum(table * seq_lens[None, :, 1], axis=1)
    start = jnp.where(place < first, 0, first)
    valid_slot = (place < first + second).astype(f32)
    keep_masks = jnp.stack([(place - lag >= start).astype(f32) for lag in range(KCONV)])
    return (valid_slot[:count], keep_masks)


class RingPlan:
    def __init__(self):
        dp, self.row, col = lax.axis_index("dp"), lax.axis_index("row"), lax.axis_index("col")
        low, high = dp % 2, dp // 2
        self.bit_first = jnp.where(col == 0, low, high)
        self.bit_second = jnp.where(col == 0, high, low)
        self.quarter = 2 * self.bit_second + self.bit_first

    def first(self, value):
        return lax.ppermute(
            value, ("dp", "col"), [(2 * p + c, 2 * (p ^ (1 << c)) + c) for p in range(4) for c in range(2)]
        )

    def second(self, value):
        return lax.ppermute(
            value, ("dp", "col"), [(2 * p + c, 2 * (p ^ (2 >> c)) + c) for p in range(4) for c in range(2)]
        )

    def onward(self, value):
        return lax.ppermute(value, "row", [(i, (i + 1) % BLOCKS) for i in range(BLOCKS)])

    def reorder(self, value, axis):
        width = value.shape[axis] // 4
        return jnp.concatenate(
            [
                lax.dynamic_slice_in_dim(value, (self.quarter ^ j) * width, width, axis)
                for j in range(4)
            ],
            axis,
        )

    def gather(self, own):
        own = self.reorder(own, 1)
        moving = own[:, : own.shape[1] // 4]
        halves = []
        for _ in range(BLOCKS - 1):
            moving = self.onward(moving)
            pair = jnp.concatenate([moving, self.first(moving)], axis=1)
            halves.append(jnp.concatenate([pair, self.second(pair)], axis=1))
        halves.append(own)
        return [jnp.concatenate([half, swap_cores(half)], axis=1) for half in halves]

    def reduce(self, block, running):
        half = block.shape[1] // 2
        total = block[:, :half].astype(f32) + swap_cores(block[:, half:]).astype(f32)
        total = total.astype(bf16)
        half //= 2
        total = (total[:, :half].astype(f32) + self.second(total[:, half:]).astype(f32)).astype(bf16)
        half //= 2
        total = total[:, :half].astype(f32) + self.first(total[:, half:]).astype(f32)
        if running is not None:
            total = total + self.onward(running).astype(f32)
        return total.astype(bf16)

    def spread(self, part):
        pair = jnp.concatenate([part, self.first(part)], axis=1)
        half = jnp.concatenate([pair, self.second(pair)], axis=1)
        return self.reorder(half, 1).astype(f32)

    def reduce_blocks(self, blocks):
        running = None
        for block in blocks:
            running = self.reduce(block, running)
        return self.spread(running)

    def ring_order(self, value, axis):
        width = value.shape[axis] // BLOCKS
        return jnp.concatenate(
            [
                lax.dynamic_slice_in_dim(value, (self.row - 1 - j) % BLOCKS * width, width, axis)
                for j in range(BLOCKS)
            ],
            axis,
        )

    def own_block(self, value, axis):
        width = value.shape[axis] // BLOCKS
        return lax.slice_in_dim(value, (BLOCKS - 1) * width, None, axis=axis)

    def shifted(self, value, steps):
        count = lax.axis_size("row") * lax.axis_size("col")
        pairs = [(i, i + steps) for i in range(count) if 0 <= i + steps < count]
        value = lax.ppermute(value, ("row", "col"), pairs)
        width = value.shape[1] // BLOCKS
        crossing = lax.axis_index("col") == (0 if steps > 0 else 1)
        return jnp.where(crossing, jnp.roll(value, steps * width, axis=1), value)


class FlatPlan:
    def reorder(self, value, axis):
        return value

    def gather(self, own):
        half = lax.all_gather(own, "row", axis=2, tiled=True)
        return jnp.split(jnp.concatenate([half, swap_cores(half)], axis=1), BLOCKS, axis=2)

    def reduce_blocks(self, blocks):
        block = jnp.concatenate(blocks, axis=2)
        half = block.shape[1] // 2
        total = block[:, :half].astype(f32) + swap_cores(block[:, half:]).astype(f32)
        total = lax.psum_scatter(total, "row", scatter_dimension=2, tiled=True)
        return lax.psum(total, "dp")

    def ring_order(self, value, axis):
        return value

    def own_block(self, value, axis):
        width = value.shape[axis] // lax.axis_size("row")
        return lax.dynamic_slice_in_dim(value, lax.axis_index("row") * width, width, axis)

    def shifted(self, value, steps):
        count = lax.axis_size("row") * lax.axis_size("col")
        pairs = [(i, i + steps) for i in range(count) if 0 <= i + steps < count]
        return lax.ppermute(value, ("row", "col"), pairs)


def norm_backward(values, rstd, gain, grad_normed):
    scaled = grad_normed * gain
    gain_grad = jnp.sum(grad_normed * values * rstd, axis=0)
    grad_values = rstd * scaled - values * (rstd * rstd * rstd) * jnp.mean(
        scaled * values, axis=1, keepdims=True
    )
    return (grad_values, gain_grad)


def shards(
    plan_of,
    tokens,
    cotangent,
    seq_lens,
    norm1_gain,
    in_weight,
    conv_weight,
    out_weight,
    norm2_gain,
    gate_up_weight,
    down_weight,
):
    plan = plan_of()
    core = lax.axis_index("col")
    count, half_width = tokens.shape[0] // 2, tokens.shape[1]
    reach = KCONV - 1

    def take_tokens(value):
        value = plan.reorder(value, 1)
        own = lax.dynamic_slice_in_dim(value, core * count, count, 0)
        other = lax.dynamic_slice_in_dim(value, (1 - core) * count, count, 0)
        return jnp.concatenate([own, swap_cores(other)], axis=1)

    def give_tokens(value):
        own, other = value[:, :half_width], swap_cores(value[:, half_width:])
        both = jnp.where(
            core == 0, jnp.concatenate([own, other], axis=0), jnp.concatenate([other, own], axis=0)
        )
        return plan.reorder(both, 1)

    def take_gain(gain):
        gain = plan.reorder(gain.astype(f32), 0)
        return jnp.concatenate([gain, swap_cores(gain)], axis=0)

    own_tokens = take_tokens(tokens)
    mix_weights = jnp.concatenate([in_weight, out_weight.T[None]], axis=0)
    feed_weights = jnp.concatenate([gate_up_weight, down_weight.T[None]], axis=0)
    mix_blocks = plan.gather(mix_weights)
    feed_blocks = plan.gather(feed_weights)
    own_cotangent = take_tokens(cotangent)
    gain_one, gain_two = take_gain(norm1_gain), take_gain(norm2_gain)
    taps = plan.ring_order(lax.all_gather(conv_weight.astype(f32), "row", axis=1, tiled=True), 1)
    valid_slot, keep_masks = slot_masks(seq_lens, count)

    inputs = own_tokens.astype(f32)
    rstd_first = lax.rsqrt(jnp.mean(inputs * inputs, axis=1, keepdims=True) + eps)
    normed = (inputs * rstd_first * gain_one).astype(bf16)
    mix = jnp.concatenate(mix_blocks, axis=2)
    gate_b, gate_c, value_part = dot(normed, mix[0]), dot(normed, mix[1]), dot(normed, mix[2])
    product = gate_b * value_part
    extended = jnp.concatenate([plan.shifted(product[count - reach :], 1), product], axis=0)
    conv = jnp.zeros_like(product)
    for lag in range(KCONV):
        conv = (
            conv
            + taps[lag]
            * keep_masks[lag, :count, None]
            * extended[reach - lag : reach - lag + count]
        )
    carried = (gate_c * conv).astype(bf16)
    hidden = inputs + dot_nt(carried, mix[3])
    rstd_second = lax.rsqrt(jnp.mean(hidden * hidden, axis=1, keepdims=True) + eps)
    normed_two = (hidden * rstd_second * gain_two).astype(bf16)

    grad_out = own_cotangent.astype(f32) * valid_slot[:, None]
    grad_low = grad_out.astype(bf16)
    output, grad_normed_two = hidden, jnp.zeros_like(hidden)
    feed_grads = []
    for block in feed_blocks:
        gate, up_part, grad_active = (
            dot(normed_two, block[0]),
            dot(normed_two, block[1]),
            dot(grad_low, block[2]),
        )
        sigmoid_gate = jax.nn.sigmoid(gate)
        silu_gate = gate * sigmoid_gate
        active = (silu_gate * up_part).astype(bf16)
        grad_gate = (
            grad_active * up_part * sigmoid_gate * (1.0 + gate * (1.0 - sigmoid_gate))
        ).astype(bf16)
        grad_up = (grad_active * silu_gate).astype(bf16)
        output = output + dot_nt(active, block[2])
        grad_normed_two = grad_normed_two + dot_nt(grad_gate, block[0]) + dot_nt(grad_up, block[1])
        feed_grads.append(
            jnp.stack(
                [dot_tn(normed_two, grad_gate), dot_tn(normed_two, grad_up), dot_tn(grad_low, active)]
            ).astype(bf16)
        )
    feed_sum = plan.reduce_blocks(feed_grads)
    grad_second, gain_second_part = norm_backward(hidden, rstd_second, gain_two, grad_normed_two)
    grad_hidden = grad_out + grad_second
    grad_o = grad_hidden.astype(bf16)
    grad_carried = dot(grad_o, mix[3])
    grad_gate_c = (grad_carried * conv).astype(bf16)
    grad_conv = grad_carried * gate_c
    grad_extended = jnp.concatenate([grad_conv, plan.shifted(grad_conv[:reach], -1)], axis=0)
    grad_product = jnp.zeros_like(product)
    conv_rows = []
    for lag in range(KCONV):
        masked = keep_masks[lag, :, None] * grad_extended
        grad_product = grad_product + taps[lag] * masked[lag : lag + count]
        conv_rows.append(
            jnp.sum(masked[:count] * extended[reach - lag : reach - lag + count], axis=0)
        )
    grad_gate_b = (grad_product * value_part).astype(bf16)
    grad_value = (grad_product * gate_b).astype(bf16)
    mix_grad = jnp.stack(
        [
            dot_tn(normed, grad_gate_b),
            dot_tn(normed, grad_gate_c),
            dot_tn(normed, grad_value),
            dot_tn(grad_o, carried),
        ]
    ).astype(bf16)
    mix_sum = plan.reduce_blocks(jnp.split(mix_grad, BLOCKS, axis=2))
    grad_normed = (
        dot_nt(grad_gate_b, mix[0]) + dot_nt(grad_gate_c, mix[1]) + dot_nt(grad_value, mix[2])
    )
    grad_first, gain_first_part = norm_backward(inputs, rstd_first, gain_one, grad_normed)
    input_grad = (grad_hidden + grad_first).astype(bf16)
    output_back, input_back = give_tokens(output.astype(bf16)), give_tokens(input_grad)

    def whole_gain(part):
        own = part[:half_width] + swap_cores(part[half_width:])
        return plan.reorder(own, 0)

    gain_one_sum, gain_two_sum = lax.psum(
        (whole_gain(gain_first_part), whole_gain(gain_second_part)), ("dp", "row")
    )
    conv_sum = plan.ring_order(jnp.stack(conv_rows), 1)
    conv_sum = lax.psum(conv_sum, ("dp", "row", "col"))
    block_width = conv_weight.shape[1]
    conv_grad = lax.dynamic_slice_in_dim(
        conv_sum, lax.axis_index("row") * block_width, block_width, axis=1
    )
    return (
        output_back,
        input_back,
        gain_one_sum,
        mix_sum[:3],
        conv_grad,
        mix_sum[3].T,
        gain_two_sum,
        feed_sum[:2],
        feed_sum[2].T,
    )


def solution(mesh):
    ring = mesh.shape["dp"] == 4 and mesh.shape["row"] == BLOCKS and mesh.shape["col"] == 2
    plan_of = RingPlan if ring else FlatPlan

    def local(*arrays):
        return shards(plan_of, *arrays)

    return jax.shard_map(
        local,
        mesh=mesh,
        in_specs=(
            P(("dp", "row"), "col"),
            P(("dp", "row"), "col"),
            P(),
            P("col"),
            P(None, "col", "row"),
            P(None, "row"),
            P("row", "col"),
            P("col"),
            P(None, "col", "row"),
            P("row", "col"),
        ),
        out_specs=(
            P(("dp", "row"), "col"),
            P(("dp", "row"), "col"),
            P("col"),
            P(None, "col", "row"),
            P(None, "row"),
            P("row", "col"),
            P("col"),
            P(None, "col", "row"),
            P("row", "col"),
        ),
        check_vma=False,
    )
```

time: 1580 us -> 806 us (0.51)
  waiting for transfers between devices: 1150 us -> 149 us
  other arithmetic: 56.2 us -> 131 us
  blocking collectives: 73.9 us -> 125 us
  local copies, waits for them, and re-layouts: 41 us -> 85.6 us
  starting transfers between devices: 13 us -> 52.4 us
  matrix products: 224 us -> 251 us
    reduce_scatter x8 -> x0, waiting for transfers between devices: 690 us -> none  [the longest x1 317 us: shards(): lax.psum_scatter(gate_cols, 'row', scatter_dimension=2, tiled=True)]
    all_gather x8 -> x0, waiting for transfers between devices: 346 us -> none  [the longest x1 168 us: collect(): lax.all_gather(gate_up_weight, 'row', axis=2, tiled=True)]
    ppermute x2 -> x70, waiting for transfers between devices: 0.01 us -> 149 us  [the longest x16 66.7 us: second(): lax.ppermute(value, ('dp', 'col'), [(2 * p + c, 2 * (p ^ 2 >> c) + c) for...]
    psum x1 -> x0, waiting for transfers between devices: 107 us -> none  [shards(): lax.psum((in_part, out_part, gate_part, down_part), 'dp')]
    psum x1 -> x2, blocking collectives: 41.6 us -> 96.2 us  [the longest x1 53.8 us: shards(): lax.psum((whole_gain(gain_first_part), whole_gain(gain_second_part)), ('d...]
    concatenate x0 -> x28, other arithmetic: none -> 51 us  [the longest x1 19.7 us: shards(): mix = jnp.concatenate(mix_blocks, axis=2)]
    ppermute x2 -> x70, starting transfers between devices: 3.41 us -> 52.4 us  [the longest x16 17.7 us: second(): lax.ppermute(value, ('dp', 'col'), [(2 * p + c, 2 * (p ^ 2 >> c) + c) for...]
    dot_general x21 -> x48, matrix products: 224 us -> 251 us  [the longest x16 101 us: dot_nt(): lax.dot_general(left, right, (((1,), (1,)), ((), ())), preferred_element_...]
  transfers between devices with their start and end apart: 21 -> 70, of which waited for: 12 -> 24; matrix products, arithmetic and copies ran while one was open for 14% -> 55% of each run, Pallas kernels for 0% -> 0%
where the time goes in v1:
time: 806 us; the launch traced here: 798 us
  matrix products  251 us (31%)
  waiting for transfers between devices  149 us (18%)
  other arithmetic  131 us (16%)
  blocking collectives  125 us (16%)
  local copies, waits for them, and re-layouts  85.6 us (11%)
  starting transfers between devices  52.4 us (7%)
    dot_general x16, matrix products, dot_nt(): lax.dot_general(left, right, (((1,), (1,)), ((), ())), preferred_element_...  101 us
    dot_general x16, matrix products, dot(): return jnp.dot(left, right, preferred_element_type=f32)  89.8 us
    ppermute x16, waiting for transfers between devices, second(): lax.ppermute(value, ('dp', 'col'), [(2 * p + c, 2 * (p ^ 2 >> c) + c) for...  66.7 us
    dot_general x16, matrix products, dot_tn(): lax.dot_general(left, right, (((0,), (0,)), ((), ())), preferred_element_...  60.9 us
    psum x1, blocking collectives, shards(): lax.psum((whole_gain(gain_first_part), whole_gain(gain_second_part)), ('d...  53.8 us
    ppermute x16, waiting for transfers between devices, first(): lax.ppermute(value, ('dp', 'col'), [(2 * p + c, 2 * (p ^ 1 << c) + c) for...  52.9 us
    psum x1, blocking collectives, shards(): conv_sum = lax.psum(conv_sum, ('dp', 'row', 'col'))  42.4 us
    unnamed x196, local copies, waits for them, and re-layouts  36.1 us
  transfers between devices with their start and end apart: 70, of which 24 were waited for; matrix products, arithmetic and copies ran while one was open for 55% of the time, Pallas kernels for 0%

profile of v1, /device:TPU:0, one launch (start us, length us, event | category | flops | bytes accessed | tf_op | source)
XLA Modules:
  0.0 797.9 jit_solution(152587644428049207)
XLA Ops:
  17.8 29.1 %all_gather.3 = f32[3,1024]{1,0:T(4,128)} all-gather(f32[3,256]{1,0:T(4,128)S(1)} %convert_element_type.373), channel_id=1, replica_groups=mesh['dp'=4,'row'=4,'col'=2] {'row'}, dimensions={1}, use_global_device_ids=true | all-gather | bytes 15360 | tf_op jit(solution)/shard_map/all_gather | solution.py:217
  109.6 7.9 collective-permute-done.12
  127.6 19.7 %pad_maximum_fusion = bf16[4,1024,1024]{2,1,0:T(8,128)(2,1)S(1)} fusion(bf16[4,1024,256]{2,1,0:T(8,128)(2,1)S(1)} %constant_dynamic-update-slice_fusion.1, bf16[4,512,256]{2,1,0:T(8,128)(2,1)S(1)} %collective-permute-done.13, bf16[4,256,256]{2,1,0:T(8,128)(2,1)S(1)} %collective-permute-done.12, bf16[4,128,256]{2,1,0:T(8,128)(2,1)S(1)} %collective-permute-done.11, ...), kind=kLoop, calls=%fused_computation.6 | loop fusion | flops 109051904 | bytes 16777216 | tf_op jit(solution)/shard_map/concatenate | solution.py:223
  158.2 6.7 multiply_convert_fusion.16
  176.4 14.0 %collective-permute-done.26 = bf16[3,128,1152]{2,1,0:T(8,128)(2,1)S(1)} collective-permute-done((bf16[3,128,1152]{2,1,0:T(8,128)(2,1)S(1)}, bf16[3,128,1152]{2,1,0:T(8,128)(2,1)S(1)}, u32[]{:S(2)}, u32[]{:S(2)}) %collective-permute-start.26) | collective-permute-done | bytes 884768 | tf_op jit(solution)/shard_map/ppermute | solution.py:59
  209.2 7.5 multiply_convert_fusion
  233.7 6.1 fusion.54
  255.9 6.3 fusion.37
  266.5 7.7 multiply_convert_fusion.6
  289.3 6.3 fusion.36
  295.5 6.3 fusion.38
  301.8 6.7 fusion.41
  315.6 6.4 fusion.46
  321.9 8.8 %multiply_convert_fusion.5 = (bf16[1024,1152]{1,0:T(8,128)(2,1)}, bf16[1024,1152]{1,0:T(8,128)(2,1)S(1)}, bf16[1024,1152]{1,0:T(8,128)(2,1)S(1)}) fusion(f32[1024,1152]{1,0:T(8,128)} %fusion.46, f32[1024,1152]{1,0:T(8,128)} %fusion.45, bf16[1024,1024]{1,0:T(8,128)(2,1)S(1)} %copy-done.34, bf16[3,1024,1152]{2,1,0:T(8,128)(2,1)} %copy-done.39), kind=kOutput, calls=%fused_computation.27 | convolution fusion | flops 2433613824 | bytes 20971520 | tf_op jit(solution)/shard_map/dot_general | solution.py:17
  347.7 7.1 fusion.42
  354.8 6.2 fusion.44
  361.0 6.3 fusion.47
  376.6 7.2 multiply_convert_fusion.3
  419.0 13.7 %multiply_reduce_fusion = (f32[1024]{0:T(1024)S(1)}, f32[1024]{0:T(1024)S(1)}, f32[1024,1024]{1,0:T(8,128)}) fusion(f32[1024,1024]{1,0:T(8,128)S(1)} %copy-done.1, f32[1024]{0:T(1024)S(1)} %copy-done.42, f32[1024]{0:T(1024)S(1)} %copy-done.44, bf16[1024,1152]{1,0:T(8,128)(2,1)S(1)} %copy-done.31, ...), kind=kOutput, calls=%fused_computation.66 | convolution fusion | flops 2429548544 | bytes 42483712 | tf_op jit(solution)/shard_map/dot_general | solution.py:21
  451.6 9.4 %add_convert_fusion.4 = bf16[1024,1024]{1,0:T(8,128)(2,1)S(1)} fusion(f32[1024,1024]{1,0:T(8,128)} %fusion.53, f32[1024,1024]{1,0:T(8,128)} %fusion.47, f32[1024,1024]{1,0:T(8,128)S(1)} %copy-done.1, f32[1024,1024]{1,0:T(8,128)} %fusion.41, bf16[1024,1152]{1,0:T(8,128)(2,1)} %copy-done.70, bf16[3,1024,1152]{2,1,0:T(8,128)(2,1)} %constant_dynamic-update-slice_fusion.19), kind=kOutput, calls=%fused_computation.77 | convolution fusion | flops 2421161984 | bytes 23592960 | tf_op jit(solution)/shard_map/dot_general | solution.py:21
  471.9 8.3 %fusion.18 = (f32[1024]{0:T(1024)S(1)}, f32[1024]{0:T(1024)S(1)}, f32[1024]{0:T(1024)S(1)}, bf16[1024,1024]{1,0:T(8,128)(2,1)}, f32[1024,1024]{1,0:T(8,128)}) fusion(f32[1026,1024]{1,0:T(8,128)S(1)} %get-tuple-element.96, f32[1024,1024]{1,0:T(8,128)S(1)} %copy-done.9, f32[2,1024]{1,0:T(2,128)S(1)} %copy-done.48, f32[1026,1024]{1,0:T(8,128)S(1)} %get-tuple-element.97, ...), kind=kLoop, calls=%fused_computation.60 | loop fusion | flops 19919872 | bytes 35696640 | tf_op jit(solution)/shard_map/reduce_sum | solution.py:278
  508.0 42.4 %psum.22 = f32[3,1024]{1,0:T(4,128)S(1)} all-reduce(f32[3,1024]{1,0:T(4,128)S(1)} %pad_maximum_fusion.33), channel_id=1, replica_groups=mesh['dp'=4,'row'=4,'col'=2] {'dp','row','col'}, use_global_device_ids=true, to_apply=%region_11.12 | all-reduce | flops 3072 | bytes 24576 | tf_op jit(solution)/shard_map/psum | solution.py:306
  575.9 13.1 %collective-permute-done.63 = bf16[3,256,1152]{2,1,0:T(8,128)(2,1)} collective-permute-done((bf16[3,256,1152]{2,1,0:T(8,128)(2,1)S(1)}, bf16[3,256,1152]{2,1,0:T(8,128)(2,1)}, u32[]{:S(2)}, u32[]{:S(2)}) %collective-permute-start.63) | collective-permute-done | bytes 1769504 | tf_op jit(solution)/shard_map/ppermute | solution.py:64
  593.3 24.1 %collective-permute-done.60 = bf16[3,256,1152]{2,1,0:T(8,128)(2,1)S(1)} collective-permute-done((bf16[3,256,1152]{2,1,0:T(8,128)(2,1)S(1)}, bf16[3,256,1152]{2,1,0:T(8,128)(2,1)S(1)}, u32[]{:S(2)}, u32[]{:S(2)}) %collective-permute-start.60) | collective-permute-done | bytes 1769504 | tf_op jit(solution)/shard_map/ppermute | solution.py:64
  623.2 53.8 %all-reduce = (f32[512]{0:T(512)}, f32[512]{0:T(512)}) all-reduce(f32[512]{0:T(512)S(1)} %pad_maximum_fusion.41, f32[512]{0:T(512)S(1)} %pad_maximum_fusion.42), channel_id=1, replica_groups=mesh['dp'=4,'row'=4,'col'=2] {'dp','row'}, use_global_device_ids=true, to_apply=%region_7.8 | all-reduce | flops 1024 | bytes 8192 | tf_op jit(solution)/shard_map/psum | solution.py:302
  697.0 9.1 %collective-permute-done.66 = bf16[3,128,1152]{2,1,0:T(8,128)(2,1)S(1)} collective-permute-done((bf16[3,128,1152]{2,1,0:T(8,128)(2,1)S(1)}, bf16[3,128,1152]{2,1,0:T(8,128)(2,1)S(1)}, u32[]{:S(2)}, u32[]{:S(2)}) %collective-permute-start.66) | collective-permute-done | bytes 884768 | tf_op jit(solution)/shard_map/ppermute | solution.py:69
  708.2 7.1 collective-permute-done.45
  716.0 9.0 %collective-permute-done.46 = bf16[4,128,256]{2,1,0:T(8,128)(2,1)S(1)} collective-permute-done((bf16[4,128,256]{2,1,0:T(8,128)(2,1)S(1)}, bf16[4,128,256]{2,1,0:T(8,128)(2,1)S(1)}, u32[]{:S(2)}, u32[]{:S(2)}) %collective-permute-start.46) | collective-permute-done | bytes 262176 | tf_op jit(solution)/shard_map/ppermute | solution.py:59
  740.0 7.9 collective-permute-done.40
  750.8 7.6 collective-permute-done.49
  760.1 7.7 collective-permute-done.50
  770.7 10.1 %collective-permute-done.51 = bf16[4,256,256]{2,1,0:T(8,128)(2,1)S(1)} collective-permute-done((bf16[4,256,256]{2,1,0:T(8,128)(2,1)S(1)}, bf16[4,256,256]{2,1,0:T(8,128)(2,1)S(1)}, u32[]{:S(2)}, u32[]{:S(2)}) %collective-permute-start.51) | collective-permute-done | bytes 524320 | tf_op jit(solution)/shard_map/ppermute | solution.py:64
  (513 shorter events, 405.3 us)
Async XLA Ops:
  5.1 78.8 %collective-permute-start.16 = (f32[512]{0:T(512)}, f32[512]{0:T(512)}, u32[]{:S(2)}, u32[]{:S(2)}) collective-permute-start(f32[512]{0:T(512)} %pad_maximum_fusion.40), channel_id=1, source_target_pairs={{0,1},{1,0},{2,3},{3,2},{4,5},{5,4},{6,7},{7,6},{8,9},{9,8},{10,11... | collective-permute-start | bytes 6152 | tf_op jit(solution)/shard_map/ppermute | solution.py:29
  8.5 62.7 %collective-permute-start.2 = (bf16[4,128,256]{2,1,0:T(8,128)(2,1)}, bf16[4,128,256]{2,1,0:T(8,128)(2,1)}, u32[]{:S(2)}, u32[]{:S(2)}) collective-permute-start(bf16[4,128,256]{2,1,0:T(8,128)(2,1)} %get-tuple-element.73), channel_id=1, source_target_pairs={{0,2},{2,4},{4,6},{6,0},{1,3},{3,5},{5,7},{7,1},{8,10},{10,12},{12... | collective-permute-start | bytes 786440 | tf_op jit(solution)/shard_map/ppermute | solution.py:69
  14.2 86.0 %collective-permute-start.17 = (bf16[3,128,1152]{2,1,0:T(8,128)(2,1)}, bf16[3,128,1152]{2,1,0:T(8,128)(2,1)}, u32[]{:S(2)}, u32[]{:S(2)}) collective-permute-start(bf16[3,128,1152]{2,1,0:T(8,128)(2,1)} %get-tuple-element.47), channel_id=1, source_target_pairs={{0,2},{2,4},{4,6},{6,0},{1,3},{3,5},{5,7},{7,1},{8,10},{10,12},{12... | collective-permute-start | bytes 2654216 | tf_op jit(solution)/shard_map/ppermute | solution.py:69
  85.1 33.4 %collective-permute-start.14 = (bf16[4,512,256]{2,1,0:T(8,128)(2,1)}, bf16[4,512,256]{2,1,0:T(8,128)(2,1)S(1)}, u32[]{:S(2)}, u32[]{:S(2)}) collective-permute-start(bf16[4,512,256]{2,1,0:T(8,128)(2,1)} %pad_maximum_fusion.26), channel_id=1, source_target_pairs={{0,1},{1,0},{2,3},{3,2},{4,5},{5,4},{6,7},{7,6},{8,9},{9,8},{10,11... | collective-permute-start | bytes 3145736 | tf_op jit(solution)/shard_map/ppermute | solution.py:29
  85.2 33.8 %collective-permute-start = (bf16[1024,512]{1,0:T(8,128)(2,1)}, bf16[1024,512]{1,0:T(8,128)(2,1)S(1)}, u32[]{:S(2)}, u32[]{:S(2)}) collective-permute-start(bf16[1024,512]{1,0:T(8,128)(2,1)} %get-tuple-element.123), channel_id=1, source_target_pairs={{0,1},{1,0},{2,3},{3,2},{4,5},{5,4},{6,7},{7,6},{8,9},{9,8},{10,11... | collective-permute-start | bytes 3145736 | tf_op jit(solution)/shard_map/ppermute | solution.py:29
  122.8 86.3 %collective-permute-start.31 = (bf16[1024,512]{1,0:T(8,128)(2,1)}, bf16[1024,512]{1,0:T(8,128)(2,1)}, u32[]{:S(2)}, u32[]{:S(2)}) collective-permute-start(bf16[1024,512]{1,0:T(8,128)(2,1)} %get-tuple-element.111), channel_id=1, source_target_pairs={{0,1},{1,0},{2,3},{3,2},{4,5},{5,4},{6,7},{7,6},{8,9},{9,8},{10,11... | collective-permute-start | bytes 3145736 | tf_op jit(solution)/shard_map/ppermute | solution.py:29
  123.9 72.0 %collective-permute-start.29 = (bf16[3,512,1152]{2,1,0:T(8,128)(2,1)S(1)}, bf16[3,512,1152]{2,1,0:T(8,128)(2,1)}, u32[]{:S(2)}, u32[]{:S(2)}) collective-permute-start(bf16[3,512,1152]{2,1,0:T(8,128)(2,1)S(1)} %pad_maximum_fusion.11), channel_id=1, source_target_pairs={{0,1},{1,0},{2,3},{3,2},{4,5},{5,4},{6,7},{7,6},{8,9},{9,8},{10,11... | collective-permute-start | bytes 10616840 | tf_op jit(solution)/shard_map/ppermute | solution.py:29
  126.9 65.7 %collective-permute-start.19 = (bf16[3,256,1152]{2,1,0:T(8,128)(2,1)}, bf16[3,256,1152]{2,1,0:T(8,128)(2,1)S(1)}, u32[]{:S(2)}, u32[]{:S(2)}) collective-permute-start(bf16[3,256,1152]{2,1,0:T(8,128)(2,1)} %pad_maximum_fusion.19), channel_id=1, source_target_pairs={{0,16},{1,9},{8,24},{9,1},{16,0},{17,25},{24,8},{25,17},{2,18},{3,... | collective-permute-start | bytes 5308424 | tf_op jit(solution)/shard_map/ppermute | solution.py:64
  127.4 42.4 %collective-permute-start.25 = (bf16[3,128,1152]{2,1,0:T(8,128)(2,1)S(1)}, bf16[3,128,1152]{2,1,0:T(8,128)(2,1)S(1)}, u32[]{:S(2)}, u32[]{:S(2)}) collective-permute-start(bf16[3,128,1152]{2,1,0:T(8,128)(2,1)S(1)} %collective-permute-done.21), channel_id=1, source_target_pairs={{0,2},{2,4},{4,6},{6,0},{1,3},{3,5},{5,7},{7,1},{8,10},{10,12},{12... | collective-permute-start | bytes 2654216 | tf_op jit(solution)/shard_map/ppermute | solution.py:69
  172.4 67.5 %collective-permute-start.23 = (bf16[3,256,1152]{2,1,0:T(8,128)(2,1)}, bf16[3,256,1152]{2,1,0:T(8,128)(2,1)S(1)}, u32[]{:S(2)}, u32[]{:S(2)}) collective-permute-start(bf16[3,256,1152]{2,1,0:T(8,128)(2,1)} %pad_maximum_fusion.20), channel_id=1, source_target_pairs={{0,16},{1,9},{8,24},{9,1},{16,0},{17,25},{24,8},{25,17},{2,18},{3,... | collective-permute-start | bytes 5308424 | tf_op jit(solution)/shard_map/ppermute | solution.py:64
  191.8 51.6 %collective-permute-start.27 = (bf16[3,256,1152]{2,1,0:T(8,128)(2,1)}, bf16[3,256,1152]{2,1,0:T(8,128)(2,1)S(1)}, u32[]{:S(2)}, u32[]{:S(2)}) collective-permute-start(bf16[3,256,1152]{2,1,0:T(8,128)(2,1)} %pad_maximum_fusion.21), channel_id=1, source_target_pairs={{0,16},{1,9},{8,24},{9,1},{16,0},{17,25},{24,8},{25,17},{2,18},{3,... | collective-permute-start | bytes 5308424 | tf_op jit(solution)/shard_map/ppermute | solution.py:64
  195.8 49.7 %collective-permute-start.20 = (bf16[3,512,1152]{2,1,0:T(8,128)(2,1)}, bf16[3,512,1152]{2,1,0:T(8,128)(2,1)}, u32[]{:S(2)}, u32[]{:S(2)}) collective-permute-start(bf16[3,512,1152]{2,1,0:T(8,128)(2,1)} %pad_maximum_fusion.8), channel_id=1, source_target_pairs={{0,1},{1,0},{2,3},{3,2},{4,5},{5,4},{6,7},{7,6},{8,9},{9,8},{10,11... | collective-permute-start | bytes 10616840 | tf_op jit(solution)/shard_map/ppermute | solution.py:29
  230.8 31.4 %collective-permute-start.53 = (bf16[3,512,1152]{2,1,0:T(8,128)(2,1)}, bf16[3,512,1152]{2,1,0:T(8,128)(2,1)}, u32[]{:S(2)}, u32[]{:S(2)}) collective-permute-start(bf16[3,512,1152]{2,1,0:T(8,128)(2,1)} %slice.503), channel_id=1, source_target_pairs={{0,1},{1,0},{2,3},{3,2},{4,5},{5,4},{6,7},{7,6},{8,9},{9,8},{10,11... | collective-permute-start | bytes 10616840 | tf_op jit(solution)/shard_map/ppermute | solution.py:29
  242.0 66.5 %collective-permute-start.24 = (bf16[3,512,1152]{2,1,0:T(8,128)(2,1)}, bf16[3,512,1152]{2,1,0:T(8,128)(2,1)}, u32[]{:S(2)}, u32[]{:S(2)}) collective-permute-start(bf16[3,512,1152]{2,1,0:T(8,128)(2,1)} %pad_maximum_fusion.9), channel_id=1, source_target_pairs={{0,1},{1,0},{2,3},{3,2},{4,5},{5,4},{6,7},{7,6},{8,9},{9,8},{10,11... | collective-permute-start | bytes 10616840 | tf_op jit(solution)/shard_map/ppermute | solution.py:29
  243.6 123.7 %collective-permute-start.28 = (bf16[3,512,1152]{2,1,0:T(8,128)(2,1)S(1)}, bf16[3,512,1152]{2,1,0:T(8,128)(2,1)S(1)}, u32[]{:S(2)}, u32[]{:S(2)}) collective-permute-start(bf16[3,512,1152]{2,1,0:T(8,128)(2,1)S(1)} %pad_maximum_fusion.10), channel_id=1, source_target_pairs={{0,1},{1,0},{2,3},{3,2},{4,5},{5,4},{6,7},{7,6},{8,9},{9,8},{10,11... | collective-permute-start | bytes 10616840 | tf_op jit(solution)/shard_map/ppermute | solution.py:29
  265.2 134.3 %collective-permute-start.54 = (bf16[3,256,1152]{2,1,0:T(8,128)(2,1)S(1)}, bf16[3,256,1152]{2,1,0:T(8,128)(2,1)S(1)}, u32[]{:S(2)}, u32[]{:S(2)}) collective-permute-start(bf16[3,256,1152]{2,1,0:T(8,128)(2,1)S(1)} %slice.505), channel_id=1, source_target_pairs={{0,16},{1,9},{8,24},{9,1},{16,0},{17,25},{24,8},{25,17},{2,18},{3,... | collective-permute-start | bytes 5308424 | tf_op jit(solution)/shard_map/ppermute | solution.py:64
  288.2 272.8 %collective-permute-start.62 = (bf16[3,512,1152]{2,1,0:T(8,128)(2,1)}, bf16[3,512,1152]{2,1,0:T(8,128)(2,1)}, u32[]{:S(2)}, u32[]{:S(2)}) collective-permute-start(bf16[3,512,1152]{2,1,0:T(8,128)(2,1)} %slice.521), channel_id=1, source_target_pairs={{0,1},{1,0},{2,3},{3,2},{4,5},{5,4},{6,7},{7,6},{8,9},{9,8},{10,11... | collective-permute-start | bytes 10616840 | tf_op jit(solution)/shard_map/ppermute | solution.py:29
  346.5 219.5 %collective-permute-start.59 = (bf16[3,512,1152]{2,1,0:T(8,128)(2,1)}, bf16[3,512,1152]{2,1,0:T(8,128)(2,1)}, u32[]{:S(2)}, u32[]{:S(2)}) collective-permute-start(bf16[3,512,1152]{2,1,0:T(8,128)(2,1)} %slice.515), channel_id=1, source_target_pairs={{0,1},{1,0},{2,3},{3,2},{4,5},{5,4},{6,7},{7,6},{8,9},{9,8},{10,11... | collective-permute-start | bytes 10616840 | tf_op jit(solution)/shard_map/ppermute | solution.py:29
  417.0 154.4 %collective-permute-start.56 = (bf16[3,512,1152]{2,1,0:T(8,128)(2,1)}, bf16[3,512,1152]{2,1,0:T(8,128)(2,1)}, u32[]{:S(2)}, u32[]{:S(2)}) collective-permute-start(bf16[3,512,1152]{2,1,0:T(8,128)(2,1)} %slice.509), channel_id=1, source_target_pairs={{0,1},{1,0},{2,3},{3,2},{4,5},{5,4},{6,7},{7,6},{8,9},{9,8},{10,11... | collective-permute-start | bytes 10616840 | tf_op jit(solution)/shard_map/ppermute | solution.py:29
  440.4 27.5 %collective-permute-start.52 = (f32[512]{0:T(512)S(1)}, f32[512]{0:T(512)S(1)}, u32[]{:S(2)}, u32[]{:S(2)}) collective-permute-start(f32[512]{0:T(512)S(1)} %slice.406), channel_id=1, source_target_pairs={{0,1},{1,0},{2,3},{3,2},{4,5},{5,4},{6,7},{7,6},{8,9},{9,8},{10,11... | collective-permute-start | bytes 6152 | tf_op jit(solution)/shard_map/ppermute | solution.py:29
  467.9 214.3 %collective-permute-start.30 = (bf16[1024,512]{1,0:T(8,128)(2,1)}, bf16[1024,512]{1,0:T(8,128)(2,1)}, u32[]{:S(2)}, u32[]{:S(2)}) collective-permute-start(bf16[1024,512]{1,0:T(8,128)(2,1)} %get-tuple-element.121), channel_id=1, source_target_pairs={{0,1},{1,0},{2,3},{3,2},{4,5},{5,4},{6,7},{7,6},{8,9},{9,8},{10,11... | collective-permute-start | bytes 3145736 | tf_op jit(solution)/shard_map/ppermute | solution.py:29
  493.5 99.6 %collective-permute-start.34 = (f32[512]{0:T(512)S(1)}, f32[512]{0:T(512)S(1)}, u32[]{:S(2)}, u32[]{:S(2)}) collective-permute-start(f32[512]{0:T(512)S(1)} %slice.376), channel_id=1, source_target_pairs={{0,1},{1,0},{2,3},{3,2},{4,5},{5,4},{6,7},{7,6},{8,9},{9,8},{10,11... | collective-permute-start | bytes 6152 | tf_op jit(solution)/shard_map/ppermute | solution.py:29
  561.1 121.1 %collective-permute-start.35 = (bf16[4,512,256]{2,1,0:T(8,128)(2,1)}, bf16[4,512,256]{2,1,0:T(8,128)(2,1)}, u32[]{:S(2)}, u32[]{:S(2)}) collective-permute-start(bf16[4,512,256]{2,1,0:T(8,128)(2,1)} %get-tuple-element.92), channel_id=1, source_target_pairs={{0,1},{1,0},{2,3},{3,2},{4,5},{5,4},{6,7},{7,6},{8,9},{9,8},{10,11... | collective-permute-start | bytes 3145736 | tf_op jit(solution)/shard_map/ppermute | solution.py:29
  571.5 45.9 %collective-permute-start.60 = (bf16[3,256,1152]{2,1,0:T(8,128)(2,1)S(1)}, bf16[3,256,1152]{2,1,0:T(8,128)(2,1)S(1)}, u32[]{:S(2)}, u32[]{:S(2)}) collective-permute-start(bf16[3,256,1152]{2,1,0:T(8,128)(2,1)S(1)} %slice.517), channel_id=1, source_target_pairs={{0,16},{1,9},{8,24},{9,1},{16,0},{17,25},{24,8},{25,17},{2,18},{3,... | collective-permute-start | bytes 5308424 | tf_op jit(solution)/shard_map/ppermute | solution.py:64
  589.0 88.0 %collective-permute-start.57 = (bf16[3,256,1152]{2,1,0:T(8,128)(2,1)}, bf16[3,256,1152]{2,1,0:T(8,128)(2,1)}, u32[]{:S(2)}, u32[]{:S(2)}) collective-permute-start(bf16[3,256,1152]{2,1,0:T(8,128)(2,1)} %slice.511), channel_id=1, source_target_pairs={{0,16},{1,9},{8,24},{9,1},{16,0},{17,25},{24,8},{25,17},{2,18},{3,... | collective-permute-start | bytes 5308424 | tf_op jit(solution)/shard_map/ppermute | solution.py:64
  593.1 28.9 %collective-permute-start.64 = (bf16[3,128,1152]{2,1,0:T(8,128)(2,1)S(1)}, bf16[3,128,1152]{2,1,0:T(8,128)(2,1)S(1)}, u32[]{:S(2)}, u32[]{:S(2)}) collective-permute-start(bf16[3,128,1152]{2,1,0:T(8,128)(2,1)S(1)} %slice.525), channel_id=1, source_target_pairs={{0,8},{1,17},{8,0},{9,25},{16,24},{17,1},{24,16},{25,9},{2,10},{3,... | collective-permute-start | bytes 2654216 | tf_op jit(solution)/shard_map/ppermute | solution.py:59
  620.0 59.3 %collective-permute-start.61 = (bf16[3,128,1152]{2,1,0:T(8,128)(2,1)}, bf16[3,128,1152]{2,1,0:T(8,128)(2,1)}, u32[]{:S(2)}, u32[]{:S(2)}) collective-permute-start(bf16[3,128,1152]{2,1,0:T(8,128)(2,1)} %slice.519), channel_id=1, source_target_pairs={{0,8},{1,17},{8,0},{9,25},{16,24},{17,1},{24,16},{25,9},{2,10},{3,... | collective-permute-start | bytes 2654216 | tf_op jit(solution)/shard_map/ppermute | solution.py:59
  623.1 56.7 %collective-permute-start.65 = (bf16[3,128,1152]{2,1,0:T(8,128)(2,1)}, bf16[3,128,1152]{2,1,0:T(8,128)(2,1)}, u32[]{:S(2)}, u32[]{:S(2)}) collective-permute-start(bf16[3,128,1152]{2,1,0:T(8,128)(2,1)} %add_convert_fusion.16), channel_id=1, source_target_pairs={{0,2},{2,4},{4,6},{6,0},{1,3},{3,5},{5,7},{7,1},{8,10},{10,12},{12... | collective-permute-start | bytes 2654216 | tf_op jit(solution)/shard_map/ppermute | solution.py:69
  686.0 40.8 %collective-permute-start.55 = (bf16[3,128,1152]{2,1,0:T(8,128)(2,1)S(1)}, bf16[3,128,1152]{2,1,0:T(8,128)(2,1)S(1)}, u32[]{:S(2)}, u32[]{:S(2)}) collective-permute-start(bf16[3,128,1152]{2,1,0:T(8,128)(2,1)S(1)} %copy-done.38), channel_id=1, source_target_pairs={{0,8},{1,17},{8,0},{9,25},{16,24},{17,1},{24,16},{25,9},{2,10},{3,... | collective-permute-start | bytes 2654216 | tf_op jit(solution)/shard_map/ppermute | solution.py:59
  688.0 71.4 %collective-permute-start.33 = (bf16[1024,512]{1,0:T(8,128)(2,1)S(1)}, bf16[1024,512]{1,0:T(8,128)(2,1)S(1)}, u32[]{:S(2)}, u32[]{:S(2)}) collective-permute-start(bf16[1024,512]{1,0:T(8,128)(2,1)S(1)} %copy-done.35), channel_id=1, source_target_pairs={{0,1},{1,0},{2,3},{3,2},{4,5},{5,4},{6,7},{7,6},{8,9},{9,8},{10,11... | collective-permute-start | bytes 3145736 | tf_op jit(solution)/shard_map/ppermute | solution.py:29
  690.5 25.2 %collective-permute-start.42 = (bf16[4,256,256]{2,1,0:T(8,128)(2,1)S(1)}, bf16[4,256,256]{2,1,0:T(8,128)(2,1)S(1)}, u32[]{:S(2)}, u32[]{:S(2)}) collective-permute-start(bf16[4,256,256]{2,1,0:T(8,128)(2,1)S(1)} %slice.490), channel_id=1, source_target_pairs={{0,16},{1,9},{8,24},{9,1},{16,0},{17,25},{24,8},{25,17},{2,18},{3,... | collective-permute-start | bytes 1572872 | tf_op jit(solution)/shard_map/ppermute | solution.py:64
  749.6 33.8 %collective-permute-start.69 = (bf16[3,256,1152]{2,1,0:T(8,128)(2,1)}, bf16[3,256,1152]{2,1,0:T(8,128)(2,1)}, u32[]{:S(2)}, u32[]{:S(2)}) collective-permute-start(bf16[3,256,1152]{2,1,0:T(8,128)(2,1)} %pad_maximum_fusion.22), channel_id=1, source_target_pairs={{0,16},{1,9},{8,24},{9,1},{16,0},{17,25},{24,8},{25,17},{2,18},{3,... | collective-permute-start | bytes 5308424 | tf_op jit(solution)/shard_map/ppermute | solution.py:64
  (127 other events, 1418.7 us)

commit v2 on v0

--- a/solution.py
+++ b/solution.py
@@ -1,13 +1,1204 @@
+import functools
+
 import jax
 import jax.numpy as jnp
 from jax import lax
+from jax.experimental import pallas as pl
+from jax.experimental.pallas import tpu as pltpu
 from jax.sharding import PartitionSpec as P
 
 KCONV = 3
 ROW_LEN = 8192
+BLOCKS = 4
+OFFSETS = (0, -1, 1, 2)
+HALO = 16
+STEP = 256
 
 
 eps = 1e-05
+bf16 = jnp.bfloat16
+f32 = jnp.float32
+VMEM_LIMIT = 64000 * 1024
+HERE = pl.BlockSpec(memory_space=pl.ANY)
+SCALARS = pl.BlockSpec(memory_space=pltpu.SMEM)
+
+
+def dot(left, right):
+    return jnp.dot(left, right, preferred_element_type=f32)
+
+
+def dot_nt(left, right):
+    return lax.dot_general(left, right, (((1,), (1,)), ((), ())), preferred_element_type=f32)
+
+
+def shape_of(*dims, dtype=bf16):
+    return jax.ShapeDtypeStruct(dims, dtype)
+
+
+def call(body, name, out_shape, flops=0, moved=0, tie=(), n_in=None, **kwargs):
+    if tie:
+        inner, at = body, n_in
+
+        def body(*refs):
+            inner(*refs[:at], *refs[at + len(tie) :])
+
+        if "grid_spec" in kwargs:
+            spec = kwargs["grid_spec"]
+            kwargs["grid_spec"] = pltpu.PrefetchScalarGridSpec(
+                num_scalar_prefetch=1,
+                grid=spec.grid,
+                in_specs=list(spec.in_specs) + [HERE] * len(tie),
+                out_specs=spec.out_specs,
+                scratch_shapes=spec.scratch_shapes,
+            )
+        else:
+            kwargs["in_specs"] = list(kwargs["in_specs"]) + [HERE] * len(tie)
+    return pl.pallas_call(
+        body,
+        out_shape=out_shape,
+        name=name,
+        compiler_params=pltpu.CompilerParams(vmem_limit_bytes=VMEM_LIMIT),
+        cost_estimate=pl.CostEstimate(flops=flops, bytes_accessed=moved, transcendentals=0),
+        **kwargs,
+    )
+
+
+def scalar_grid(grid, in_specs, out_specs, scratch_shapes=()):
+    return pltpu.PrefetchScalarGridSpec(
+        num_scalar_prefetch=1,
+        grid=grid,
+        in_specs=in_specs,
+        out_specs=out_specs,
+        scratch_shapes=scratch_shapes,
+    )
+
+
+def quarter_of(place, j):
+    dp, core = place[0], place[1]
+    low, high = j % 2, j // 2
+    mask = jnp.where(core == 0, 2 * high + low, 2 * low + high)
+    return jnp.bitwise_xor(dp, mask)
+
+
+def join_tokens(mine, theirs, place):
+    count, half = mine.shape
+
+    def body(place, mine, theirs, out):
+        own = pl.program_id(0) == place[1]
+
+        @pl.when(own)
+        def _():
+            out[...] = mine[...]
+
+        @pl.when(jnp.logical_not(own))
+        def _():
+            out[...] = theirs[...]
+
+    kept = pl.BlockSpec((count, half), lambda h, place: (0, 0))
+    return call(
+        body,
+        "join_tokens",
+        shape_of(2 * count, half),
+        grid_spec=scalar_grid(
+            (2,), [kept, kept], pl.BlockSpec((count, half), lambda h, place: (h, 0))
+        ),
+    )(place, mine, theirs)
+
+
+def outgoing(place, tokens, cotangent, before, gains):
+    count, half = tokens.shape[0] // 2, tokens.shape[1]
+    rows = 2 * count + 2 * HALO
+
+    def body(place, tokens, cotangent, between, before, gains, out):
+        out[:count] = tokens[...]
+        out[count : 2 * count] = cotangent[...]
+
+        @pl.when(place[1] == 0)
+        def _():
+            out[2 * count : 2 * count + HALO] = between[...]
+
+        @pl.when(place[1] == 1)
+        def _():
+            out[2 * count : 2 * count + HALO] = before[...]
+
+        out[2 * count + HALO :] = gains[...]
+
+    theirs = pl.BlockSpec((count, half), lambda i, place: (1 - place[1], 0))
+    few = pl.BlockSpec((HALO, half), lambda i, place: (0, 0))
+    return call(
+        body,
+        "outgoing",
+        shape_of(rows, half),
+        grid_spec=scalar_grid(
+            (1,),
+            [theirs, theirs, pl.BlockSpec((HALO, half), lambda i, place: (count // HALO - 1, 0)), few, few],
+            pl.BlockSpec((rows, half), lambda i, place: (0, 0)),
+        ),
+    )(place, tokens, cotangent, tokens, before, gains)
+
+
+def pack(stack, turned, place, quarters, rows=None, tie=()):
+    k, half, n = stack.shape
+    width = half // 4
+    lanes = (k + 1) * n
+    below = [] if rows is None else [rows]
+
+    def body(place, stack, turned, *refs):
+        out = refs[-1]
+        for i in range(k):
+            out[:width, i * n : (i + 1) * n] = stack[i]
+        out[:width, k * n :] = turned[...].astype(f32).T.astype(out.dtype)
+        if below:
+            out[width:, :] = jnp.zeros((HALO, lanes), out.dtype)
+            out[width : width + KCONV, :n] = refs[0][...]
+
+    def source(j, place):
+        return place[0] if quarters == 1 else j
+
+    return call(
+        body,
+        "pack",
+        shape_of(quarters * width + HALO * len(below), lanes),
+        tie=tie,
+        n_in=3 + len(below),
+        grid_spec=scalar_grid(
+            (quarters,),
+            [
+                pl.BlockSpec((k, width, n), lambda j, place: (0, source(j, place), 0)),
+                pl.BlockSpec((n, width), lambda j, place: (0, source(j, place))),
+            ]
+            + [pl.BlockSpec((KCONV, n), lambda j, place: (0, 0))] * len(below),
+            pl.BlockSpec((width + HALO * len(below), lanes), lambda j, place: (j, 0)),
+        ),
+    )(place, stack, turned, *below, *tie)
+
+
+def join_rows(parts, tie):
+    rows, lanes = parts[0].shape
+
+    def body(*refs):
+        for i in range(len(parts)):
+            refs[-1][i * rows : (i + 1) * rows] = refs[i][...]
+
+    whole = pl.BlockSpec(memory_space=pltpu.VMEM)
+    return call(
+        body,
+        "join_rows",
+        shape_of(len(parts) * rows, lanes),
+        tie=tie,
+        n_in=len(parts),
+        in_specs=[whole] * len(parts),
+        out_specs=whole,
+    )(*parts, *tie)
+
+
+def mix_assemble(own, pieces, place, tie):
+    half, lanes = own.shape
+    width = half // 4
+    stride = width + HALO
+
+    def body(place, own, *refs):
+        out = refs[-1]
+        out[0] = own[...]
+        for s in range(1, BLOCKS):
+            for j in range(4):
+                rows = pl.ds(pl.multiple_of(quarter_of(place, j) * width, width), width)
+                out[s, rows, :] = refs[j][(s - 1) * stride : (s - 1) * stride + width, :]
+
+    whole = pl.BlockSpec(memory_space=pltpu.VMEM)
+    return call(
+        body,
+        "mix_assemble",
+        shape_of(BLOCKS, half, lanes),
+        tie=tie,
+        n_in=6,
+        in_specs=[SCALARS] + [whole] * 5,
+        out_specs=whole,
+    )(place, own, *pieces, *tie)
+
+
+def unpack(pieces, k, place):
+    width, lanes = pieces[0].shape
+    half, n = 4 * width, lanes // (k + 1)
+
+    def body(place, *refs):
+        stack, turned = refs[4:]
+        for j in range(4):
+
+            @pl.when(pl.program_id(0) == j)
+            def _(piece=refs[j]):
+                for i in range(k):
+                    stack[i] = piece[:, i * n : (i + 1) * n].astype(f32)
+                turned[...] = piece[:, k * n :].astype(f32).T
+
+    whole = pl.BlockSpec((width, lanes), lambda j, place: (0, 0))
+    return call(
+        body,
+        "unpack",
+        (shape_of(k, half, n, dtype=f32), shape_of(n, half, dtype=f32)),
+        grid_spec=scalar_grid(
+            (4,),
+            [whole] * 4,
+            [
+                pl.BlockSpec((k, width, n), lambda j, place: (0, quarter_of(place, j), 0)),
+                pl.BlockSpec((n, width), lambda j, place: (0, quarter_of(place, j))),
+            ],
+        ),
+    )(place, *pieces)
+
+
+def rows_of(i, step=STEP):
+    return pl.ds(pl.multiple_of(i * step, step), step)
+
+
+def slots(place, start, count):
+    slot = place[2] + start + lax.broadcasted_iota(jnp.int32, (count, 1), 0)
+    return slot, jnp.where(slot < place[3], 0, place[3])
+
+
+def inverse_rms(*parts):
+    width = sum(part.shape[1] for part in parts)
+    total = sum(jnp.sum(part * part, axis=1, keepdims=True) for part in parts)
+    return lax.rsqrt(total / width + eps)
+
+
+def prepare(place, tokens, theirs, before, cotangent, gain, tie):
+    count, half = tokens.shape[0] // 2, tokens.shape[1]
+    width = 2 * half
+
+    def body(
+        place, own, other, before, between, halo_other, cot, cot_other, gain, normed, normed_t, low, low_t
+    ):
+        def norm(left, right):
+            left, right = left.astype(f32), right.astype(f32)
+            rstd = inverse_rms(left, right)
+            return (
+                (left * rstd * gain[:, :half]).astype(bf16),
+                (right * rstd * gain[:, half:]).astype(bf16),
+            )
+
+        halo = jnp.where(place[1] == 0, before[...].astype(f32), between[...].astype(f32))
+
+        @pl.when(pl.program_id(0) == 0)
+        def _():
+            left, right = norm(halo, halo_other[...])
+            normed[:HALO, :half] = left
+            normed[:HALO, half:] = right
+
+        tile = pl.program_id(0)
+        here = pl.ds(pl.multiple_of(HALO + tile * STEP, HALO), STEP)
+        for i, value in enumerate(norm(own[...], other[...])):
+            lanes = slice(i * half, (i + 1) * half)
+            normed[here, lanes] = value
+            normed_t[lanes, :] = value.astype(f32).T.astype(bf16)
+        slot, _ = slots(place, tile * STEP, STEP)
+        valid = (slot < place[4]).astype(f32)
+        for i, value in enumerate((cot[...], cot_other[...])):
+            lanes = slice(i * half, (i + 1) * half)
+            value = value.astype(f32) * valid
+            low[:, lanes] = value.astype(bf16)
+            low_t[lanes, :] = value.T.astype(bf16)
+
+    tiles = count // STEP
+    mine = pl.BlockSpec((STEP, half), lambda m, place: (place[1] * tiles + m, 0))
+
+    def received(first):
+        return pl.BlockSpec((STEP, half), lambda m, place: (first + m, 0))
+
+    def few(block):
+        return pl.BlockSpec((HALO, half), lambda m, place: (block, 0))
+
+    turned = pl.BlockSpec((width, STEP), lambda m, place: (0, m))
+    return call(
+        body,
+        "prepare",
+        (
+            shape_of(HALO + count, width),
+            shape_of(width, count),
+            shape_of(count, width),
+            shape_of(width, count),
+        ),
+        moved=16 * count * width,
+        tie=tie,
+        n_in=9,
+        grid_spec=scalar_grid(
+            (tiles,),
+            [
+                mine,
+                received(0),
+                few(0),
+                few(count // HALO - 1),
+                few(2 * count // HALO),
+                mine,
+                received(tiles),
+                pl.BlockSpec((1, width), lambda m, place: (0, 0)),
+            ],
+            [
+                pl.BlockSpec((HALO + count, width), lambda m, place: (0, 0)),
+                turned,
+                pl.BlockSpec((STEP, width), lambda m, place: (m, 0)),
+                turned,
+            ],
+        ),
+    )(place, tokens, theirs, before, tokens, theirs, cotangent, theirs, gain, *tie)
+
+
+def mix_copies(sources, inward, outward, sems):
+    copies = []
+    for s in range(BLOCKS):
+        for side in range(2):
+            source = sources[side].at[s]
+            half, lanes = source.shape
+            n = lanes // 4
+            rows = pl.ds(side * half, half)
+            at = 4 * s + 2 * side
+            copies.append(
+                pltpu.make_async_copy(
+                    source.at[:, pl.ds(0, 3 * n)],
+                    inward.at[rows, pl.ds(s * 3 * n, 3 * n)],
+                    sems.at[at],
+                )
+            )
+            copies.append(
+                pltpu.make_async_copy(
+                    source.at[:, pl.ds(3 * n, n)],
+                    outward.at[rows, pl.ds(s * n, n)],
+                    sems.at[at + 1],
+                )
+            )
+    return copies
+
+
+def mix_forward(place, normed, halves, tokens, theirs, taps, gain, tie):
+    count, half = tokens.shape[0] // 2, tokens.shape[1]
+    width = 2 * half
+    n = width // BLOCKS
+    part = (HALO + count) // 5
+    kept = 4
+
+    def body(place, *refs):
+        normed_hbm, sources, refs = refs[0], refs[1:3], refs[3:]
+        tokens_hbm, theirs_hbm, taps, gain = refs[:4]
+        results, hidden_hbm, carried_hbm, normed2_hbm, turned_hbm = (
+            refs[4:8],
+            refs[8],
+            refs[9],
+            refs[10],
+            refs[11],
+        )
+        normed, inward, outward, mine, other, mixed, product, carried, hidden, normed2, turned = refs[
+            12:23
+        ]
+        saved = refs[23:27]
+        in_sems, weight_sems, saved_sems, out_sems = refs[27:]
+        loads = [
+            pltpu.make_async_copy(normed_hbm, normed, in_sems.at[0]),
+            pltpu.make_async_copy(
+                tokens_hbm.at[pl.ds(pl.multiple_of(place[1] * count, count), count)],
+                mine,
+                in_sems.at[1],
+            ),
+            pltpu.make_async_copy(theirs_hbm.at[pl.ds(0, count)], other, in_sems.at[2]),
+        ]
+        weights = mix_copies(sources, inward, outward, weight_sems)
+        loads[0].start()
+        for copy in weights:
+            copy.start()
+        loads[1].start()
+        loads[2].start()
+        loads[0].wait()
+        pending = []
+        for s in range(BLOCKS):
+            for copy in weights[4 * s : 4 * s + 4]:
+                copy.wait()
+
+            def project(i, carry, s=s):
+                rows = rows_of(i, part)
+                value = dot(normed[rows, :], inward[:, s * 3 * n : (s + 1) * 3 * n])
+                mixed[rows, :] = value
+                product[rows, :] = value[:, :n] * value[:, 2 * n :]
+                return carry
+
+            lax.fori_loop(0, 5, project, 0)
+            lanes = slice(s * n, (s + 1) * n)
+            for m in range(count // STEP):
+                first = HALO + m * STEP
+                rows = slice(m * STEP, (m + 1) * STEP)
+                slot, start = slots(place, m * STEP, STEP)
+                conv = jnp.zeros((STEP, n), f32)
+                for lag in range(KCONV):
+                    keep = (slot - lag >= start).astype(f32)
+                    conv = conv + taps[lag : lag + 1, lanes] * (
+                        keep * product[first - lag : first - lag + STEP, :]
+                    )
+                inside = mixed[first : first + STEP, :]
+                carried[rows, lanes] = (inside[:, n : 2 * n] * conv).astype(bf16)
+                for i, value in enumerate((inside[:, :n], inside[:, n : 2 * n], inside[:, 2 * n :], conv)):
+                    saved[i][rows, lanes] = value.astype(bf16)
+            for i in range(kept):
+                copy = pltpu.make_async_copy(
+                    saved[i].at[:, pl.ds(s * n, n)],
+                    results[i].at[:, pl.ds(s * n, n)],
+                    saved_sems.at[kept * s + i],
+                )
+                copy.start()
+                pending.append(copy)
+        copy = pltpu.make_async_copy(carried, carried_hbm, in_sems.at[3])
+        copy.start()
+        pending.append(copy)
+        loads[1].wait()
+        loads[2].wait()
+        for m in range(count // STEP):
+            rows = slice(m * STEP, (m + 1) * STEP)
+            term = dot_nt(carried[rows, :], outward[...])
+            left = mine[rows, :].astype(f32) + term[:, :half]
+            right = other[rows, :].astype(f32) + term[:, half:]
+            rstd = inverse_rms(left, right)
+            for i, value in enumerate((left, right)):
+                lanes = slice(i * half, (i + 1) * half)
+                hidden[rows, lanes] = value
+                value = value * rstd * gain[:, lanes]
+                normed2[rows, lanes] = value.astype(bf16)
+                turned[lanes, rows] = value.T.astype(bf16)
+            for i, (source, target, by) in enumerate(
+                (
+                    (hidden, hidden_hbm, 0),
+                    (normed2, normed2_hbm, 0),
+                    (turned, turned_hbm, 1),
+                )
+            ):
+                here = pl.ds(m * STEP, STEP)
+                source, target = (
+                    (source.at[:, here], target.at[:, here])
+                    if by
+                    else (source.at[here], target.at[here])
+                )
+                copy = pltpu.make_async_copy(source, target, out_sems.at[3 * m + i])
+                copy.start()
+                pending.append(copy)
+        for copy in pending:
+            copy.wait()
+
+    tiles = count // STEP
+    wide = shape_of(count, width, dtype=f32)
+    flat = shape_of(count, width)
+    whole = pl.BlockSpec(memory_space=pltpu.VMEM)
+    return call(
+        body,
+        "mix_forward",
+        (flat, flat, flat, flat, wide, flat, flat, shape_of(width, count)),
+        flops=8 * count * width * width,
+        moved=30 * count * width + 8 * width * width,
+        tie=tie,
+        n_in=8,
+        in_specs=[SCALARS] + [HERE] * 5 + [whole] * 2,
+        out_specs=(HERE,) * 8,
+        scratch_shapes=[
+            pltpu.VMEM((HALO + count, width), bf16),
+            pltpu.VMEM((width, 3 * width), bf16),
+            pltpu.VMEM((width, width), bf16),
+            pltpu.VMEM((count, half), bf16),
+            pltpu.VMEM((count, half), bf16),
+            pltpu.VMEM((HALO + count, 3 * n), f32),
+            pltpu.VMEM((HALO + count, n), f32),
+            pltpu.VMEM((count, width), bf16),
+            pltpu.VMEM((count, width), f32),
+            pltpu.VMEM((count, width), bf16),
+            pltpu.VMEM((width, count), bf16),
+        ]
+        + [pltpu.VMEM((count, width), bf16)] * kept
+        + [
+            pltpu.SemaphoreType.DMA((4,)),
+            pltpu.SemaphoreType.DMA((4 * BLOCKS,)),
+            pltpu.SemaphoreType.DMA((kept * BLOCKS,)),
+            pltpu.SemaphoreType.DMA((3 * tiles,)),
+        ],
+    )(place, normed, *halves, tokens, theirs, taps, gain, *tie)
+
+
+def feed_body(
+    lanes,
+    started,
+    normed_hbm,
+    low_hbm,
+    normed_t_hbm,
+    low_t_hbm,
+    own_hbm,
+    other_hbm,
+    grad_in,
+    grad_hbm,
+    acts_hbm,
+    theirs_hbm,
+    normed,
+    low,
+    normed_t,
+    low_t,
+    weights,
+    grad,
+    acts,
+    theirs,
+    in_sems,
+    grad_sems,
+    acts_sems,
+    their_sems,
+):
+    f = lanes // 3
+    count, width = normed.shape
+    half = width // 2
+    loads = [
+        pltpu.make_async_copy(source, target, in_sems.at[i])
+        for i, (source, target) in enumerate(
+            (
+                (normed_hbm, normed),
+                (own_hbm, weights.at[pl.ds(0, half)]),
+                (other_hbm, weights.at[pl.ds(half, half)]),
+                (low_hbm, low),
+                (normed_t_hbm.at[pl.ds(half, half)], normed_t),
+                (low_t_hbm.at[pl.ds(half, half)], low_t),
+            )
+        )
+    ]
+    if started:
+        loads.append(pltpu.make_async_copy(grad_in, grad, in_sems.at[6]))
+    for load in loads[:4]:
+        load.start()
+    for load in loads[:4]:
+        load.wait()
+    for load in loads[4:]:
+        load.start()
+
+    def acts_copy(i):
+        rows = rows_of(i)
+        return pltpu.make_async_copy(acts.at[rows], acts_hbm.at[rows], acts_sems.at[i])
+
+    def activations(i, carry):
+        rows = rows_of(i)
+        for start in range(0, f, 256):
+            stop = min(start + 256, f)
+            gate_lanes = slice(start, stop)
+            up_lanes = slice(f + start, f + stop)
+            down_lanes = slice(2 * f + start, 2 * f + stop)
+            gate = dot(normed[rows, :], weights[:, gate_lanes])
+            up_part = dot(normed[rows, :], weights[:, up_lanes])
+            grad_active = dot(low[rows, :], weights[:, down_lanes])
+            sigmoid_gate = jax.nn.sigmoid(gate)
+            silu_gate = gate * sigmoid_gate
+            acts[rows, gate_lanes] = (
+                grad_active * up_part * sigmoid_gate * (1.0 + gate * (1.0 - sigmoid_gate))
+            ).astype(bf16)
+            acts[rows, up_lanes] = (grad_active * silu_gate).astype(bf16)
+            acts[rows, down_lanes] = (silu_gate * up_part).astype(bf16)
+        acts_copy(i).start()
+        return carry
+
+    lax.fori_loop(0, count // STEP, activations, 0)
+    loads[4].wait()
+    loads[5].wait()
+
+    def their_copy(i):
+        rows = rows_of(i)
+        return pltpu.make_async_copy(theirs.at[rows], theirs_hbm.at[rows], their_sems.at[i])
+
+    def outer(i, carry):
+        rows = rows_of(i)
+        theirs[rows, : 2 * f] = dot(normed_t[rows, :], acts[:, : 2 * f]).astype(bf16)
+        theirs[rows, 2 * f :] = dot(low_t[rows, :], acts[:, 2 * f :]).astype(bf16)
+        their_copy(i).start()
+        return carry
+
+    lax.fori_loop(0, half // STEP, outer, 0)
+    if started:
+        loads[6].wait()
+
+    def grad_copy(i):
+        rows = rows_of(i)
+        return pltpu.make_async_copy(grad.at[rows], grad_hbm.at[rows], grad_sems.at[i])
+
+    def inner(i, carry):
+        rows = rows_of(i)
+        term = dot_nt(acts[rows, : 2 * f], weights[:, : 2 * f])
+        grad[rows, :] = grad[rows, :] + term if started else term
+        grad_copy(i).start()
+        return carry
+
+    lax.fori_loop(0, count // STEP, inner, 0)
+    for i in range(half // STEP):
+        their_copy(i).wait()
+    for i in range(count // STEP):
+        acts_copy(i).wait()
+        grad_copy(i).wait()
+
+
+def feed(normed, low, normed_t, low_t, own, other, grad, tie):
+    count, width = normed.shape
+    half, lanes = own.shape
+    f = lanes // 3
+    started = grad is not None
+    tiles = count // STEP
+    before = [grad] if started else []
+    body = functools.partial(feed_body, lanes, started)
+    if not started:
+        inner = body
+
+        def body(*refs):
+            inner(*refs[:6], None, *refs[6:])
+
+    return call(
+        body,
+        "feed",
+        (shape_of(count, width, dtype=f32), shape_of(count, lanes), shape_of(half, lanes)),
+        flops=13 * count * width * f,
+        moved=2 * (4 * count * width + 3 * half * lanes + count * lanes) + 8 * count * width,
+        tie=tie,
+        n_in=6 + len(before),
+        in_specs=[HERE] * (6 + len(before)),
+        out_specs=(HERE,) * 3,
+        scratch_shapes=[
+            pltpu.VMEM((count, width), bf16),
+            pltpu.VMEM((count, width), bf16),
+            pltpu.VMEM((half, count), bf16),
+            pltpu.VMEM((half, count), bf16),
+            pltpu.VMEM((width, lanes), bf16),
+            pltpu.VMEM((count, width), f32),
+            pltpu.VMEM((count, lanes), bf16),
+            pltpu.VMEM((half, lanes), bf16),
+            pltpu.SemaphoreType.DMA((7,)),
+            pltpu.SemaphoreType.DMA((tiles,)),
+            pltpu.SemaphoreType.DMA((tiles,)),
+            pltpu.SemaphoreType.DMA((half // STEP,)),
+        ],
+    )(normed, low, normed_t, low_t, own, other, *before, *tie)
+
+
+def feed_output(hidden, acts, owns, others, tie):
+    count, width = hidden.shape
+    half, lanes = owns[0].shape
+    f = lanes // 3
+
+    def body(hidden, *refs):
+        acts, owns, others, outs = refs[:4], refs[4:8], refs[8:12], refs[12:]
+        for side, weights in enumerate((owns, others)):
+            total = hidden[:, side * half : (side + 1) * half]
+            for k in range(BLOCKS):
+                total = total + dot_nt(acts[k][...], weights[k][...])
+            outs[side][...] = total.astype(bf16)
+
+    rows = pl.BlockSpec((STEP, f), lambda m: (m, 2))
+    whole = pl.BlockSpec((half, f), lambda m: (0, 2))
+    part = pl.BlockSpec((STEP, half), lambda m: (m, 0))
+    return call(
+        body,
+        "feed_output",
+        (shape_of(count, half),) * 2,
+        flops=2 * BLOCKS * count * width * f,
+        moved=2 * BLOCKS * (count + width) * f + 6 * count * width,
+        tie=tie,
+        n_in=13,
+        grid=(count // STEP,),
+        in_specs=[pl.BlockSpec((STEP, width), lambda m: (m, 0))] + [rows] * 4 + [whole] * 8,
+        out_specs=(part, part),
+    )(hidden, *acts, *owns, *others, *tie)
+
+
+def keep_and_send(place, total, keep, send):
+    width = keep.shape[0] // 2
+    for j in range(4):
+        target = keep if j < 2 else send
+        rows = pl.ds(pl.multiple_of(quarter_of(place, j) * width, width), width)
+        target[(j % 2) * width : (j % 2 + 1) * width, :] = total[rows, :].astype(bf16)
+
+
+def feed_weights(place, normed_t, low_t, acts, received, tie):
+    width, count = normed_t.shape
+    half, lanes = received.shape
+    f = lanes // 3
+    step = f
+
+    def body(place, normed_t, low_t, acts, received, keep, send, total):
+        def put(left):
+            total[...] = dot(left[...], acts[...]) + received[...].astype(f32)
+
+        is_down = pl.program_id(0) >= 2 * f // step
+
+        @pl.when(jnp.logical_not(is_down))
+        def _():
+            put(normed_t)
+
+        @pl.when(is_down)
+        def _():
+            put(low_t)
+
+        keep_and_send(place, total, keep, send)
+
+    left = pl.BlockSpec((half, count), lambda j, place: (0, 0))
+    part = pl.BlockSpec((half // 2, step), lambda j, place: (0, j))
+    return call(
+        body,
+        "feed_weights",
+        (shape_of(half // 2, lanes),) * 2,
+        flops=6 * count * half * f,
+        moved=2 * (2 * half * count + count * lanes + 2 * half * lanes),
+        tie=tie,
+        n_in=5,
+        grid_spec=scalar_grid(
+            (lanes // step,),
+            [
+                left,
+                left,
+                pl.BlockSpec((count, step), lambda j, place: (0, j)),
+                pl.BlockSpec((half, step), lambda j, place: (0, j)),
+            ],
+            [part, part],
+            [pltpu.VMEM((half, step), f32)],
+        ),
+    )(place, normed_t, low_t, acts, received, *tie)
+
+
+def hidden_backward(hidden, grad_normed, grad_out, gain):
+    width = hidden.shape[1]
+    rstd = lax.rsqrt(jnp.sum(hidden * hidden, axis=1, keepdims=True) / width + eps)
+    scaled = grad_normed * gain
+    mean = jnp.sum(scaled * hidden, axis=1, keepdims=True) / width
+    grad = grad_out + (rstd * scaled - hidden * (rstd * rstd * rstd) * mean)
+    return grad, grad_normed * hidden * rstd
+
+
+def first_rows(hidden, grad_normed, low, gate_c, gain, halves):
+    width = hidden.shape[1]
+    n = width // BLOCKS
+    half = width // 2
+
+    def body(hidden, grad_normed, low, gate_c, gain, *refs):
+        grad, _ = hidden_backward(hidden[...], grad_normed[...], low[...].astype(f32), gain[...])
+        grad_o = grad.astype(bf16)
+        for s in range(BLOCKS):
+            value = dot(grad_o[:, :half], refs[0][s]) + dot(grad_o[:, half:], refs[1][s])
+            lanes = slice(s * n, (s + 1) * n)
+            refs[-1][:, lanes] = (value * gate_c[:, lanes].astype(f32))[:8]
+
+    few = pl.BlockSpec((HALO, width), lambda i: (0, 0))
+    return call(
+        body,
+        "first_rows",
+        shape_of(8, width, dtype=f32),
+        grid=(1,),
+        in_specs=[few] * 4
+        + [pl.BlockSpec((1, width), lambda i: (0, 0))]
+        + [pl.BlockSpec((BLOCKS, half, n), lambda i: (0, 0, 3))] * 2,
+        out_specs=pl.BlockSpec((8, width), lambda i: (0, 0)),
+    )(hidden, grad_normed, low, gate_c, gain, *halves)
+
+
+def mix_backward(
+    place, hidden, grad_normed, low, tokens, theirs, saved, later, taps, gain_one, gain_two, halves, tie
+):
+    count, width = hidden.shape
+    half = width // 2
+    n = width // BLOCKS
+    tiles = count // STEP
+
+    def body(place, *refs):
+        hidden, grad_normed, low, mine, other = refs[:5]
+        gate_b, gate_c, value_part, conv, later, taps, gain_one, gain_two = refs[5:13]
+        sources = refs[13:15]
+        grad_own, grad_other, grads, turned, sums = refs[15:20]
+        inward, outward, extended, sems = refs[20:]
+        step = pl.program_id(0)
+        tile = tiles - 1 - step
+
+        @pl.when(step == 0)
+        def _():
+            copies = mix_copies(sources, inward, outward, sems)
+            for copy in copies:
+                copy.start()
+            sums[...] = jnp.zeros_like(sums)
+            extended[STEP:, :] = later[...]
+            for copy in copies:
+                copy.wait()
+
+        @pl.when(step > 0)
+        def _():
+            extended[STEP:, :] = extended[:8, :]
+
+        grad, gain_terms = hidden_backward(
+            hidden[...], grad_normed[...], low[...].astype(f32), gain_two[...]
+        )
+        sums[1:2, :] += jnp.sum(gain_terms, axis=0, keepdims=True)
+        grad_o = grad.astype(bf16)
+        turned[...] = grad.T.astype(bf16)
+        grad_carried = dot(grad_o, outward[...])
+        extended[:STEP, :] = grad_carried * gate_c[...].astype(f32)
+        grad_c = (grad_carried * conv[...].astype(f32)).astype(bf16)
+        left_gate, right_gate = gate_b[...].astype(f32), value_part[...].astype(f32)
+        product = left_gate * right_gate
+        grad_product = jnp.zeros((STEP, width), f32)
+        for lag in range(KCONV):
+            slot, start = slots(place, tile * STEP + lag, STEP)
+            keep = (slot - lag >= start).astype(f32)
+            masked = keep * extended[lag : lag + STEP, :]
+            grad_product = grad_product + taps[lag : lag + 1, :] * masked
+            sums[2 + lag : 3 + lag, :] += jnp.sum(masked * product, axis=0, keepdims=True)
+        grad_b = (grad_product * right_gate).astype(bf16)
+        grad_v = (grad_product * left_gate).astype(bf16)
+        for s in range(BLOCKS):
+            lanes = slice(s * n, (s + 1) * n)
+            at = s * 3 * n
+            grads[:, at : at + n] = grad_b[:, lanes]
+            grads[:, at + n : at + 2 * n] = grad_c[:, lanes]
+            grads[:, at + 2 * n : at + 3 * n] = grad_v[:, lanes]
+        grad_first = dot_nt(grads[...], inward[...])
+        left, right = mine[...].astype(f32), other[...].astype(f32)
+        rstd = inverse_rms(left, right)
+        scaled = grad_first * gain_one[...]
+        mean = (
+            jnp.sum(scaled[:, :half] * left, axis=1, keepdims=True)
+            + jnp.sum(scaled[:, half:] * right, axis=1, keepdims=True)
+        ) / width
+        for i, (value, target) in enumerate(((left, grad_own), (right, grad_other))):
+            lanes = slice(i * half, (i + 1) * half)
+            sums[0:1, lanes] += jnp.sum(grad_first[:, lanes] * value * rstd, axis=0, keepdims=True)
+            target[...] = (
+                grad[:, lanes] + (rstd * scaled[:, lanes] - value * (rstd * rstd * rstd) * mean)
+            ).astype(bf16)
+
+    def tile_of(m):
+        return tiles - 1 - m
+
+    rows = pl.BlockSpec((STEP, width), lambda m, place: (tile_of(m), 0))
+    one = pl.BlockSpec((1, width), lambda m, place: (0, 0))
+    eight = pl.BlockSpec((8, width), lambda m, place: (0, 0))
+    narrow = pl.BlockSpec((STEP, half), lambda m, place: (tile_of(m), 0))
+    return call(
+        body,
+        "mix_backward",
+        (
+            shape_of(count, half),
+            shape_of(count, half),
+            shape_of(count, 3 * width),
+            shape_of(width, count),
+            shape_of(8, width, dtype=f32),
+        ),
+        flops=8 * count * width * width,
+        moved=44 * count * width,
+        tie=tie,
+        n_in=16,
+        grid_spec=scalar_grid(
+            (tiles,),
+            [
+                rows,
+                rows,
+                rows,
+                pl.BlockSpec(
+                    (STEP, half), lambda m, place: (place[1] * tiles + tile_of(m), 0)
+                ),
+                narrow,
+                rows,
+                rows,
+                rows,
+                rows,
+                eight,
+                pl.BlockSpec((KCONV, width), lambda m, place: (0, 0)),
+                one,
+                one,
+            ]
+            + [HERE] * 2,
+            [
+                narrow,
+                narrow,
+                pl.BlockSpec((STEP, 3 * width), lambda m, place: (tile_of(m), 0)),
+                pl.BlockSpec((width, STEP), lambda m, place: (0, tile_of(m))),
+                eight,
+            ],
+            [
+                pltpu.VMEM((width, 3 * width), bf16),
+                pltpu.VMEM((width, width), bf16),
+                pltpu.VMEM((STEP + 8, width), f32),
+                pltpu.SemaphoreType.DMA((4 * BLOCKS,)),
+            ],
+        ),
+    )(
+        place,
+        hidden,
+        grad_normed,
+        low,
+        tokens,
+        theirs,
+        *saved,
+        later,
+        taps,
+        gain_one,
+        gain_two,
+        *halves,
+        *tie,
+    )
+
+
+def mix_weights(place, normed_t, grad_t, grads, carried, received, tie):
+    width, count = normed_t.shape
+    half = width // 2
+    n = width // BLOCKS
+    side = 1 if received is None else 0
+
+    def body(place, normed_t, grad_t, grads, carried, *refs):
+        inward = dot(normed_t[...], grads[...])
+        outward = dot(grad_t[...], carried[...])
+        if received is None:
+            out = refs[0]
+            out[:, : 3 * n] = inward.astype(bf16)
+            out[:, 3 * n :] = outward.astype(bf16)
+        else:
+            received_part, keep, send, total = refs
+            total[:, : 3 * n] = inward + received_part[:, : 3 * n].astype(f32)
+            total[:, 3 * n :] = outward + received_part[:, 3 * n :].astype(f32)
+            keep_and_send(place, total, keep, send)
+
+    left = pl.BlockSpec((half, count), lambda s, place: (side, 0))
+    part = pl.BlockSpec((half, 4 * n), lambda s, place: (0, s))
+    small = pl.BlockSpec((half // 2, 4 * n), lambda s, place: (0, s))
+    more = [] if received is None else [received]
+    return call(
+        body,
+        "mix_weights",
+        (shape_of(half // 2, 4 * width),) * 2 if more else shape_of(half, 4 * width),
+        flops=8 * count * half * width,
+        moved=2 * (2 * half * count + (count + half) * 4 * width),
+        tie=tie,
+        n_in=5 + len(more),
+        grid_spec=scalar_grid(
+            (BLOCKS,),
+            [
+                left,
+                left,
+                pl.BlockSpec((count, 3 * n), lambda s, place: (0, s)),
+                pl.BlockSpec((count, n), lambda s, place: (0, s)),
+            ]
+            + [part] * len(more),
+            [small, small] if more else part,
+            [pltpu.VMEM((half, 4 * n), f32)] if more else [],
+        ),
+    )(place, normed_t, grad_t, grads, carried, *more, *tie)
+
+
+def after(value, *earlier):
+    return lax.optimization_barrier((value, *earlier))[0]
+
+
+def swap_cores(value):
+    return lax.ppermute(value, "col", [(0, 1), (1, 0)])
+
+
+def across_first(value):
+    return lax.ppermute(
+        value, ("dp", "col"), [(2 * p + c, 2 * (p ^ (1 << c)) + c) for p in range(4) for c in range(2)]
+    )
+
+
+def across_second(value):
+    return lax.ppermute(
+        value, ("dp", "col"), [(2 * p + c, 2 * (p ^ (2 >> c)) + c) for p in range(4) for c in range(2)]
+    )
+
+
+def along_row(value, steps):
+    return lax.ppermute(value, "row", [(i, (i + steps) % BLOCKS) for i in range(BLOCKS)])
+
+
+def quarters(part):
+    across = across_first(part)
+    return (part, across, across_second(part), across_second(across))
+
+
+def add(*parts):
+    return sum(part.astype(f32) for part in parts).astype(bf16)
+
+
+def upper(value):
+    return value[: value.shape[0] // 2]
+
+
+def lower(value):
+    return value[value.shape[0] // 2 :]
+
+
+def block_of(value, b, axis=0):
+    width = value.shape[axis] // BLOCKS
+    return lax.dynamic_slice_in_dim(value, b * width, width, axis)
+
+
+def later_rows(value):
+    pairs = [(i, i - 1) for i in range(1, 2 * BLOCKS)]
+    value = lax.ppermute(value, ("row", "col"), pairs)
+    parts = jnp.split(value, BLOCKS, axis=1)
+    order = [OFFSETS.index(offset % BLOCKS - 1) for offset in OFFSETS]
+    moved = jnp.concatenate([parts[i] for i in order], axis=1)
+    return jnp.where(lax.axis_index("col") == 1, moved, value)
+
+
+def shards(
+    tokens,
+    cotangent,
+    seq_lens,
+    norm1_gain,
+    in_weight,
+    conv_weight,
+    out_weight,
+    norm2_gain,
+    gate_up_weight,
+    down_weight,
+):
+    dp, row, core = lax.axis_index("dp"), lax.axis_index("row"), lax.axis_index("col")
+    count, half = tokens.shape[0] // 2, tokens.shape[1]
+    position = ((dp * BLOCKS + row) * 2 + core) * count
+    lengths = lax.dynamic_slice_in_dim(seq_lens, position // ROW_LEN, 1, 0)[0]
+    place = jnp.stack(
+        [dp, core, position % ROW_LEN, lengths[0], lengths[0] + lengths[1]]
+    ).astype(jnp.int32)
+
+    def of_the_other(value):
+        return lax.dynamic_slice_in_dim(value, (1 - core) * count, count, 0)
+
+    mix_first = pack(in_weight, out_weight, place, 1, conv_weight)
+    mix_quarters = [along_row(mix_first, -offset) for offset in OFFSETS[1:]]
+    before = lax.ppermute(
+        after(tokens[2 * count - HALO :], mix_first),
+        "row",
+        [(i, i + 1) for i in range(BLOCKS - 1)],
+    )
+    own_gains = jnp.pad(jnp.stack([norm1_gain, norm2_gain]), ((0, HALO - 2), (0, 0)))
+    mix_own = pack(in_weight, out_weight, place, 4, tie=[mix_first])
+    feed_own = pack(gate_up_weight, down_weight, place, 4, tie=[mix_own])
+    sent = outgoing(place, tokens, cotangent, before, own_gains)
+    theirs = swap_cores(sent)
+    joined = join_rows(mix_quarters, [mix_own, feed_own, sent])
+    feed_first = pack(gate_up_weight, down_weight, place, 1, tie=[joined])
+    gains = jnp.concatenate([own_gains[:2], theirs[2 * count + HALO :][:2]], axis=1).astype(f32)
+    gain_one, gain_two = gains[:1], gains[1:]
+    normed, normed_t, low, low_t = prepare(
+        place, tokens, theirs, before, cotangent, gain_one, [joined]
+    )
+    width = half // 4
+    taps = jnp.concatenate(
+        [conv_weight] + [part[width : width + KCONV, : conv_weight.shape[1]] for part in mix_quarters],
+        axis=1,
+    ).astype(f32)
+    quarter_one = along_row(feed_first, -OFFSETS[1])
+    mix_half = mix_assemble(mix_own, quarters(joined), place, [normed, quarter_one])
+    mix_halves = [mix_half, swap_cores(mix_half)]
+    half_one = lax.all_gather(after(quarter_one, mix_half), "dp", axis=0, tiled=True)
+
+    *saved, hidden, carried, normed_two, normed_two_t = mix_forward(
+        place, normed, mix_halves, tokens, theirs, taps, gain_two, []
+    )
+    feed_halves, others = [feed_own], [swap_cores(feed_own)]
+    activations, from_them = [], []
+
+    def gathered(k, last, here):
+        part = along_row(after(feed_first, last), -OFFSETS[k])
+        return lax.all_gather(after(part, here), "dp", axis=0, tiled=True)
+
+    def have(half):
+        feed_halves.append(half)
+        others.append(swap_cores(half))
+
+    def activate(grad, tie):
+        k = len(activations)
+        grad, acts, for_them = feed(
+            normed_two, low, normed_two_t, low_t, feed_halves[k], others[k], grad, tie
+        )
+        activations.append(acts)
+        from_them.append(swap_cores(for_them))
+        return grad, for_them
+
+    def weights_of(k, tie):
+        keep, send = feed_weights(place, normed_two_t, low_t, activations[k], from_them[k], tie)
+        return keep, across_second(send)
+
+    grad_normed_two, done = activate(None, [])
+    half_two = gathered(2, hidden, done)
+    have(after(half_one, done))
+    last = done
+    grad_normed_two, done = activate(grad_normed_two, [])
+    half_three = gathered(3, last, done)
+    keep, send = weights_of(0, [done])
+    have(after(half_two, keep))
+    grad_normed_two, done = activate(grad_normed_two, [keep])
+    zero = (keep, send)
+    keep, send = weights_of(1, [done, send])
+    have(after(half_three, keep))
+    grad_normed_two, done = activate(grad_normed_two, [keep])
+    one = add(keep, send)
+    keep, send = weights_of(2, [done, send])
+    one_across = across_first(lower(after(one, keep)))
+    first = first_rows(hidden, grad_normed_two, low, saved[1], gain_two, mix_halves)
+    later = later_rows(first)
+    one = add(upper(one), one_across)
+    two = add(keep, send)
+    keep, send = weights_of(3, [keep, first, one])
+    one = along_row(one, OFFSETS[1])
+    zero_across = across_first(after(add(*map(lower, zero)), keep))
+
+    grad_own, grad_other, grads, grad_t, sums = mix_backward(
+        place,
+        hidden,
+        grad_normed_two,
+        low,
+        tokens,
+        theirs,
+        saved,
+        later,
+        taps,
+        gain_one,
+        gain_two,
+        mix_halves,
+        [keep, two],
+    )
+    two = add(upper(two), across_first(lower(after(two, keep))))
+    three = add(keep, send)
+    where = jnp.array([OFFSETS.index(offset) for offset in (0, 1, 2, -1)], jnp.int32)
+    own_taps = jnp.concatenate(
+        [block_of(sums[2:], where[(b - row) % BLOCKS], 1) for b in range(BLOCKS)], axis=1
+    )
+    packed_sums = jnp.concatenate([sums[:2], own_taps], axis=0)
+    every = lax.all_gather(packed_sums, ("dp", "row", "col"), axis=0)
+    sums = jnp.sum(every.reshape(16, 2, *packed_sums.shape), axis=0)
+    mine, other = sums[core], sums[1 - core]
+    gain_grads = mine[:2, :half] + other[:2, half:]
+    taps_grad = block_of(mine[2 : 2 + KCONV] + other[2 : 2 + KCONV], row, 1)
+
+    for_them = mix_weights(place, normed_t, grad_t, grads, carried, None, [one, two, three, packed_sums])
+    received = swap_cores(for_them)
+    three = add(upper(three), across_first(lower(three)))
+    two = along_row(two, OFFSETS[2])
+    grad_theirs = swap_cores(grad_other)
+    keep, send = mix_weights(
+        place, normed_t, grad_t, grads, carried, received, [three, grad_theirs, two]
+    )
+    send = across_second(send)
+    three = along_row(three, OFFSETS[3])
+    own_out, other_out = feed_output(hidden, activations, feed_halves, others, [keep])
+    three, send = lax.optimization_barrier((three, send, own_out))[:2]
+    other_out = swap_cores(other_out)
+    feed_sum = add(*map(upper, zero), zero_across, one, two, three)
+    feed_sum = quarters(feed_sum)
+    go = across_first(add(lower(keep), lower(send)))
+    mix_quarters = jnp.split(add(upper(keep), upper(send), go), BLOCKS, axis=1)
+    mix_quarters = [along_row(part, OFFSETS[k]) if k else part for k, part in enumerate(mix_quarters)]
+    mix_sum = quarters(add(*mix_quarters))
+    output_back = join_tokens(own_out, other_out, place)
+    input_back = join_tokens(grad_own, grad_theirs, place)
+    gate_up_grad, down_grad = unpack(feed_sum, 2, place)
+    in_grad, out_grad = unpack(mix_sum, 3, place)
+    return (
+        output_back,
+        input_back,
+        gain_grads[0],
+        in_grad,
+        taps_grad,
+        out_grad,
+        gain_grads[1],
+        gate_up_grad,
+        down_grad,
+    )
 
 
 def from_behind(value, axis, steps):
@@ -23,7 +1214,7 @@
     return flat_rank * count + jnp.arange(count + extra, dtype=jnp.int32)
 
 
-def slot_masks(seq_lens, count, extra):
+def flat_slot_masks(seq_lens, count, extra):
     position = token_index(count, extra)
     packed = position // ROW_LEN
     place = position - packed * ROW_LEN
@@ -59,7 +1250,7 @@
     return (gain_first, in_full, conv_full, out_full, gain_second, gate_full, down_full)
 
 
-def norm_backward(values, rstd, gain, grad_normed):
+def flat_norm_backward(values, rstd, gain, grad_normed):
     scaled = grad_normed * gain
     gain_grad = jnp.sum(grad_normed * values * rstd, axis=0)
     grad_values = rstd * scaled - values * (rstd * rstd * rstd) * jnp.mean(
@@ -80,7 +1271,7 @@
     return jnp.einsum("te,de->td", grad, matrix, preferred_element_type=jnp.float32)
 
 
-def shards(
+def flat_shards(
     tokens,
     cotangent,
     seq_lens,
@@ -101,7 +1292,7 @@
     )
     count, width = own_tokens.shape
     reach = KCONV - 1
-    valid_slot, keep_masks = slot_masks(seq_lens, count, reach)
+    valid_slot, keep_masks = flat_slot_masks(seq_lens, count, reach)
     conv_taps = conv_full.astype(jnp.float32)
     gain_one_f = gain_first.astype(jnp.float32)
     gain_two_f = gain_second.astype(jnp.float32)
@@ -142,7 +1333,7 @@
     grad_up = (grad_active * silu_gate).astype(jnp.bfloat16)
     gate_grad = jnp.stack([weight_grad(normed_two, grad_gate), weight_grad(normed_two, grad_up)])
     grad_normed_two = back_project(grad_gate, gate_full[0]) + back_project(grad_up, gate_full[1])
-    grad_second, gain_second_part = norm_backward(hidden, rstd_second, gain_two_f, grad_normed_two)
+    grad_second, gain_second_part = flat_norm_backward(hidden, rstd_second, gain_two_f, grad_normed_two)
     grad_hidden = grad_out + grad_second
     grad_o = grad_hidden.astype(jnp.bfloat16)
     out_grad = weight_grad(carried, grad_o)
@@ -174,7 +1365,7 @@
         + back_project(grad_gate_c, in_full[1])
         + back_project(grad_value, in_full[2])
     )
-    grad_first, gain_first_part = norm_backward(inputs, rstd_first, gain_one_f, grad_normed)
+    grad_first, gain_first_part = flat_norm_backward(inputs, rstd_first, gain_one_f, grad_normed)
     input_grad = (grad_hidden + grad_first).astype(jnp.bfloat16)
     output_back, input_back = (
         lax.all_to_all(output.astype(jnp.bfloat16), "col", split_axis=1, concat_axis=0, tiled=True),
@@ -221,8 +1412,9 @@
 
 
 def solution(mesh):
+    ring = mesh.shape["dp"] == 4 and mesh.shape["row"] == BLOCKS and mesh.shape["col"] == 2
     return jax.shard_map(
-        shards,
+        shards if ring else flat_shards,
         mesh=mesh,
         in_specs=(
             P(("dp", "row"), "col"),

time: 1580 us -> 571 us (0.36)
  waiting for transfers between devices: 1150 us -> 159 us
  Pallas kernels: 0 us -> 283 us
  matrix products: 224 us -> 0 us
  blocking collectives: 73.9 us -> 0 us
  starting transfers between devices: 13 us -> 45.9 us
  other arithmetic: 56.2 us -> 31.5 us
  local copies, waits for them, and re-layouts: 41 us -> 22.3 us
    reduce_scatter x8 -> x0, waiting for transfers between devices: 690 us -> none  [the longest x1 317 us: shards(): lax.psum_scatter(gate_cols, 'row', scatter_dimension=2, tiled=True)]
    all_gather x8 -> x4, waiting for transfers between devices: 346 us -> 13.9 us  [the longest x2 13.9 us: gathered(): return lax.all_gather(after(part, here), 'dp', axis=0, tiled=True)]
    pallas_call x0 -> x26, Pallas kernels: none -> 283 us  [the longest x4 102 us: feed(): call(body, 'feed', (shape_of(count, width, dtype=f32), shape_of(count, la...]
    dot_general x21 -> x0, matrix products: 224 us -> none  [the longest x7 87.5 us: back_project(): jnp.einsum('te,de->td', grad, matrix, preferred_element_type=jnp.float32)]
    ppermute x2 -> x46, waiting for transfers between devices: 0.01 us -> 145 us  [the longest x12 61.9 us: along_row(): lax.ppermute(value, 'row', [(i, (i + steps) % BLOCKS) for i in range(BLOC...]
    psum x1 -> x0, waiting for transfers between devices: 107 us -> none  [shards(): lax.psum((in_part, out_part, gate_part, down_part), 'dp')]
    ppermute x2 -> x46, starting transfers between devices: 3.41 us -> 45.3 us  [the longest x12 16.5 us: along_row(): lax.ppermute(value, 'row', [(i, (i + steps) % BLOCKS) for i in range(BLOC...]
    psum x1 -> x0, blocking collectives: 41.6 us -> none  [shards(): lax.psum((gain_first_part, gain_second_part, conv_grad), ('dp', 'row', 'c...]
  transfers between devices with their start and end apart: 21 -> 50, of which waited for: 12 -> 20; matrix products, arithmetic and copies ran while one was open for 14% -> 8% of each run, Pallas kernels for 0% -> 44%
where the time goes in v2:
time: 571 us; the launch traced here: 560 us
  Pallas kernels  283 us (50%)
  waiting for transfers between devices  159 us (28%)
  starting transfers between devices  45.9 us (8%)
  other arithmetic  31.5 us (6%)
  local copies, waits for them, and re-layouts  22.3 us (4%)
  between operations  18.3 us (3%)
    pallas_call x4, Pallas kernels, feed(): call(body, 'feed', (shape_of(count, width, dtype=f32), shape_of(count, la...  102 us
    ppermute x12, waiting for transfers between devices, along_row(): lax.ppermute(value, 'row', [(i, (i + steps) % BLOCKS) for i in range(BLOC...  61.9 us
    ppermute x8, waiting for transfers between devices, across_first(): lax.ppermute(value, ('dp', 'col'), [(2 * p + c, 2 * (p ^ 1 << c) + c) for...  57 us
    pallas_call x4, Pallas kernels, feed_weights(): call(body, 'feed_weights', (shape_of(half // 2, lanes),) * 2, flops=6 * c...  40.3 us
    convert_element_type x11, other arithmetic, add(): return sum((part.astype(f32) for part in parts)).astype(bf16)  27.1 us
    pallas_call x1, Pallas kernels, mix_backward(): call(body, 'mix_backward', (shape_of(count, half), shape_of(count, half),...  25.9 us
    pallas_call x1, Pallas kernels, mix_forward(): call(body, 'mix_forward', (flat, flat, flat, flat, wide, flat, flat, shap...  23.3 us
    pallas_call x2, Pallas kernels, mix_weights(): call(body, 'mix_weights', (shape_of(half // 2, 4 * width),) * 2 if more e...  20.7 us
  transfers between devices with their start and end apart: 50, of which 20 were waited for; matrix products, arithmetic and copies ran while one was open for 8% of the time, Pallas kernels for 44%

profile of v2, /device:TPU:0, one launch (start us, length us, event | category | flops | bytes accessed | tf_op | source)
XLA Modules:
  0.0 559.5 jit_solution(6729956579752918330)
XLA Ops:
  14.1 4.9 collective-permute-start
  30.1 4.2 pack.5.refs_3_.refs_1_
  34.3 5.2 pack.6.refs_4_.refs_5_
  42.5 13.2 %collective-permute-done.4.refs_2_ = bf16[144,1024]{1,0:T(8,128)(2,1)S(1)} collective-permute-done((bf16[144,1024]{1,0:T(8,128)(2,1)S(1)}, bf16[144,1024]{1,0:T(8,128)(2,1)S(1)}, u32[]{:S(2)}, u32[]{:S(2)}) %collective-permute-start.4) | collective-permute-done | bytes 294944 | tf_op jit(solution)/shard_map/ppermute | solution.py:1003
  64.5 16.6 %collective-permute-done.5.refs_3_ = bf16[432,1024]{1,0:T(8,128)(2,1)} collective-permute-done((bf16[432,1024]{1,0:T(8,128)(2,1)}, bf16[432,1024]{1,0:T(8,128)(2,1)}, u32[]{:S(2)}, u32[]{:S(2)}) %collective-permute-start.5) | collective-permute-done | bytes 884768 | tf_op jit(solution)/shard_map/ppermute | solution.py:991
  83.5 7.5 %prepare.1 = (bf16[1040,1024]{1,0:T(8,128)(2,1)}, bf16[1024,1024]{1,0:T(8,128)(2,1)}, bf16[1024,1024]{1,0:T(8,128)(2,1)}, bf16[1024,1024]{1,0:T(8,128)(2,1)}) custom-call(s32[5]{0:T(128)} %stack.29.place.refs_0_, bf16[2048,512]{1,0:T(8,128)(2,1)} %refs_4_.3, bf16[2080,512]{1,0:T(8,128)(2,1)} %collective-permute-done.1.refs_2_.refs_5_.refs_7_.refs_4_, ...), custom_call_target="tpu_custom_call" | custom-call | bytes 16777216 | tf_op jit(solution)/shard_map/prepare/pallas_call | solution.py:312
  94.4 4.6 mix_assemble.1.refs_1_.refs_0_.refs_14_
  102.3 4.2 collective-permute-done.9.refs_2_.refs_1_.refs_15_
  106.5 23.3 %mix_forward.1 = (bf16[1024,1024]{1,0:T(8,128)(2,1)}, bf16[1024,1024]{1,0:T(8,128)(2,1)}, bf16[1024,1024]{1,0:T(8,128)(2,1)}, bf16[1024,1024]{1,0:T(8,128)(2,1)}...) custom-call(s32[5]{0:T(128)} %stack.29.place.refs_0_, ...), custom_call_target="tpu_custom_call" | custom-call | flops 8589934592 | bytes 39845888 | tf_op jit(solution)/shard_map/mix_forward/pallas_call | solution.py:486
  132.4 25.3 %feed.4 = (f32[1024,1024]{1,0:T(8,128)}, bf16[1024,3456]{1,0:T(8,128)(2,1)}, bf16[512,3456]{1,0:T(8,128)(2,1)}) custom-call(bf16[1024,1024]{1,0:T(8,128)(2,1)} %get-tuple-element.71.refs_0_.normed_hbm, bf16[1024,1024]{1,0:T(8,128)(2,1)} %get-tuple-element.72.refs_1_.low_hbm.low.refs_3_, bf16[1024,1024]{1,0:T(8,128)(2,1)} %get-tuple-element.73.refs_2_.normed_t_hbm.refs_1_, ...), custom_call_target="tpu_custom_call" | custom-call | flops 15703474176 | bytes 34471936 | tf_op jit(solution)/shard_map/feed/pallas_call | solution.py:646
  159.3 5.0 collective-permute-done.11.other_hbm.refs_10_
  164.3 25.6 %feed.5 = (f32[1024,1024]{1,0:T(8,128)}, bf16[1024,3456]{1,0:T(8,128)(2,1)}, bf16[512,3456]{1,0:T(8,128)(2,1)}) custom-call(bf16[1024,1024]{1,0:T(8,128)(2,1)} %get-tuple-element.71.refs_0_.normed_hbm, bf16[1024,1024]{1,0:T(8,128)(2,1)} %get-tuple-element.72.refs_1_.low_hbm.low.refs_3_, bf16[1024,1024]{1,0:T(8,128)(2,1)} %get-tuple-element.73.refs_2_.normed_t_hbm.refs_1_, ...), custom_call_target="tpu_custom_call" | custom-call | flops 15703474176 | bytes 34471936 | tf_op jit(solution)/shard_map/feed/pallas_call | solution.py:646
  190.0 10.0 %feed_weights.4 = (bf16[256,3456]{1,0:T(8,128)(2,1)}, bf16[256,3456]{1,0:T(8,128)(2,1)}) custom-call(s32[5]{0:T(128)} %stack.29.place.refs_0_, bf16[1024,1024]{1,0:T(8,128)(2,1)} %get-tuple-element.73.refs_2_.normed_t_hbm.refs_1_, bf16[1024,1024]{1,0:T(8,128)(2,1)} %get-tuple-element.74.refs_3_.low_t_hbm.refs_2_, ...), custom_call_target="tpu_custom_call" | custom-call | flops 3623878656 | bytes 16252928 | tf_op jit(solution)/shard_map/feed_weights/pallas_call | solution.py:735
  210.3 26.0 %feed.6 = (f32[1024,1024]{1,0:T(8,128)}, bf16[1024,3456]{1,0:T(8,128)(2,1)}, bf16[512,3456]{1,0:T(8,128)(2,1)}) custom-call(bf16[1024,1024]{1,0:T(8,128)(2,1)} %get-tuple-element.71.refs_0_.normed_hbm, bf16[1024,1024]{1,0:T(8,128)(2,1)} %get-tuple-element.72.refs_1_.low_hbm.low.refs_3_, bf16[1024,1024]{1,0:T(8,128)(2,1)} %get-tuple-element.73.refs_2_.normed_t_hbm.refs_1_, ...), custom_call_target="tpu_custom_call" | custom-call | flops 15703474176 | bytes 34471936 | tf_op jit(solution)/shard_map/feed/pallas_call | solution.py:646
  238.0 10.1 %feed_weights.5 = (bf16[256,3456]{1,0:T(8,128)(2,1)}, bf16[256,3456]{1,0:T(8,128)(2,1)}) custom-call(s32[5]{0:T(128)} %stack.29.place.refs_0_, bf16[1024,1024]{1,0:T(8,128)(2,1)} %get-tuple-element.73.refs_2_.normed_t_hbm.refs_1_, bf16[1024,1024]{1,0:T(8,128)(2,1)} %get-tuple-element.74.refs_3_.low_t_hbm.refs_2_, ...), custom_call_target="tpu_custom_call" | custom-call | flops 3623878656 | bytes 16252928 | tf_op jit(solution)/shard_map/feed_weights/pallas_call | solution.py:735
  248.1 10.1 %all-gather.10.cloned.1.call-done.refs_4_.refs_8_ = bf16[512,3456]{1,0:T(8,128)(2,1)} async-done(((bf16[128,3456]{1,0:T(8,128)(2,1)}), bf16[512,3456]{1,0:T(8,128)(2,1)}) %all-gather.10.cloned.1.call-update) | async-done | bytes 3538960 | tf_op jit(solution)/shard_map/all_gather | solution.py:1097
  260.2 4.6 collective-permute-done.18.refs_5_.refs_12_
  264.8 25.4 %feed.7 = (f32[1024,1024]{1,0:T(8,128)}, bf16[1024,3456]{1,0:T(8,128)(2,1)}, bf16[512,3456]{1,0:T(8,128)(2,1)}) custom-call(bf16[1024,1024]{1,0:T(8,128)(2,1)} %get-tuple-element.71.refs_0_.normed_hbm, bf16[1024,1024]{1,0:T(8,128)(2,1)} %get-tuple-element.72.refs_1_.low_hbm.low.refs_3_, bf16[1024,1024]{1,0:T(8,128)(2,1)} %get-tuple-element.73.refs_2_.normed_t_hbm.refs_1_, ...), custom_call_target="tpu_custom_call" | custom-call | flops 15703474176 | bytes 34471936 | tf_op jit(solution)/shard_map/feed/pallas_call | solution.py:646
  294.1 10.1 %feed_weights.6 = (bf16[256,3456]{1,0:T(8,128)(2,1)}, bf16[256,3456]{1,0:T(8,128)(2,1)}) custom-call(s32[5]{0:T(128)} %stack.29.place.refs_0_, bf16[1024,1024]{1,0:T(8,128)(2,1)} %get-tuple-element.73.refs_2_.normed_t_hbm.refs_1_, bf16[1024,1024]{1,0:T(8,128)(2,1)} %get-tuple-element.74.refs_3_.low_t_hbm.refs_2_, ...), custom_call_target="tpu_custom_call" | custom-call | flops 3623878656 | bytes 16252928 | tf_op jit(solution)/shard_map/feed_weights/pallas_call | solution.py:735
  315.6 11.7 %collective-permute-done.23 = bf16[128,3456]{1,0:T(8,128)(2,1)} collective-permute-done((bf16[128,3456]{1,0:T(8,128)(2,1)S(1)}, bf16[128,3456]{1,0:T(8,128)(2,1)}, u32[]{:S(2)}, u32[]{:S(2)}) %collective-permute-start.23) | collective-permute-done | bytes 884768 | tf_op jit(solution)/shard_map/ppermute | solution.py:991
  340.1 10.1 %feed_weights.7 = (bf16[256,3456]{1,0:T(8,128)(2,1)}, bf16[256,3456]{1,0:T(8,128)(2,1)}) custom-call(s32[5]{0:T(128)} %stack.29.place.refs_0_, bf16[1024,1024]{1,0:T(8,128)(2,1)} %get-tuple-element.73.refs_2_.normed_t_hbm.refs_1_, bf16[1024,1024]{1,0:T(8,128)(2,1)} %get-tuple-element.74.refs_3_.low_t_hbm.refs_2_, ...), custom_call_target="tpu_custom_call" | custom-call | flops 3623878656 | bytes 16252928 | tf_op jit(solution)/shard_map/feed_weights/pallas_call | solution.py:735
  354.4 25.9 %mix_backward.1 = (bf16[1024,512]{1,0:T(8,128)(2,1)}, bf16[1024,512]{1,0:T(8,128)(2,1)}, bf16[1024,3072]{1,0:T(8,128)(2,1)}, bf16[1024,1024]{1,0:T(8,128)(2,1)}, f32[8,1024]{1,0:T(8,128)}) custom-call(s32[5]{0:T(128)} %stack.29.place.refs_0_, f32[1024,1024]{1,0:T(8,128)} %get-tuple-element.70.hidden.refs_1_.refs_0_, ...), custom_call_target="tpu_custom_call" | custom-call | flops 8589934592 | bytes 46137344 | tf_op jit(solution)/shard_map/mix_backward/pallas_call | solution.py:871
  389.2 9.7 %mix_weights.2 = bf16[512,4096]{1,0:T(8,128)(2,1)} custom-call(s32[5]{0:T(128)} %stack.29.place.refs_0_, bf16[1024,1024]{1,0:T(8,128)(2,1)} %get-tuple-element.96.refs_1_, bf16[1024,1024]{1,0:T(8,128)(2,1)} %get-tuple-element.108.refs_2_, bf16[1024,3072]{1,0:T(8,128)(2,1)} %get-tuple-element.109.refs_3_, bf16[1024,1024]{1,0:T(8,128)(2,1)} %get-tuple-element.110.refs_4_, ...), custom_call_target="tpu_custom_call" | custom-call | flops 4294967296 | bytes 14680064 | tf_op jit(solution)/shard_map/mix_weights/pallas_call | solution.py:959
  403.4 10.0 %collective-permute-done.29 = bf16[128,3456]{1,0:T(8,128)(2,1)S(1)} collective-permute-done((bf16[128,3456]{1,0:T(8,128)(2,1)S(1)}, bf16[128,3456]{1,0:T(8,128)(2,1)S(1)}, u32[]{:S(2)}, u32[]{:S(2)}) %collective-permute-start.29) | collective-permute-done | bytes 884768 | tf_op jit(solution)/shard_map/ppermute | solution.py:991
  414.6 11.4 %collective-permute-done.31.refs_8_ = bf16[128,3456]{1,0:T(8,128)(2,1)} collective-permute-done((bf16[128,3456]{1,0:T(8,128)(2,1)}, bf16[128,3456]{1,0:T(8,128)(2,1)}, u32[]{:S(2)}, u32[]{:S(2)}) %collective-permute-start.31) | collective-permute-done | bytes 884768 | tf_op jit(solution)/shard_map/ppermute | solution.py:1003
  426.0 11.0 %mix_weights.3 = (bf16[256,4096]{1,0:T(8,128)(2,1)}, bf16[256,4096]{1,0:T(8,128)(2,1)}) custom-call(s32[5]{0:T(128)} %stack.29.place.refs_0_, bf16[1024,1024]{1,0:T(8,128)(2,1)} %get-tuple-element.96.refs_1_, bf16[1024,1024]{1,0:T(8,128)(2,1)} %get-tuple-element.108.refs_2_, bf16[1024,3072]{1,0:T(8,128)(2,1)} %get-tuple-element.109.refs_3_, ...), custom_call_target="tpu_custom_call" | custom-call | flops 4294967296 | bytes 14680064 | tf_op jit(solution)/shard_map/mix_weights/pallas_call | solution.py:959
  442.3 17.6 %feed_output.1 = (bf16[1024,512]{1,0:T(8,128)(2,1)}, bf16[1024,512]{1,0:T(8,128)(2,1)}) custom-call(f32[1024,1024]{1,0:T(8,128)} %get-tuple-element.70.hidden.refs_1_.refs_0_, bf16[1024,3456]{1,0:T(8,128)(2,1)} %get-tuple-element.75.refs_3_.refs_1_, bf16[1024,3456]{1,0:T(8,128)(2,1)} %get-tuple-element.80.refs_3_.refs_2_, ...), custom_call_target="tpu_custom_call" | custom-call | flops 9663676416 | bytes 25165824 | tf_op jit(solution)/shard_map/feed_output/pallas_call | solution.py:689
  460.0 23.1 %collective-permute-done.33 = bf16[128,3456]{1,0:T(8,128)(2,1)} collective-permute-done((bf16[128,3456]{1,0:T(8,128)(2,1)S(1)}, bf16[128,3456]{1,0:T(8,128)(2,1)}, u32[]{:S(2)}, u32[]{:S(2)}) %collective-permute-start.33) | collective-permute-done | bytes 884768 | tf_op jit(solution)/shard_map/ppermute | solution.py:1003
  490.6 11.1 %collective-permute-done.35 = bf16[128,4096]{1,0:T(8,128)(2,1)S(1)} collective-permute-done((bf16[128,4096]{1,0:T(8,128)(2,1)S(1)}, bf16[128,4096]{1,0:T(8,128)(2,1)S(1)}, u32[]{:S(2)}, u32[]{:S(2)}) %collective-permute-start.35) | collective-permute-done | bytes 1048608 | tf_op jit(solution)/shard_map/ppermute | solution.py:991
  513.5 10.3 %collective-permute-done.38 = bf16[128,1024]{1,0:T(8,128)(2,1)S(1)} collective-permute-done((bf16[128,1024]{1,0:T(8,128)(2,1)}, bf16[128,1024]{1,0:T(8,128)(2,1)S(1)}, u32[]{:S(2)}, u32[]{:S(2)}) %collective-permute-start.38) | collective-permute-done | bytes 262176 | tf_op jit(solution)/shard_map/ppermute | solution.py:1003
  528.4 7.5 %collective-permute-done.39.refs_1_ = bf16[128,1024]{1,0:T(8,128)(2,1)S(1)} collective-permute-done((bf16[128,1024]{1,0:T(8,128)(2,1)S(1)}, bf16[128,1024]{1,0:T(8,128)(2,1)S(1)}, u32[]{:S(2)}, u32[]{:S(2)}) %collective-permute-start.39) | collective-permute-done | bytes 262176 | tf_op jit(solution)/shard_map/ppermute | solution.py:991
  541.4 6.1 %unpack.3 = (f32[2,512,1152]{2,1,0:T(8,128)}, f32[1152,512]{1,0:T(8,128)}) custom-call(s32[5]{0:T(128)} %stack.29.place.refs_0_, bf16[128,3456]{1,0:T(8,128)(2,1)} %add_convert_fusion.5.refs_0_, bf16[128,3456]{1,0:T(8,128)(2,1)} %collective-permute-done.43.refs_1_, bf16[128,3456]{1,0:T(8,128)(2,1)} %collective-permute-done.44.refs_2_, ...), custom_call_target="tpu_custom_call" | custom-call | tf_op jit(solution)/shard_map/unpack/pallas_call | solution.py:235
  (191 shorter events, 139.7 us)
Async XLA Ops:
  7.2 150.5 %all-gather.6.cloned.1.call-start = ((), (), s32[]{:S(2)}) async-start(), calls=%async_computation | async-start | bytes 4423680 | tf_op jit(solution)/shard_map/all_gather | solution.py:1087
  25.3 56.9 %collective-permute-start.1 = (bf16[2080,512]{1,0:T(8,128)(2,1)}, bf16[2080,512]{1,0:T(8,128)(2,1)}, u32[]{:S(2)}, u32[]{:S(2)}) collective-permute-start(bf16[2080,512]{1,0:T(8,128)(2,1)} %outgoing.1.refs_5_), channel_id=1, source_target_pairs={{0,1},{1,0},{2,3},{3,2},{4,5},{5,4},{6,7},{7,6},{8,9},{9,8},{10,11... | collective-permute-start | bytes 6389768 | tf_op jit(solution)/shard_map/ppermute | solution.py:987
  29.2 26.6 %collective-permute-start.4 = (bf16[144,1024]{1,0:T(8,128)(2,1)S(1)}, bf16[144,1024]{1,0:T(8,128)(2,1)S(1)}, u32[]{:S(2)}, u32[]{:S(2)}) collective-permute-start(bf16[144,1024]{1,0:T(8,128)(2,1)S(1)} %copy-done.12), channel_id=1, source_target_pairs={{0,4},{2,6},{4,0},{6,2},{1,5},{3,7},{5,1},{7,3},{8,12},{10,14},{12... | collective-permute-start | bytes 884744 | tf_op jit(solution)/shard_map/ppermute | solution.py:1003
  58.6 22.5 %collective-permute-start.5 = (bf16[432,1024]{1,0:T(8,128)(2,1)}, bf16[432,1024]{1,0:T(8,128)(2,1)}, u32[]{:S(2)}, u32[]{:S(2)}) collective-permute-start(bf16[432,1024]{1,0:T(8,128)(2,1)} %join_rows.1.refs_9_.refs_3_.refs_2_), channel_id=1, source_target_pairs={{0,8},{1,17},{8,0},{9,25},{16,24},{17,1},{24,16},{25,9},{2,10},{3,... | collective-permute-start | bytes 2654216 | tf_op jit(solution)/shard_map/ppermute | solution.py:991
  60.0 31.0 %collective-permute-start.6 = (bf16[432,1024]{1,0:T(8,128)(2,1)}, bf16[432,1024]{1,0:T(8,128)(2,1)}, u32[]{:S(2)}, u32[]{:S(2)}) collective-permute-start(bf16[432,1024]{1,0:T(8,128)(2,1)} %join_rows.1.refs_9_.refs_3_.refs_2_), channel_id=1, source_target_pairs={{0,16},{1,9},{8,24},{9,1},{16,0},{17,25},{24,8},{25,17},{2,18},{3,... | collective-permute-start | bytes 2654216 | tf_op jit(solution)/shard_map/ppermute | solution.py:997
  64.5 26.5 %collective-permute-start.8 = (bf16[128,3456]{1,0:T(8,128)(2,1)}, bf16[128,3456]{1,0:T(8,128)(2,1)S(1)}, u32[]{:S(2)}, u32[]{:S(2)}) collective-permute-start(bf16[128,3456]{1,0:T(8,128)(2,1)} %pack.7), channel_id=1, source_target_pairs={{0,2},{2,4},{4,6},{6,0},{1,3},{3,5},{5,7},{7,1},{8,10},{10,12},{12... | collective-permute-start | bytes 2654216 | tf_op jit(solution)/shard_map/ppermute | solution.py:1003
  99.1 104.7 %all-gather.8.cloned.1.call-start = ((), (), s32[]{:S(2)}) async-start(), calls=%async_computation.1 | async-start | bytes 4423680 | tf_op jit(solution)/shard_map/all_gather | solution.py:1097
  99.1 33.3 %collective-permute-start.10 = (bf16[512,3456]{1,0:T(8,128)(2,1)}, bf16[512,3456]{1,0:T(8,128)(2,1)}, u32[]{:S(2)}, u32[]{:S(2)}) collective-permute-start(bf16[512,3456]{1,0:T(8,128)(2,1)} %pack.6.refs_4_.refs_5_), channel_id=1, source_target_pairs={{0,1},{1,0},{2,3},{3,2},{4,5},{5,4},{6,7},{7,6},{8,9},{9,8},{10,11... | collective-permute-start | bytes 10616840 | tf_op jit(solution)/shard_map/ppermute | solution.py:987
  129.8 27.9 %collective-permute-start.12 = (bf16[128,3456]{1,0:T(8,128)(2,1)}, bf16[128,3456]{1,0:T(8,128)(2,1)S(1)}, u32[]{:S(2)}, u32[]{:S(2)}) collective-permute-start(bf16[128,3456]{1,0:T(8,128)(2,1)} %pack.7), channel_id=1, source_target_pairs={{0,6},{2,0},{4,2},{6,4},{1,7},{3,1},{5,3},{7,5},{8,14},{10,8},{12,... | collective-permute-start | bytes 2654216 | tf_op jit(solution)/shard_map/ppermute | solution.py:1003
  158.7 99.5 %all-gather.10.cloned.1.call-start = ((), (), s32[]{:S(2)}) async-start(), calls=%async_computation.2 | async-start | bytes 4423680 | tf_op jit(solution)/shard_map/all_gather | solution.py:1097
  158.8 31.2 %collective-permute-start.13 = (bf16[512,3456]{1,0:T(8,128)(2,1)}, bf16[512,3456]{1,0:T(8,128)(2,1)}, u32[]{:S(2)}, u32[]{:S(2)}) collective-permute-start(bf16[512,3456]{1,0:T(8,128)(2,1)} %get-tuple-element.77), channel_id=1, source_target_pairs={{0,1},{1,0},{2,3},{3,2},{4,5},{5,4},{6,7},{7,6},{8,9},{9,8},{10,11... | collective-permute-start | bytes 10616840 | tf_op jit(solution)/shard_map/ppermute | solution.py:987
  159.3 44.4 %collective-permute-start.15 = (bf16[128,3456]{1,0:T(8,128)(2,1)}, bf16[128,3456]{1,0:T(8,128)(2,1)S(1)}, u32[]{:S(2)}, u32[]{:S(2)}) collective-permute-start(bf16[128,3456]{1,0:T(8,128)(2,1)} %pack.7), channel_id=1, source_target_pairs={{0,4},{2,6},{4,0},{6,2},{1,5},{3,7},{5,1},{7,3},{8,12},{10,14},{12... | collective-permute-start | bytes 2654216 | tf_op jit(solution)/shard_map/ppermute | solution.py:1003
  204.7 306.9 %all-gather.12.cloned.1.call-start = ((), (), s32[]{:S(2)}) async-start(), calls=%async_computation.3 | async-start | bytes 1081344 | tf_op jit(solution)/shard_map/all_gather | solution.py:1162
  205.1 32.9 %collective-permute-start.16 = (bf16[512,3456]{1,0:T(8,128)(2,1)}, bf16[512,3456]{1,0:T(8,128)(2,1)}, u32[]{:S(2)}, u32[]{:S(2)}) collective-permute-start(bf16[512,3456]{1,0:T(8,128)(2,1)} %get-tuple-element.83.refs_5_), channel_id=1, source_target_pairs={{0,1},{1,0},{2,3},{3,2},{4,5},{5,4},{6,7},{7,6},{8,9},{9,8},{10,11... | collective-permute-start | bytes 10616840 | tf_op jit(solution)/shard_map/ppermute | solution.py:987
  205.7 32.3 %collective-permute-start.17 = (bf16[256,3456]{1,0:T(8,128)(2,1)}, bf16[256,3456]{1,0:T(8,128)(2,1)}, u32[]{:S(2)}, u32[]{:S(2)}) collective-permute-start(bf16[256,3456]{1,0:T(8,128)(2,1)} %get-tuple-element.91), channel_id=1, source_target_pairs={{0,16},{1,9},{8,24},{9,1},{16,0},{17,25},{24,8},{25,17},{2,18},{3,... | collective-permute-start | bytes 5308424 | tf_op jit(solution)/shard_map/ppermute | solution.py:997
  258.3 35.8 %collective-permute-start.21 = (bf16[512,3456]{1,0:T(8,128)(2,1)}, bf16[512,3456]{1,0:T(8,128)(2,1)}, u32[]{:S(2)}, u32[]{:S(2)}) collective-permute-start(bf16[512,3456]{1,0:T(8,128)(2,1)} %get-tuple-element.90.refs_5_), channel_id=1, source_target_pairs={{0,1},{1,0},{2,3},{3,2},{4,5},{5,4},{6,7},{7,6},{8,9},{9,8},{10,11... | collective-permute-start | bytes 10616840 | tf_op jit(solution)/shard_map/ppermute | solution.py:987
  258.8 31.6 %collective-permute-start.22 = (bf16[256,3456]{1,0:T(8,128)(2,1)}, bf16[256,3456]{1,0:T(8,128)(2,1)}, u32[]{:S(2)}, u32[]{:S(2)}) collective-permute-start(bf16[256,3456]{1,0:T(8,128)(2,1)} %get-tuple-element.103), channel_id=1, source_target_pairs={{0,16},{1,9},{8,24},{9,1},{16,0},{17,25},{24,8},{25,17},{2,18},{3,... | collective-permute-start | bytes 5308424 | tf_op jit(solution)/shard_map/ppermute | solution.py:997
  290.2 49.9 %collective-permute-start.20 = (bf16[512,3456]{1,0:T(8,128)(2,1)}, bf16[512,3456]{1,0:T(8,128)(2,1)}, u32[]{:S(2)}, u32[]{:S(2)}) collective-permute-start(bf16[512,3456]{1,0:T(8,128)(2,1)} %get-tuple-element.102.refs_5_), channel_id=1, source_target_pairs={{0,1},{1,0},{2,3},{3,2},{4,5},{5,4},{6,7},{7,6},{8,9},{9,8},{10,11... | collective-permute-start | bytes 10616840 | tf_op jit(solution)/shard_map/ppermute | solution.py:987
  305.4 21.9 %collective-permute-start.23 = (bf16[128,3456]{1,0:T(8,128)(2,1)S(1)}, bf16[128,3456]{1,0:T(8,128)(2,1)}, u32[]{:S(2)}, u32[]{:S(2)}) collective-permute-start(bf16[128,3456]{1,0:T(8,128)(2,1)S(1)} %slice.117), channel_id=1, source_target_pairs={{0,8},{1,17},{8,0},{9,25},{16,24},{17,1},{24,16},{25,9},{2,10},{3,... | collective-permute-start | bytes 2654216 | tf_op jit(solution)/shard_map/ppermute | solution.py:991
  306.9 30.1 %collective-permute-start.24 = (bf16[256,3456]{1,0:T(8,128)(2,1)}, bf16[256,3456]{1,0:T(8,128)(2,1)}, u32[]{:S(2)}, u32[]{:S(2)}) collective-permute-start(bf16[256,3456]{1,0:T(8,128)(2,1)} %get-tuple-element.107), channel_id=1, source_target_pairs={{0,16},{1,9},{8,24},{9,1},{16,0},{17,25},{24,8},{25,17},{2,18},{3,... | collective-permute-start | bytes 5308424 | tf_op jit(solution)/shard_map/ppermute | solution.py:997
  329.8 58.5 %collective-permute-start.25 = (bf16[128,3456]{1,0:T(8,128)(2,1)}, bf16[128,3456]{1,0:T(8,128)(2,1)S(1)}, u32[]{:S(2)}, u32[]{:S(2)}) collective-permute-start(bf16[128,3456]{1,0:T(8,128)(2,1)} %add_convert_fusion.9.refs_7_), channel_id=1, source_target_pairs={{0,6},{2,0},{4,2},{6,4},{1,7},{3,1},{5,3},{7,5},{8,14},{10,8},{12,... | collective-permute-start | bytes 2654216 | tf_op jit(solution)/shard_map/ppermute | solution.py:1003
  352.4 30.2 %collective-permute-start.26 = (bf16[128,3456]{1,0:T(8,128)(2,1)}, bf16[128,3456]{1,0:T(8,128)(2,1)}, u32[]{:S(2)}, u32[]{:S(2)}) collective-permute-start(bf16[128,3456]{1,0:T(8,128)(2,1)} %slice.119), channel_id=1, source_target_pairs={{0,8},{1,17},{8,0},{9,25},{16,24},{17,1},{24,16},{25,9},{2,10},{3,... | collective-permute-start | bytes 2654216 | tf_op jit(solution)/shard_map/ppermute | solution.py:991
  353.9 31.3 %collective-permute-start.27 = (bf16[256,3456]{1,0:T(8,128)(2,1)}, bf16[256,3456]{1,0:T(8,128)(2,1)}, u32[]{:S(2)}, u32[]{:S(2)}) collective-permute-start(bf16[256,3456]{1,0:T(8,128)(2,1)} %get-tuple-element.112), channel_id=1, source_target_pairs={{0,16},{1,9},{8,24},{9,1},{16,0},{17,25},{24,8},{25,17},{2,18},{3,... | collective-permute-start | bytes 5308424 | tf_op jit(solution)/shard_map/ppermute | solution.py:997
  398.9 27.1 %collective-permute-start.28 = (bf16[512,4096]{1,0:T(8,128)(2,1)}, bf16[512,4096]{1,0:T(8,128)(2,1)}, u32[]{:S(2)}, u32[]{:S(2)}) collective-permute-start(bf16[512,4096]{1,0:T(8,128)(2,1)} %mix_weights.2), channel_id=1, source_target_pairs={{0,1},{1,0},{2,3},{3,2},{4,5},{5,4},{6,7},{7,6},{8,9},{9,8},{10,11... | collective-permute-start | bytes 12582920 | tf_op jit(solution)/shard_map/ppermute | solution.py:987
  401.9 24.1 %collective-permute-start.31 = (bf16[128,3456]{1,0:T(8,128)(2,1)}, bf16[128,3456]{1,0:T(8,128)(2,1)}, u32[]{:S(2)}, u32[]{:S(2)}) collective-permute-start(bf16[128,3456]{1,0:T(8,128)(2,1)} %add_convert_fusion.8.refs_6_), channel_id=1, source_target_pairs={{0,2},{2,4},{4,6},{6,0},{1,3},{3,5},{5,7},{7,1},{8,10},{10,12},{12... | collective-permute-start | bytes 2654216 | tf_op jit(solution)/shard_map/ppermute | solution.py:1003
  437.0 46.0 %collective-permute-start.34 = (bf16[256,4096]{1,0:T(8,128)(2,1)}, bf16[256,4096]{1,0:T(8,128)(2,1)}, u32[]{:S(2)}, u32[]{:S(2)}) collective-permute-start(bf16[256,4096]{1,0:T(8,128)(2,1)} %get-tuple-element.119), channel_id=1, source_target_pairs={{0,16},{1,9},{8,24},{9,1},{16,0},{17,25},{24,8},{25,17},{2,18},{3,... | collective-permute-start | bytes 6291464 | tf_op jit(solution)/shard_map/ppermute | solution.py:997
  440.2 45.2 %collective-permute-start.42 = (bf16[128,3456]{1,0:T(8,128)(2,1)}, bf16[128,3456]{1,0:T(8,128)(2,1)}, u32[]{:S(2)}, u32[]{:S(2)}) collective-permute-start(bf16[128,3456]{1,0:T(8,128)(2,1)} %add_convert_fusion.6), channel_id=1, source_target_pairs={{0,8},{1,17},{8,0},{9,25},{16,24},{17,1},{24,16},{25,9},{2,10},{3,... | collective-permute-start | bytes 2654216 | tf_op jit(solution)/shard_map/ppermute | solution.py:991
  441.7 41.3 %collective-permute-start.33 = (bf16[128,3456]{1,0:T(8,128)(2,1)S(1)}, bf16[128,3456]{1,0:T(8,128)(2,1)}, u32[]{:S(2)}, u32[]{:S(2)}) collective-permute-start(bf16[128,3456]{1,0:T(8,128)(2,1)S(1)} %copy-done.10), channel_id=1, source_target_pairs={{0,4},{2,6},{4,0},{6,2},{1,5},{3,7},{5,1},{7,3},{8,12},{10,14},{12... | collective-permute-start | bytes 2654216 | tf_op jit(solution)/shard_map/ppermute | solution.py:1003
  489.1 23.8 %collective-permute-start.43 = (bf16[128,3456]{1,0:T(8,128)(2,1)}, bf16[128,3456]{1,0:T(8,128)(2,1)}, u32[]{:S(2)}, u32[]{:S(2)}) collective-permute-start(bf16[128,3456]{1,0:T(8,128)(2,1)} %add_convert_fusion.5.refs_0_), channel_id=1, source_target_pairs={{0,8},{1,17},{8,0},{9,25},{16,24},{17,1},{24,16},{25,9},{2,10},{3,... | collective-permute-start | bytes 2654216 | tf_op jit(solution)/shard_map/ppermute | solution.py:991
  508.0 29.6 %collective-permute-start.32 = (bf16[1024,512]{1,0:T(8,128)(2,1)}, bf16[1024,512]{1,0:T(8,128)(2,1)}, u32[]{:S(2)}, u32[]{:S(2)}) collective-permute-start(bf16[1024,512]{1,0:T(8,128)(2,1)} %get-tuple-element.117), channel_id=1, source_target_pairs={{0,1},{1,0},{2,3},{3,2},{4,5},{5,4},{6,7},{7,6},{8,9},{9,8},{10,11... | collective-permute-start | bytes 3145736 | tf_op jit(solution)/shard_map/ppermute | solution.py:987
  512.9 28.4 %collective-permute-start.44 = (bf16[128,3456]{1,0:T(8,128)(2,1)}, bf16[128,3456]{1,0:T(8,128)(2,1)}, u32[]{:S(2)}, u32[]{:S(2)}) collective-permute-start(bf16[128,3456]{1,0:T(8,128)(2,1)} %add_convert_fusion.5.refs_0_), channel_id=1, source_target_pairs={{0,16},{1,9},{8,24},{9,1},{16,0},{17,25},{24,8},{25,17},{2,18},{3,... | collective-permute-start | bytes 2654216 | tf_op jit(solution)/shard_map/ppermute | solution.py:997
  527.0 20.5 %collective-permute-start.40 = (bf16[128,1024]{1,0:T(8,128)(2,1)S(1)}, bf16[128,1024]{1,0:T(8,128)(2,1)S(1)}, u32[]{:S(2)}, u32[]{:S(2)}) collective-permute-start(bf16[128,1024]{1,0:T(8,128)(2,1)S(1)} %add_convert_fusion.10.refs_0_), channel_id=1, source_target_pairs={{0,16},{1,9},{8,24},{9,1},{16,0},{17,25},{24,8},{25,17},{2,18},{3,... | collective-permute-start | bytes 786440 | tf_op jit(solution)/shard_map/ppermute | solution.py:997
  (44 other events, 441.4 us)
Sparse Core Ops, SparseCore 0:
  99.2 46.0 all-gather.5
  158.9 44.8 all-gather.7
  206.2 52.0 all-gather.9
  440.3 66.9 all-gather.11

commit v3 on v2

--- a/solution.py
+++ b/solution.py
@@ -105,7 +105,7 @@
     )(place, mine, theirs)
 
 
-def outgoing(place, tokens, cotangent, before, gains):
+def outgoing(place, tokens, cotangent, before, gains, tie):
     count, half = tokens.shape[0] // 2, tokens.shape[1]
     rows = 2 * count + 2 * HALO
 
@@ -129,12 +129,14 @@
         body,
         "outgoing",
         shape_of(rows, half),
+        tie=tie,
+        n_in=6,
         grid_spec=scalar_grid(
             (1,),
             [theirs, theirs, pl.BlockSpec((HALO, half), lambda i, place: (count // HALO - 1, 0)), few, few],
             pl.BlockSpec((rows, half), lambda i, place: (0, 0)),
         ),
-    )(place, tokens, cotangent, tokens, before, gains)
+    )(place, tokens, cotangent, tokens, before, gains, *tie)
 
 
 def pack(stack, turned, place, quarters, rows=None, tie=()):
@@ -1059,17 +1061,14 @@
 
     mix_first = pack(in_weight, out_weight, place, 1, conv_weight)
     mix_quarters = [along_row(mix_first, -offset) for offset in OFFSETS[1:]]
-    before = lax.ppermute(
-        after(tokens[2 * count - HALO :], mix_first),
-        "row",
-        [(i, i + 1) for i in range(BLOCKS - 1)],
-    )
     own_gains = jnp.pad(jnp.stack([norm1_gain, norm2_gain]), ((0, HALO - 2), (0, 0)))
     mix_own = pack(in_weight, out_weight, place, 4, tie=[mix_first])
     feed_own = pack(gate_up_weight, down_weight, place, 4, tie=[mix_own])
-    sent = outgoing(place, tokens, cotangent, before, own_gains)
-    theirs = swap_cores(sent)
-    joined = join_rows(mix_quarters, [mix_own, feed_own, sent])
+    before = lax.ppermute(
+        after(tokens[2 * count - HALO :], mix_own), "row", [(i, i + 1) for i in range(BLOCKS - 1)]
+    )
+    joined = join_rows(mix_quarters, [mix_own, feed_own])
+    theirs = swap_cores(outgoing(place, tokens, cotangent, before, own_gains, [joined]))
     feed_first = pack(gate_up_weight, down_weight, place, 1, tie=[joined])
     gains = jnp.concatenate([own_gains[:2], theirs[2 * count + HALO :][:2]], axis=1).astype(f32)
     gain_one, gain_two = gains[:1], gains[1:]
@@ -1114,27 +1113,28 @@
         return keep, across_second(send)
 
     grad_normed_two, done = activate(None, [])
-    half_two = gathered(2, hidden, done)
+    half_two = gathered(2, mix_half, done)
     have(after(half_one, done))
-    last = done
-    grad_normed_two, done = activate(grad_normed_two, [])
-    half_three = gathered(3, last, done)
+    grad_normed_two, last = activate(grad_normed_two, [])
+    half_three = gathered(3, done, last)
+    done = last
     keep, send = weights_of(0, [done])
     have(after(half_two, keep))
     grad_normed_two, done = activate(grad_normed_two, [keep])
     zero = (keep, send)
     keep, send = weights_of(1, [done, send])
-    have(after(half_three, keep))
+    one = (keep, send)
+    keep, send = weights_of(2, [keep])
+    two = (keep, send)
+    have(after(half_three, one[0]))
     grad_normed_two, done = activate(grad_normed_two, [keep])
-    one = add(keep, send)
-    keep, send = weights_of(2, [done, send])
-    one_across = across_first(lower(after(one, keep)))
+    one_low, two_low = add(*map(lower, one)), add(*map(lower, two))
+    one_across, two_across = across_first(one_low), across_first(two_low)
     first = first_rows(hidden, grad_normed_two, low, saved[1], gain_two, mix_halves)
     later = later_rows(first)
-    one = add(upper(one), one_across)
-    two = add(keep, send)
-    keep, send = weights_of(3, [keep, first, one])
-    one = along_row(one, OFFSETS[1])
+    keep, send = weights_of(3, [first, one_low, two_low])
+    one = add(*map(upper, one), one_across)
+    two = add(*map(upper, two), two_across)
     zero_across = across_first(after(add(*map(lower, zero)), keep))
 
     grad_own, grad_other, grads, grad_t, sums = mix_backward(
@@ -1150,44 +1150,46 @@
         gain_one,
         gain_two,
         mix_halves,
-        [keep, two],
-    )
-    two = add(upper(two), across_first(lower(after(two, keep))))
-    three = add(keep, send)
+        [keep, one, two],
+    )
+    three = (keep, send)
+    three_low = add(*map(lower, three))
+    one, two = along_row(one, OFFSETS[1]), along_row(two, OFFSETS[2])
     where = jnp.array([OFFSETS.index(offset) for offset in (0, 1, 2, -1)], jnp.int32)
     own_taps = jnp.concatenate(
         [block_of(sums[2:], where[(b - row) % BLOCKS], 1) for b in range(BLOCKS)], axis=1
     )
     packed_sums = jnp.concatenate([sums[:2], own_taps], axis=0)
     every = lax.all_gather(packed_sums, ("dp", "row", "col"), axis=0)
+
+    for_them = mix_weights(place, normed_t, grad_t, grads, carried, None, [one, three_low, packed_sums])
+    received = swap_cores(for_them)
+    three = add(*map(upper, three), across_first(three_low))
+    grad_theirs = swap_cores(grad_other)
+    input_back = join_tokens(grad_own, after(grad_theirs, for_them), place)
+    keep, send = mix_weights(
+        place, normed_t, grad_t, grads, carried, received, [three, two, input_back]
+    )
+    send = across_second(send)
+    three = along_row(three, OFFSETS[3])
+    own_out, other_out = feed_output(hidden, activations, feed_halves, others, [keep])
+    send = after(send, own_out)
+    other_out = swap_cores(other_out)
+    mix_low = add(lower(keep), lower(send))
+    mix_across = across_first(mix_low)
+    three = after(three, mix_low)
+    feed_sum = quarters(add(*map(upper, zero), zero_across, one, two, three))
+    mix_quarters = jnp.split(add(upper(keep), upper(send), mix_across), BLOCKS, axis=1)
+    mix_quarters = [along_row(part, OFFSETS[k]) if k else part for k, part in enumerate(mix_quarters)]
+    mix_sum = quarters(add(*mix_quarters))
+    output_back = join_tokens(own_out, other_out, place)
+    gate_up_grad, down_grad = unpack(feed_sum, 2, place)
+    in_grad, out_grad = unpack(mix_sum, 3, place)
+    every = after(every, gate_up_grad)
     sums = jnp.sum(every.reshape(16, 2, *packed_sums.shape), axis=0)
     mine, other = sums[core], sums[1 - core]
     gain_grads = mine[:2, :half] + other[:2, half:]
     taps_grad = block_of(mine[2 : 2 + KCONV] + other[2 : 2 + KCONV], row, 1)
-
-    for_them = mix_weights(place, normed_t, grad_t, grads, carried, None, [one, two, three, packed_sums])
-    received = swap_cores(for_them)
-    three = add(upper(three), across_first(lower(three)))
-    two = along_row(two, OFFSETS[2])
-    grad_theirs = swap_cores(grad_other)
-    keep, send = mix_weights(
-        place, normed_t, grad_t, grads, carried, received, [three, grad_theirs, two]
-    )
-    send = across_second(send)
-    three = along_row(three, OFFSETS[3])
-    own_out, other_out = feed_output(hidden, activations, feed_halves, others, [keep])
-    three, send = lax.optimization_barrier((three, send, own_out))[:2]
-    other_out = swap_cores(other_out)
-    feed_sum = add(*map(upper, zero), zero_across, one, two, three)
-    feed_sum = quarters(feed_sum)
-    go = across_first(add(lower(keep), lower(send)))
-    mix_quarters = jnp.split(add(upper(keep), upper(send), go), BLOCKS, axis=1)
-    mix_quarters = [along_row(part, OFFSETS[k]) if k else part for k, part in enumerate(mix_quarters)]
-    mix_sum = quarters(add(*mix_quarters))
-    output_back = join_tokens(own_out, other_out, place)
-    input_back = join_tokens(grad_own, grad_theirs, place)
-    gate_up_grad, down_grad = unpack(feed_sum, 2, place)
-    in_grad, out_grad = unpack(mix_sum, 3, place)
     return (
         output_back,
         input_back,

time: 571 us -> 521 us (0.912); the launches traced: 560 us -> 516 us
  waiting for transfers between devices: 159 us -> 128 us
  local copies, waits for them, and re-layouts: 22.3 us -> 12.6 us
    ppermute x12, waiting for transfers between devices: 61.9 us -> 34.8 us  [along_row(): lax.ppermute(value, 'row', [(i, (i + steps) % BLOCKS) for i in range(BLOC...]
    ppermute x8, waiting for transfers between devices: 57 us -> 40.6 us  [across_first(): lax.ppermute(value, ('dp', 'col'), [(2 * p + c, 2 * (p ^ 1 << c) + c) for...]
    ppermute x11, waiting for transfers between devices: 8.89 us -> 16.8 us  [across_second(): lax.ppermute(value, ('dp', 'col'), [(2 * p + c, 2 * (p ^ 2 >> c) + c) for...]
    ppermute x11, starting transfers between devices: 9.95 us -> 16.1 us  [across_second(): lax.ppermute(value, ('dp', 'col'), [(2 * p + c, 2 * (p ^ 2 >> c) + c) for...]
  transfers between devices with their start and end apart: 50 -> 50, of which waited for: 20 -> 20; matrix products, arithmetic and copies ran while one was open for 8% -> 7% of each run, Pallas kernels for 44% -> 48%
where the time goes in v3:
time: 521 us; the launch traced here: 516 us
  Pallas kernels  285 us (55%)
  waiting for transfers between devices  128 us (25%)
  starting transfers between devices  44.8 us (9%)
  other arithmetic  28 us (5%)
  between operations  18.3 us (4%)
  local copies, waits for them, and re-layouts  12.6 us (2%)
    pallas_call x4, Pallas kernels, feed(): call(body, 'feed', (shape_of(count, width, dtype=f32), shape_of(count, la...  104 us
    ppermute x8, waiting for transfers between devices, across_first(): lax.ppermute(value, ('dp', 'col'), [(2 * p + c, 2 * (p ^ 1 << c) + c) for...  40.6 us
    pallas_call x4, Pallas kernels, feed_weights(): call(body, 'feed_weights', (shape_of(half // 2, lanes),) * 2, flops=6 * c...  40.3 us
    ppermute x12, waiting for transfers between devices, along_row(): lax.ppermute(value, 'row', [(i, (i + steps) % BLOCKS) for i in range(BLOC...  34.8 us
    pallas_call x1, Pallas kernels, mix_backward(): call(body, 'mix_backward', (shape_of(count, half), shape_of(count, half),...  25.9 us
    pallas_call x1, Pallas kernels, mix_forward(): call(body, 'mix_forward', (flat, flat, flat, flat, wide, flat, flat, shap...  23.7 us
    convert_element_type x11, other arithmetic, add(): return sum((part.astype(f32) for part in parts)).astype(bf16)  23.6 us
    pallas_call x2, Pallas kernels, mix_weights(): call(body, 'mix_weights', (shape_of(half // 2, 4 * width),) * 2 if more e...  20.7 us
  transfers between devices with their start and end apart: 50, of which 20 were waited for; matrix products, arithmetic and copies ran while one was open for 7% of the time, Pallas kernels for 48%

profile of v3, /device:TPU:0, one launch (start us, length us, event | category | flops | bytes accessed | tf_op | source)
XLA Modules:
  0.0 516.3 jit_solution(18419593504040157172)
XLA Ops:
  19.7 4.2 pack.5.refs_3_.refs_1_
  28.8 5.2 %pack.6.refs_4_.refs_5_ = bf16[512,3456]{1,0:T(8,128)(2,1)} custom-call(s32[5]{0:T(128)} %stack.29.place.refs_0_, bf16[2,512,1152]{2,1,0:T(8,128)(2,1)} %refs_1_.9, bf16[1152,512]{1,0:T(8,128)(2,1)} %refs_2_.7, bf16[512,1024]{1,0:T(8,128)(2,1)} %pack.5.refs_3_.refs_1_), custom_call_target="tpu_custom_call" | custom-call | tf_op jit(solution)/shard_map/pack/pallas_call | solution.py:160
  34.0 10.9 %collective-permute-done.3.refs_2_ = bf16[144,1024]{1,0:T(8,128)(2,1)S(1)} collective-permute-done((bf16[144,1024]{1,0:T(8,128)(2,1)}, bf16[144,1024]{1,0:T(8,128)(2,1)S(1)}, u32[]{:S(2)}, u32[]{:S(2)}) %collective-permute-start.3) | collective-permute-done | bytes 294944 | tf_op jit(solution)/shard_map/ppermute | solution.py:1005
  57.9 13.2 %collective-permute-done.5.refs_3_ = bf16[432,1024]{1,0:T(8,128)(2,1)} collective-permute-done((bf16[432,1024]{1,0:T(8,128)(2,1)}, bf16[432,1024]{1,0:T(8,128)(2,1)}, u32[]{:S(2)}, u32[]{:S(2)}) %collective-permute-start.5) | collective-permute-done | bytes 884768 | tf_op jit(solution)/shard_map/ppermute | solution.py:993
  75.0 7.5 %prepare.1 = (bf16[1040,1024]{1,0:T(8,128)(2,1)}, bf16[1024,1024]{1,0:T(8,128)(2,1)}, bf16[1024,1024]{1,0:T(8,128)(2,1)}, bf16[1024,1024]{1,0:T(8,128)(2,1)}) custom-call(s32[5]{0:T(128)} %stack.29.place.refs_0_, bf16[2048,512]{1,0:T(8,128)(2,1)} %refs_4_.3, bf16[2080,512]{1,0:T(8,128)(2,1)} %collective-permute-done.4.refs_2_.refs_5_.refs_7_.refs_4_, ...), custom_call_target="tpu_custom_call" | custom-call | bytes 16777216 | tf_op jit(solution)/shard_map/prepare/pallas_call | solution.py:314
  85.0 4.6 mix_assemble.1.refs_1_.refs_0_.refs_14_
  97.1 23.7 %mix_forward.1 = (bf16[1024,1024]{1,0:T(8,128)(2,1)}, bf16[1024,1024]{1,0:T(8,128)(2,1)}, bf16[1024,1024]{1,0:T(8,128)(2,1)}, bf16[1024,1024]{1,0:T(8,128)(2,1)}...) custom-call(s32[5]{0:T(128)} %stack.29.place.refs_0_, ...), custom_call_target="tpu_custom_call" | custom-call | flops 8589934592 | bytes 39845888 | tf_op jit(solution)/shard_map/mix_forward/pallas_call | solution.py:488
  120.8 25.5 %feed.4 = (f32[1024,1024]{1,0:T(8,128)}, bf16[1024,3456]{1,0:T(8,128)(2,1)}, bf16[512,3456]{1,0:T(8,128)(2,1)}) custom-call(bf16[1024,1024]{1,0:T(8,128)(2,1)} %get-tuple-element.71.refs_0_.normed_hbm, bf16[1024,1024]{1,0:T(8,128)(2,1)} %get-tuple-element.72.refs_1_.low_hbm.low.refs_3_, bf16[1024,1024]{1,0:T(8,128)(2,1)} %get-tuple-element.73.refs_2_.normed_t_hbm.refs_1_, ...), custom_call_target="tpu_custom_call" | custom-call | flops 15703474176 | bytes 34471936 | tf_op jit(solution)/shard_map/feed/pallas_call | solution.py:648
  148.0 5.0 collective-permute-done.11.other_hbm.refs_10_
  152.9 26.3 %feed.5 = (f32[1024,1024]{1,0:T(8,128)}, bf16[1024,3456]{1,0:T(8,128)(2,1)}, bf16[512,3456]{1,0:T(8,128)(2,1)}) custom-call(bf16[1024,1024]{1,0:T(8,128)(2,1)} %get-tuple-element.71.refs_0_.normed_hbm, bf16[1024,1024]{1,0:T(8,128)(2,1)} %get-tuple-element.72.refs_1_.low_hbm.low.refs_3_, bf16[1024,1024]{1,0:T(8,128)(2,1)} %get-tuple-element.73.refs_2_.normed_t_hbm.refs_1_, ...), custom_call_target="tpu_custom_call" | custom-call | flops 15703474176 | bytes 34471936 | tf_op jit(solution)/shard_map/feed/pallas_call | solution.py:648
  179.2 10.0 %feed_weights.4 = (bf16[256,3456]{1,0:T(8,128)(2,1)}, bf16[256,3456]{1,0:T(8,128)(2,1)}) custom-call(s32[5]{0:T(128)} %stack.29.place.refs_0_, bf16[1024,1024]{1,0:T(8,128)(2,1)} %get-tuple-element.73.refs_2_.normed_t_hbm.refs_1_, bf16[1024,1024]{1,0:T(8,128)(2,1)} %get-tuple-element.74.refs_3_.low_t_hbm.refs_2_, ...), custom_call_target="tpu_custom_call" | custom-call | flops 3623878656 | bytes 16252928 | tf_op jit(solution)/shard_map/feed_weights/pallas_call | solution.py:737
  189.2 5.9 %all-gather.8.cloned.1.call-done.refs_4_.refs_7_ = bf16[512,3456]{1,0:T(8,128)(2,1)} async-done(((bf16[128,3456]{1,0:T(8,128)(2,1)}), bf16[512,3456]{1,0:T(8,128)(2,1)}) %all-gather.8.cloned.1.call-update) | async-done | bytes 3538960 | tf_op jit(solution)/shard_map/all_gather | solution.py:1096
  201.7 26.4 %feed.6 = (f32[1024,1024]{1,0:T(8,128)}, bf16[1024,3456]{1,0:T(8,128)(2,1)}, bf16[512,3456]{1,0:T(8,128)(2,1)}) custom-call(bf16[1024,1024]{1,0:T(8,128)(2,1)} %get-tuple-element.71.refs_0_.normed_hbm, bf16[1024,1024]{1,0:T(8,128)(2,1)} %get-tuple-element.72.refs_1_.low_hbm.low.refs_3_, bf16[1024,1024]{1,0:T(8,128)(2,1)} %get-tuple-element.73.refs_2_.normed_t_hbm.refs_1_, ...), custom_call_target="tpu_custom_call" | custom-call | flops 15703474176 | bytes 34471936 | tf_op jit(solution)/shard_map/feed/pallas_call | solution.py:648
  229.1 10.1 %feed_weights.5 = (bf16[256,3456]{1,0:T(8,128)(2,1)}, bf16[256,3456]{1,0:T(8,128)(2,1)}) custom-call(s32[5]{0:T(128)} %stack.29.place.refs_0_, bf16[1024,1024]{1,0:T(8,128)(2,1)} %get-tuple-element.73.refs_2_.normed_t_hbm.refs_1_, bf16[1024,1024]{1,0:T(8,128)(2,1)} %get-tuple-element.74.refs_3_.low_t_hbm.refs_2_, ...), custom_call_target="tpu_custom_call" | custom-call | flops 3623878656 | bytes 16252928 | tf_op jit(solution)/shard_map/feed_weights/pallas_call | solution.py:737
  239.1 10.6 %all-gather.10.cloned.1.call-done.refs_4_.refs_8_ = bf16[512,3456]{1,0:T(8,128)(2,1)} async-done(((bf16[128,3456]{1,0:T(8,128)(2,1)}), bf16[512,3456]{1,0:T(8,128)(2,1)}) %all-gather.10.cloned.1.call-update) | async-done | bytes 3538960 | tf_op jit(solution)/shard_map/all_gather | solution.py:1096
  251.2 10.1 %feed_weights.6 = (bf16[256,3456]{1,0:T(8,128)(2,1)}, bf16[256,3456]{1,0:T(8,128)(2,1)}) custom-call(s32[5]{0:T(128)} %stack.29.place.refs_0_, bf16[1024,1024]{1,0:T(8,128)(2,1)} %get-tuple-element.73.refs_2_.normed_t_hbm.refs_1_, bf16[1024,1024]{1,0:T(8,128)(2,1)} %get-tuple-element.74.refs_3_.low_t_hbm.refs_2_, ...), custom_call_target="tpu_custom_call" | custom-call | flops 3623878656 | bytes 16252928 | tf_op jit(solution)/shard_map/feed_weights/pallas_call | solution.py:737
  261.8 25.6 %feed.7 = (f32[1024,1024]{1,0:T(8,128)}, bf16[1024,3456]{1,0:T(8,128)(2,1)}, bf16[512,3456]{1,0:T(8,128)(2,1)}) custom-call(bf16[1024,1024]{1,0:T(8,128)(2,1)} %get-tuple-element.71.refs_0_.normed_hbm, bf16[1024,1024]{1,0:T(8,128)(2,1)} %get-tuple-element.72.refs_1_.low_hbm.low.refs_3_, bf16[1024,1024]{1,0:T(8,128)(2,1)} %get-tuple-element.73.refs_2_.normed_t_hbm.refs_1_, ...), custom_call_target="tpu_custom_call" | custom-call | flops 15703474176 | bytes 34471936 | tf_op jit(solution)/shard_map/feed/pallas_call | solution.py:648
  301.2 4.4 collective-permute-done.24
  311.3 10.1 %feed_weights.7 = (bf16[256,3456]{1,0:T(8,128)(2,1)}, bf16[256,3456]{1,0:T(8,128)(2,1)}) custom-call(s32[5]{0:T(128)} %stack.29.place.refs_0_, bf16[1024,1024]{1,0:T(8,128)(2,1)} %get-tuple-element.73.refs_2_.normed_t_hbm.refs_1_, bf16[1024,1024]{1,0:T(8,128)(2,1)} %get-tuple-element.74.refs_3_.low_t_hbm.refs_2_, ...), custom_call_target="tpu_custom_call" | custom-call | flops 3623878656 | bytes 16252928 | tf_op jit(solution)/shard_map/feed_weights/pallas_call | solution.py:737
  325.8 25.9 %mix_backward.1 = (bf16[1024,512]{1,0:T(8,128)(2,1)}, bf16[1024,512]{1,0:T(8,128)(2,1)}, bf16[1024,3072]{1,0:T(8,128)(2,1)}, bf16[1024,1024]{1,0:T(8,128)(2,1)}, f32[8,1024]{1,0:T(8,128)}) custom-call(s32[5]{0:T(128)} %stack.29.place.refs_0_, f32[1024,1024]{1,0:T(8,128)} %get-tuple-element.70.hidden.refs_1_.refs_0_, ...), custom_call_target="tpu_custom_call" | custom-call | flops 8589934592 | bytes 46137344 | tf_op jit(solution)/shard_map/mix_backward/pallas_call | solution.py:873
  356.5 9.8 %mix_weights.2 = bf16[512,4096]{1,0:T(8,128)(2,1)} custom-call(s32[5]{0:T(128)} %stack.29.place.refs_0_, bf16[1024,1024]{1,0:T(8,128)(2,1)} %get-tuple-element.97.refs_1_, bf16[1024,1024]{1,0:T(8,128)(2,1)} %get-tuple-element.107.refs_2_, bf16[1024,3072]{1,0:T(8,128)(2,1)} %get-tuple-element.108.refs_3_, bf16[1024,1024]{1,0:T(8,128)(2,1)} %get-tuple-element.109.refs_4_, ...), custom_call_target="tpu_custom_call" | custom-call | flops 4294967296 | bytes 14680064 | tf_op jit(solution)/shard_map/mix_weights/pallas_call | solution.py:961
  367.4 7.9 %collective-permute-done.31.theirs = bf16[1024,512]{1,0:T(8,128)(2,1)} collective-permute-done((bf16[1024,512]{1,0:T(8,128)(2,1)}, bf16[1024,512]{1,0:T(8,128)(2,1)}, u32[]{:S(2)}, u32[]{:S(2)}) %collective-permute-start.31) | collective-permute-done | bytes 1048608 | tf_op jit(solution)/shard_map/ppermute | solution.py:989
  383.1 7.5 %collective-permute-done.30.refs_7_ = bf16[128,3456]{1,0:T(8,128)(2,1)} collective-permute-done((bf16[128,3456]{1,0:T(8,128)(2,1)S(1)}, bf16[128,3456]{1,0:T(8,128)(2,1)}, u32[]{:S(2)}, u32[]{:S(2)}) %collective-permute-start.30) | collective-permute-done | bytes 884768 | tf_op jit(solution)/shard_map/ppermute | solution.py:1005
  390.6 10.9 %mix_weights.3 = (bf16[256,4096]{1,0:T(8,128)(2,1)}, bf16[256,4096]{1,0:T(8,128)(2,1)}) custom-call(s32[5]{0:T(128)} %stack.29.place.refs_0_, bf16[1024,1024]{1,0:T(8,128)(2,1)} %get-tuple-element.97.refs_1_, bf16[1024,1024]{1,0:T(8,128)(2,1)} %get-tuple-element.107.refs_2_, bf16[1024,3072]{1,0:T(8,128)(2,1)} %get-tuple-element.108.refs_3_, ...), custom_call_target="tpu_custom_call" | custom-call | flops 4294967296 | bytes 14680064 | tf_op jit(solution)/shard_map/mix_weights/pallas_call | solution.py:961
  406.1 17.7 %feed_output.1 = (bf16[1024,512]{1,0:T(8,128)(2,1)}, bf16[1024,512]{1,0:T(8,128)(2,1)}) custom-call(f32[1024,1024]{1,0:T(8,128)} %get-tuple-element.70.hidden.refs_1_.refs_0_, bf16[1024,3456]{1,0:T(8,128)(2,1)} %get-tuple-element.75.refs_3_.refs_1_, bf16[1024,3456]{1,0:T(8,128)(2,1)} %get-tuple-element.80.refs_3_.refs_2_, ...), custom_call_target="tpu_custom_call" | custom-call | flops 9663676416 | bytes 25165824 | tf_op jit(solution)/shard_map/feed_output/pallas_call | solution.py:691
  423.9 13.6 %collective-permute-done.35 = bf16[256,4096]{1,0:T(8,128)(2,1)} collective-permute-done((bf16[256,4096]{1,0:T(8,128)(2,1)}, bf16[256,4096]{1,0:T(8,128)(2,1)}, u32[]{:S(2)}, u32[]{:S(2)}) %collective-permute-start.35) | collective-permute-done | bytes 2097184 | tf_op jit(solution)/shard_map/ppermute | solution.py:999
  440.9 4.7 collective-permute-done.34
  450.1 4.1 collective-permute-done.39
  457.8 15.3 %collective-permute-done.36.refs_1_ = bf16[128,3456]{1,0:T(8,128)(2,1)} collective-permute-done((bf16[128,3456]{1,0:T(8,128)(2,1)S(1)}, bf16[128,3456]{1,0:T(8,128)(2,1)}, u32[]{:S(2)}, u32[]{:S(2)}) %collective-permute-start.36) | collective-permute-done | bytes 884768 | tf_op jit(solution)/shard_map/ppermute | solution.py:993
  476.2 7.2 %collective-permute-done.41 = bf16[128,1024]{1,0:T(8,128)(2,1)S(1)} collective-permute-done((bf16[128,1024]{1,0:T(8,128)(2,1)S(1)}, bf16[128,1024]{1,0:T(8,128)(2,1)S(1)}, u32[]{:S(2)}, u32[]{:S(2)}) %collective-permute-start.41) | collective-permute-done | bytes 262176 | tf_op jit(solution)/shard_map/ppermute | solution.py:1005
  483.3 4.6 collective-permute-done.42
  496.8 6.2 %unpack.2 = (f32[2,512,1152]{2,1,0:T(8,128)}, f32[1152,512]{1,0:T(8,128)}) custom-call(s32[5]{0:T(128)} %stack.29.place.refs_0_, bf16[128,3456]{1,0:T(8,128)(2,1)} %copy-done.7, bf16[128,3456]{1,0:T(8,128)(2,1)} %collective-permute-done.36.refs_1_, bf16[128,3456]{1,0:T(8,128)(2,1)} %collective-permute-done.37.refs_2_, ...), custom_call_target="tpu_custom_call" | custom-call | tf_op jit(solution)/shard_map/unpack/pallas_call | solution.py:237
  (182 shorter events, 123.5 us)
Async XLA Ops:
  7.2 139.1 %all-gather.6.cloned.1.call-start = ((), (), s32[]{:S(2)}) async-start(), calls=%async_computation | async-start | bytes 4423680 | tf_op jit(solution)/shard_map/all_gather | solution.py:1086
  13.6 20.3 %collective-permute-start.1 = (bf16[144,1024]{1,0:T(8,128)(2,1)}, bf16[144,1024]{1,0:T(8,128)(2,1)S(1)}, u32[]{:S(2)}, u32[]{:S(2)}) collective-permute-start(bf16[144,1024]{1,0:T(8,128)(2,1)} %pack.4.refs_3_), channel_id=1, source_target_pairs={{0,2},{2,4},{4,6},{6,0},{1,3},{3,5},{5,7},{7,1},{8,10},{10,12},{12... | collective-permute-start | bytes 884744 | tf_op jit(solution)/shard_map/ppermute | solution.py:1005
  18.7 26.2 %collective-permute-start.3 = (bf16[144,1024]{1,0:T(8,128)(2,1)}, bf16[144,1024]{1,0:T(8,128)(2,1)S(1)}, u32[]{:S(2)}, u32[]{:S(2)}) collective-permute-start(bf16[144,1024]{1,0:T(8,128)(2,1)} %pack.4.refs_3_), channel_id=1, source_target_pairs={{0,4},{2,6},{4,0},{6,2},{1,5},{3,7},{5,1},{7,3},{8,12},{10,14},{12... | collective-permute-start | bytes 884744 | tf_op jit(solution)/shard_map/ppermute | solution.py:1005
  24.6 23.1 %collective-permute-start = (bf16[16,512]{1,0:T(8,128)(2,1)S(1)}, bf16[16,512]{1,0:T(8,128)(2,1)S(1)}, u32[]{:S(2)}, u32[]{:S(2)}) collective-permute-start(bf16[16,512]{1,0:T(8,128)(2,1)S(1)} %slice.127), channel_id=1, source_target_pairs={{0,2},{2,4},{4,6},{1,3},{3,5},{5,7},{8,10},{10,12},{12,14},{9,11},... | collective-permute-start | bytes 49160 | tf_op jit(solution)/shard_map/ppermute | solution.py:1067
  52.0 21.7 %collective-permute-start.4 = (bf16[2080,512]{1,0:T(8,128)(2,1)}, bf16[2080,512]{1,0:T(8,128)(2,1)}, u32[]{:S(2)}, u32[]{:S(2)}) collective-permute-start(bf16[2080,512]{1,0:T(8,128)(2,1)} %outgoing.1), channel_id=1, source_target_pairs={{0,1},{1,0},{2,3},{3,2},{4,5},{5,4},{6,7},{7,6},{8,9},{9,8},{10,11... | collective-permute-start | bytes 6389768 | tf_op jit(solution)/shard_map/ppermute | solution.py:989
  56.4 26.1 %collective-permute-start.6 = (bf16[432,1024]{1,0:T(8,128)(2,1)}, bf16[432,1024]{1,0:T(8,128)(2,1)}, u32[]{:S(2)}, u32[]{:S(2)}) collective-permute-start(bf16[432,1024]{1,0:T(8,128)(2,1)} %join_rows.1.refs_6_.refs_9_.refs_3_.refs_2_), channel_id=1, source_target_pairs={{0,16},{1,9},{8,24},{9,1},{16,0},{17,25},{24,8},{25,17},{2,18},{3,... | collective-permute-start | bytes 2654216 | tf_op jit(solution)/shard_map/ppermute | solution.py:999
  57.9 24.5 %collective-permute-start.8 = (bf16[128,3456]{1,0:T(8,128)(2,1)}, bf16[128,3456]{1,0:T(8,128)(2,1)S(1)}, u32[]{:S(2)}, u32[]{:S(2)}) collective-permute-start(bf16[128,3456]{1,0:T(8,128)(2,1)} %pack.7), channel_id=1, source_target_pairs={{0,2},{2,4},{4,6},{6,0},{1,3},{3,5},{5,7},{7,1},{8,10},{10,12},{12... | collective-permute-start | bytes 2654216 | tf_op jit(solution)/shard_map/ppermute | solution.py:1005
  89.6 105.6 %all-gather.8.cloned.1.call-start = ((), (), s32[]{:S(2)}) async-start(), calls=%async_computation.1 | async-start | bytes 4423680 | tf_op jit(solution)/shard_map/all_gather | solution.py:1096
  89.7 31.1 %collective-permute-start.10 = (bf16[512,3456]{1,0:T(8,128)(2,1)}, bf16[512,3456]{1,0:T(8,128)(2,1)}, u32[]{:S(2)}, u32[]{:S(2)}) collective-permute-start(bf16[512,3456]{1,0:T(8,128)(2,1)} %pack.6.refs_4_.refs_5_), channel_id=1, source_target_pairs={{0,1},{1,0},{2,3},{3,2},{4,5},{5,4},{6,7},{7,6},{8,9},{9,8},{10,11... | collective-permute-start | bytes 10616840 | tf_op jit(solution)/shard_map/ppermute | solution.py:989
  92.9 53.6 %collective-permute-start.12 = (bf16[128,3456]{1,0:T(8,128)(2,1)}, bf16[128,3456]{1,0:T(8,128)(2,1)S(1)}, u32[]{:S(2)}, u32[]{:S(2)}) collective-permute-start(bf16[128,3456]{1,0:T(8,128)(2,1)} %pack.7), channel_id=1, source_target_pairs={{0,6},{2,0},{4,2},{6,4},{1,7},{3,1},{5,3},{7,5},{8,14},{10,8},{12,... | collective-permute-start | bytes 2654216 | tf_op jit(solution)/shard_map/ppermute | solution.py:1005
  147.5 102.2 %all-gather.10.cloned.1.call-start = ((), (), s32[]{:S(2)}) async-start(), calls=%async_computation.2 | async-start | bytes 4423680 | tf_op jit(solution)/shard_map/all_gather | solution.py:1096
  147.5 31.7 %collective-permute-start.13 = (bf16[512,3456]{1,0:T(8,128)(2,1)}, bf16[512,3456]{1,0:T(8,128)(2,1)}, u32[]{:S(2)}, u32[]{:S(2)}) collective-permute-start(bf16[512,3456]{1,0:T(8,128)(2,1)} %get-tuple-element.77), channel_id=1, source_target_pairs={{0,1},{1,0},{2,3},{3,2},{4,5},{5,4},{6,7},{7,6},{8,9},{9,8},{10,11... | collective-permute-start | bytes 10616840 | tf_op jit(solution)/shard_map/ppermute | solution.py:989
  147.9 47.2 %collective-permute-start.15 = (bf16[128,3456]{1,0:T(8,128)(2,1)}, bf16[128,3456]{1,0:T(8,128)(2,1)S(1)}, u32[]{:S(2)}, u32[]{:S(2)}) collective-permute-start(bf16[128,3456]{1,0:T(8,128)(2,1)} %pack.7), channel_id=1, source_target_pairs={{0,4},{2,6},{4,0},{6,2},{1,5},{3,7},{5,1},{7,3},{8,12},{10,14},{12... | collective-permute-start | bytes 2654216 | tf_op jit(solution)/shard_map/ppermute | solution.py:1005
  196.1 306.9 %all-gather.12.cloned.1.call-start = ((), (), s32[]{:S(2)}) async-start(), calls=%async_computation.3 | async-start | bytes 1081344 | tf_op jit(solution)/shard_map/all_gather | solution.py:1163
  196.2 32.9 %collective-permute-start.16 = (bf16[512,3456]{1,0:T(8,128)(2,1)}, bf16[512,3456]{1,0:T(8,128)(2,1)}, u32[]{:S(2)}, u32[]{:S(2)}) collective-permute-start(bf16[512,3456]{1,0:T(8,128)(2,1)} %get-tuple-element.83.refs_5_), channel_id=1, source_target_pairs={{0,1},{1,0},{2,3},{3,2},{4,5},{5,4},{6,7},{7,6},{8,9},{9,8},{10,11... | collective-permute-start | bytes 10616840 | tf_op jit(solution)/shard_map/ppermute | solution.py:989
  196.7 32.3 %collective-permute-start.17 = (bf16[256,3456]{1,0:T(8,128)(2,1)}, bf16[256,3456]{1,0:T(8,128)(2,1)}, u32[]{:S(2)}, u32[]{:S(2)}) collective-permute-start(bf16[256,3456]{1,0:T(8,128)(2,1)} %get-tuple-element.91), channel_id=1, source_target_pairs={{0,16},{1,9},{8,24},{9,1},{16,0},{17,25},{24,8},{25,17},{2,18},{3,... | collective-permute-start | bytes 5308424 | tf_op jit(solution)/shard_map/ppermute | solution.py:999
  228.2 23.0 %collective-permute-start.19 = (bf16[512,3456]{1,0:T(8,128)(2,1)}, bf16[512,3456]{1,0:T(8,128)(2,1)}, u32[]{:S(2)}, u32[]{:S(2)}) collective-permute-start(bf16[512,3456]{1,0:T(8,128)(2,1)} %get-tuple-element.90.refs_5_), channel_id=1, source_target_pairs={{0,1},{1,0},{2,3},{3,2},{4,5},{5,4},{6,7},{7,6},{8,9},{9,8},{10,11... | collective-permute-start | bytes 10616840 | tf_op jit(solution)/shard_map/ppermute | solution.py:989
  249.7 41.0 %collective-permute-start.22 = (bf16[256,3456]{1,0:T(8,128)(2,1)}, bf16[256,3456]{1,0:T(8,128)(2,1)}, u32[]{:S(2)}, u32[]{:S(2)}) collective-permute-start(bf16[256,3456]{1,0:T(8,128)(2,1)} %get-tuple-element.104), channel_id=1, source_target_pairs={{0,16},{1,9},{8,24},{9,1},{16,0},{17,25},{24,8},{25,17},{2,18},{3,... | collective-permute-start | bytes 5308424 | tf_op jit(solution)/shard_map/ppermute | solution.py:999
  261.2 36.8 %collective-permute-start.23 = (bf16[256,3456]{1,0:T(8,128)(2,1)}, bf16[256,3456]{1,0:T(8,128)(2,1)}, u32[]{:S(2)}, u32[]{:S(2)}) collective-permute-start(bf16[256,3456]{1,0:T(8,128)(2,1)} %get-tuple-element.105), channel_id=1, source_target_pairs={{0,16},{1,9},{8,24},{9,1},{16,0},{17,25},{24,8},{25,17},{2,18},{3,... | collective-permute-start | bytes 5308424 | tf_op jit(solution)/shard_map/ppermute | solution.py:999
  287.4 23.9 %collective-permute-start.21 = (bf16[512,3456]{1,0:T(8,128)(2,1)}, bf16[512,3456]{1,0:T(8,128)(2,1)}, u32[]{:S(2)}, u32[]{:S(2)}) collective-permute-start(bf16[512,3456]{1,0:T(8,128)(2,1)} %get-tuple-element.103), channel_id=1, source_target_pairs={{0,1},{1,0},{2,3},{3,2},{4,5},{5,4},{6,7},{7,6},{8,9},{9,8},{10,11... | collective-permute-start | bytes 10616840 | tf_op jit(solution)/shard_map/ppermute | solution.py:989
  300.6 22.3 %collective-permute-start.25 = (bf16[128,3456]{1,0:T(8,128)(2,1)}, bf16[128,3456]{1,0:T(8,128)(2,1)}, u32[]{:S(2)}, u32[]{:S(2)}) collective-permute-start(bf16[128,3456]{1,0:T(8,128)(2,1)} %add_convert_fusion.8.refs_7_), channel_id=1, source_target_pairs={{0,8},{1,17},{8,0},{9,25},{16,24},{17,1},{24,16},{25,9},{2,10},{3,... | collective-permute-start | bytes 2654216 | tf_op jit(solution)/shard_map/ppermute | solution.py:993
  307.3 49.2 %collective-permute-start.26 = (bf16[128,3456]{1,0:T(8,128)(2,1)S(1)}, bf16[128,3456]{1,0:T(8,128)(2,1)}, u32[]{:S(2)}, u32[]{:S(2)}) collective-permute-start(bf16[128,3456]{1,0:T(8,128)(2,1)S(1)} %add_convert_fusion.7.refs_17_), channel_id=1, source_target_pairs={{0,6},{2,0},{4,2},{6,4},{1,7},{3,1},{5,3},{7,5},{8,14},{10,8},{12,... | collective-permute-start | bytes 2654216 | tf_op jit(solution)/shard_map/ppermute | solution.py:1005
  321.4 32.5 %collective-permute-start.27 = (bf16[256,3456]{1,0:T(8,128)(2,1)}, bf16[256,3456]{1,0:T(8,128)(2,1)}, u32[]{:S(2)}, u32[]{:S(2)}) collective-permute-start(bf16[256,3456]{1,0:T(8,128)(2,1)} %get-tuple-element.110), channel_id=1, source_target_pairs={{0,16},{1,9},{8,24},{9,1},{16,0},{17,25},{24,8},{25,17},{2,18},{3,... | collective-permute-start | bytes 5308424 | tf_op jit(solution)/shard_map/ppermute | solution.py:999
  366.3 24.3 %collective-permute-start.28 = (bf16[512,4096]{1,0:T(8,128)(2,1)}, bf16[512,4096]{1,0:T(8,128)(2,1)}, u32[]{:S(2)}, u32[]{:S(2)}) collective-permute-start(bf16[512,4096]{1,0:T(8,128)(2,1)} %mix_weights.2), channel_id=1, source_target_pairs={{0,1},{1,0},{2,3},{3,2},{4,5},{5,4},{6,7},{7,6},{8,9},{9,8},{10,11... | collective-permute-start | bytes 12582920 | tf_op jit(solution)/shard_map/ppermute | solution.py:989
  367.4 23.2 %collective-permute-start.30 = (bf16[128,3456]{1,0:T(8,128)(2,1)S(1)}, bf16[128,3456]{1,0:T(8,128)(2,1)}, u32[]{:S(2)}, u32[]{:S(2)}) collective-permute-start(bf16[128,3456]{1,0:T(8,128)(2,1)S(1)} %copy-done.5), channel_id=1, source_target_pairs={{0,2},{2,4},{4,6},{6,0},{1,3},{3,5},{5,7},{7,1},{8,10},{10,12},{12... | collective-permute-start | bytes 2654216 | tf_op jit(solution)/shard_map/ppermute | solution.py:1005
  401.5 36.1 %collective-permute-start.35 = (bf16[256,4096]{1,0:T(8,128)(2,1)}, bf16[256,4096]{1,0:T(8,128)(2,1)}, u32[]{:S(2)}, u32[]{:S(2)}) collective-permute-start(bf16[256,4096]{1,0:T(8,128)(2,1)} %get-tuple-element.119), channel_id=1, source_target_pairs={{0,16},{1,9},{8,24},{9,1},{16,0},{17,25},{24,8},{25,17},{2,18},{3,... | collective-permute-start | bytes 6291464 | tf_op jit(solution)/shard_map/ppermute | solution.py:999
  405.5 40.1 %collective-permute-start.33 = (bf16[128,3456]{1,0:T(8,128)(2,1)}, bf16[128,3456]{1,0:T(8,128)(2,1)}, u32[]{:S(2)}, u32[]{:S(2)}) collective-permute-start(bf16[128,3456]{1,0:T(8,128)(2,1)} %add_convert_fusion.3), channel_id=1, source_target_pairs={{0,8},{1,17},{8,0},{9,25},{16,24},{17,1},{24,16},{25,9},{2,10},{3,... | collective-permute-start | bytes 2654216 | tf_op jit(solution)/shard_map/ppermute | solution.py:993
  406.1 39.5 %collective-permute-start.34 = (bf16[128,3456]{1,0:T(8,128)(2,1)S(1)}, bf16[128,3456]{1,0:T(8,128)(2,1)}, u32[]{:S(2)}, u32[]{:S(2)}) collective-permute-start(bf16[128,3456]{1,0:T(8,128)(2,1)S(1)} %copy-done.8), channel_id=1, source_target_pairs={{0,4},{2,6},{4,0},{6,2},{1,5},{3,7},{5,1},{7,3},{8,12},{10,14},{12... | collective-permute-start | bytes 2654216 | tf_op jit(solution)/shard_map/ppermute | solution.py:1005
  423.9 64.6 %collective-permute-start.32 = (bf16[1024,512]{1,0:T(8,128)(2,1)}, bf16[1024,512]{1,0:T(8,128)(2,1)}, u32[]{:S(2)}, u32[]{:S(2)}) collective-permute-start(bf16[1024,512]{1,0:T(8,128)(2,1)} %get-tuple-element.117), channel_id=1, source_target_pairs={{0,1},{1,0},{2,3},{3,2},{4,5},{5,4},{6,7},{7,6},{8,9},{9,8},{10,11... | collective-permute-start | bytes 3145736 | tf_op jit(solution)/shard_map/ppermute | solution.py:989
  448.6 24.5 %collective-permute-start.36 = (bf16[128,3456]{1,0:T(8,128)(2,1)S(1)}, bf16[128,3456]{1,0:T(8,128)(2,1)}, u32[]{:S(2)}, u32[]{:S(2)}) collective-permute-start(bf16[128,3456]{1,0:T(8,128)(2,1)S(1)} %add_convert_fusion.2.refs_0_), channel_id=1, source_target_pairs={{0,8},{1,17},{8,0},{9,25},{16,24},{17,1},{24,16},{25,9},{2,10},{3,... | collective-permute-start | bytes 2654216 | tf_op jit(solution)/shard_map/ppermute | solution.py:993
  456.3 40.5 %collective-permute-start.37 = (bf16[128,3456]{1,0:T(8,128)(2,1)S(1)}, bf16[128,3456]{1,0:T(8,128)(2,1)}, u32[]{:S(2)}, u32[]{:S(2)}) collective-permute-start(bf16[128,3456]{1,0:T(8,128)(2,1)S(1)} %add_convert_fusion.2.refs_0_), channel_id=1, source_target_pairs={{0,16},{1,9},{8,24},{9,1},{16,0},{17,25},{24,8},{25,17},{2,18},{3,... | collective-permute-start | bytes 2654216 | tf_op jit(solution)/shard_map/ppermute | solution.py:999
  473.1 23.7 %collective-permute-start.38 = (bf16[128,3456]{1,0:T(8,128)(2,1)}, bf16[128,3456]{1,0:T(8,128)(2,1)}, u32[]{:S(2)}, u32[]{:S(2)}) collective-permute-start(bf16[128,3456]{1,0:T(8,128)(2,1)} %collective-permute-done.36.refs_1_), channel_id=1, source_target_pairs={{0,16},{1,9},{8,24},{9,1},{16,0},{17,25},{24,8},{25,17},{2,18},{3,... | collective-permute-start | bytes 2654216 | tf_op jit(solution)/shard_map/ppermute | solution.py:999
  (41 other events, 425.1 us)
Sparse Core Ops, SparseCore 0:
  89.7 47.3 all-gather.5
  147.6 47.5 all-gather.7
  197.6 52.0 all-gather.9
  405.6 64.5 all-gather.11

commit v4 on v3

--- a/solution.py
+++ b/solution.py
@@ -13,6 +13,7 @@
 OFFSETS = (0, -1, 1, 2)
 HALO = 16
 STEP = 256
+WIDE = 512
 
 
 eps = 1e-05
@@ -570,11 +571,11 @@
         load.start()
 
     def acts_copy(i):
-        rows = rows_of(i)
+        rows = rows_of(i, WIDE)
         return pltpu.make_async_copy(acts.at[rows], acts_hbm.at[rows], acts_sems.at[i])
 
     def activations(i, carry):
-        rows = rows_of(i)
+        rows = rows_of(i, WIDE)
         for start in range(0, f, 256):
             stop = min(start + 256, f)
             gate_lanes = slice(start, stop)
@@ -593,40 +594,40 @@
         acts_copy(i).start()
         return carry
 
-    lax.fori_loop(0, count // STEP, activations, 0)
+    lax.fori_loop(0, count // WIDE, activations, 0)
     loads[4].wait()
     loads[5].wait()
 
     def their_copy(i):
-        rows = rows_of(i)
+        rows = rows_of(i, WIDE)
         return pltpu.make_async_copy(theirs.at[rows], theirs_hbm.at[rows], their_sems.at[i])
 
     def outer(i, carry):
-        rows = rows_of(i)
+        rows = rows_of(i, WIDE)
         theirs[rows, : 2 * f] = dot(normed_t[rows, :], acts[:, : 2 * f]).astype(bf16)
         theirs[rows, 2 * f :] = dot(low_t[rows, :], acts[:, 2 * f :]).astype(bf16)
         their_copy(i).start()
         return carry
 
-    lax.fori_loop(0, half // STEP, outer, 0)
+    lax.fori_loop(0, half // WIDE, outer, 0)
     if started:
         loads[6].wait()
 
     def grad_copy(i):
-        rows = rows_of(i)
+        rows = rows_of(i, WIDE)
         return pltpu.make_async_copy(grad.at[rows], grad_hbm.at[rows], grad_sems.at[i])
 
     def inner(i, carry):
-        rows = rows_of(i)
+        rows = rows_of(i, WIDE)
         term = dot_nt(acts[rows, : 2 * f], weights[:, : 2 * f])
         grad[rows, :] = grad[rows, :] + term if started else term
         grad_copy(i).start()
         return carry
 
-    lax.fori_loop(0, count // STEP, inner, 0)
-    for i in range(half // STEP):
+    lax.fori_loop(0, count // WIDE, inner, 0)
+    for i in range(half // WIDE):
         their_copy(i).wait()
-    for i in range(count // STEP):
+    for i in range(count // WIDE):
         acts_copy(i).wait()
         grad_copy(i).wait()
 
@@ -636,7 +637,7 @@
     half, lanes = own.shape
     f = lanes // 3
     started = grad is not None
-    tiles = count // STEP
+    tiles = count // WIDE
     before = [grad] if started else []
     body = functools.partial(feed_body, lanes, started)
     if not started:
@@ -667,7 +668,7 @@
             pltpu.SemaphoreType.DMA((7,)),
             pltpu.SemaphoreType.DMA((tiles,)),
             pltpu.SemaphoreType.DMA((tiles,)),
-            pltpu.SemaphoreType.DMA((half // STEP,)),
+            pltpu.SemaphoreType.DMA((half // WIDE,)),
         ],
     )(normed, low, normed_t, low_t, own, other, *before, *tie)
 

time: 521 us -> 525 us (level); the launches traced: 516 us -> 515 us
  no operation moved by 1% of the time
where the time goes in v4:
time: 525 us; the launch traced here: 515 us
  Pallas kernels  281 us (54%)
  waiting for transfers between devices  130 us (25%)
  starting transfers between devices  45.1 us (9%)
  other arithmetic  28 us (5%)
  between operations  18.3 us (3%)
  local copies, waits for them, and re-layouts  12.6 us (2%)
    pallas_call x4, Pallas kernels, feed(): call(body, 'feed', (shape_of(count, width, dtype=f32), shape_of(count, la...  99.3 us
    pallas_call x4, Pallas kernels, feed_weights(): call(body, 'feed_weights', (shape_of(half // 2, lanes),) * 2, flops=6 * c...  40.9 us
    ppermute x8, waiting for transfers between devices, across_first(): lax.ppermute(value, ('dp', 'col'), [(2 * p + c, 2 * (p ^ 1 << c) + c) for...  40.4 us
    ppermute x12, waiting for transfers between devices, along_row(): lax.ppermute(value, 'row', [(i, (i + steps) % BLOCKS) for i in range(BLOC...  34.9 us
    pallas_call x1, Pallas kernels, mix_backward(): call(body, 'mix_backward', (shape_of(count, half), shape_of(count, half),...  25.9 us
    pallas_call x1, Pallas kernels, mix_forward(): call(body, 'mix_forward', (flat, flat, flat, flat, wide, flat, flat, shap...  23.7 us
    convert_element_type x11, other arithmetic, add(): return sum((part.astype(f32) for part in parts)).astype(bf16)  23.6 us
    pallas_call x2, Pallas kernels, mix_weights(): call(body, 'mix_weights', (shape_of(half // 2, 4 * width),) * 2 if more e...  20.7 us
  transfers between devices with their start and end apart: 50, of which 20 were waited for; matrix products, arithmetic and copies ran while one was open for 7% of the time, Pallas kernels for 48%

profile of v4, /device:TPU:0, one launch (start us, length us, event | category | flops | bytes accessed | tf_op | source)
XLA Modules:
  0.0 514.9 jit_solution(6516015804478731394)
XLA Ops:
  19.7 4.2 pack.5.refs_3_.refs_1_
  28.8 5.2 %pack.6.refs_4_.refs_5_ = bf16[512,3456]{1,0:T(8,128)(2,1)} custom-call(s32[5]{0:T(128)} %stack.29.place.refs_0_, bf16[2,512,1152]{2,1,0:T(8,128)(2,1)} %refs_1_.9, bf16[1152,512]{1,0:T(8,128)(2,1)} %refs_2_.7, bf16[512,1024]{1,0:T(8,128)(2,1)} %pack.5.refs_3_.refs_1_), custom_call_target="tpu_custom_call" | custom-call | tf_op jit(solution)/shard_map/pack/pallas_call | solution.py:161
  34.0 10.9 %collective-permute-done.3.refs_2_ = bf16[144,1024]{1,0:T(8,128)(2,1)S(1)} collective-permute-done((bf16[144,1024]{1,0:T(8,128)(2,1)}, bf16[144,1024]{1,0:T(8,128)(2,1)S(1)}, u32[]{:S(2)}, u32[]{:S(2)}) %collective-permute-start.3) | collective-permute-done | bytes 294944 | tf_op jit(solution)/shard_map/ppermute | solution.py:1006
  57.9 13.2 %collective-permute-done.5.refs_3_ = bf16[432,1024]{1,0:T(8,128)(2,1)} collective-permute-done((bf16[432,1024]{1,0:T(8,128)(2,1)}, bf16[432,1024]{1,0:T(8,128)(2,1)}, u32[]{:S(2)}, u32[]{:S(2)}) %collective-permute-start.5) | collective-permute-done | bytes 884768 | tf_op jit(solution)/shard_map/ppermute | solution.py:994
  75.0 7.5 %prepare.1 = (bf16[1040,1024]{1,0:T(8,128)(2,1)}, bf16[1024,1024]{1,0:T(8,128)(2,1)}, bf16[1024,1024]{1,0:T(8,128)(2,1)}, bf16[1024,1024]{1,0:T(8,128)(2,1)}) custom-call(s32[5]{0:T(128)} %stack.29.place.refs_0_, bf16[2048,512]{1,0:T(8,128)(2,1)} %refs_4_.3, bf16[2080,512]{1,0:T(8,128)(2,1)} %collective-permute-done.4.refs_2_.refs_5_.refs_7_.refs_4_, ...), custom_call_target="tpu_custom_call" | custom-call | bytes 16777216 | tf_op jit(solution)/shard_map/prepare/pallas_call | solution.py:315
  85.0 4.6 mix_assemble.1.refs_1_.refs_0_.refs_14_
  97.1 23.7 %mix_forward.1 = (bf16[1024,1024]{1,0:T(8,128)(2,1)}, bf16[1024,1024]{1,0:T(8,128)(2,1)}, bf16[1024,1024]{1,0:T(8,128)(2,1)}, bf16[1024,1024]{1,0:T(8,128)(2,1)}...) custom-call(s32[5]{0:T(128)} %stack.29.place.refs_0_, ...), custom_call_target="tpu_custom_call" | custom-call | flops 8589934592 | bytes 39845888 | tf_op jit(solution)/shard_map/mix_forward/pallas_call | solution.py:489
  120.8 24.7 %feed.4 = (f32[1024,1024]{1,0:T(8,128)}, bf16[1024,3456]{1,0:T(8,128)(2,1)}, bf16[512,3456]{1,0:T(8,128)(2,1)}) custom-call(bf16[1024,1024]{1,0:T(8,128)(2,1)} %get-tuple-element.71.refs_0_.normed_hbm, bf16[1024,1024]{1,0:T(8,128)(2,1)} %get-tuple-element.72.refs_1_.low_hbm.low.refs_3_, bf16[1024,1024]{1,0:T(8,128)(2,1)} %get-tuple-element.73.refs_2_.normed_t_hbm.refs_1_, ...), custom_call_target="tpu_custom_call" | custom-call | flops 15703474176 | bytes 34471936 | tf_op jit(solution)/shard_map/feed/pallas_call | solution.py:649
  147.1 5.0 collective-permute-done.11.other_hbm.refs_10_
  152.1 25.3 %feed.5 = (f32[1024,1024]{1,0:T(8,128)}, bf16[1024,3456]{1,0:T(8,128)(2,1)}, bf16[512,3456]{1,0:T(8,128)(2,1)}) custom-call(bf16[1024,1024]{1,0:T(8,128)(2,1)} %get-tuple-element.71.refs_0_.normed_hbm, bf16[1024,1024]{1,0:T(8,128)(2,1)} %get-tuple-element.72.refs_1_.low_hbm.low.refs_3_, bf16[1024,1024]{1,0:T(8,128)(2,1)} %get-tuple-element.73.refs_2_.normed_t_hbm.refs_1_, ...), custom_call_target="tpu_custom_call" | custom-call | flops 15703474176 | bytes 34471936 | tf_op jit(solution)/shard_map/feed/pallas_call | solution.py:649
  177.4 10.0 %feed_weights.4 = (bf16[256,3456]{1,0:T(8,128)(2,1)}, bf16[256,3456]{1,0:T(8,128)(2,1)}) custom-call(s32[5]{0:T(128)} %stack.29.place.refs_0_, bf16[1024,1024]{1,0:T(8,128)(2,1)} %get-tuple-element.73.refs_2_.normed_t_hbm.refs_1_, bf16[1024,1024]{1,0:T(8,128)(2,1)} %get-tuple-element.74.refs_3_.low_t_hbm.refs_2_, ...), custom_call_target="tpu_custom_call" | custom-call | flops 3623878656 | bytes 16252928 | tf_op jit(solution)/shard_map/feed_weights/pallas_call | solution.py:738
  187.4 6.9 %all-gather.8.cloned.1.call-done.refs_4_.refs_7_ = bf16[512,3456]{1,0:T(8,128)(2,1)} async-done(((bf16[128,3456]{1,0:T(8,128)(2,1)}), bf16[512,3456]{1,0:T(8,128)(2,1)}) %all-gather.8.cloned.1.call-update) | async-done | bytes 3538960 | tf_op jit(solution)/shard_map/all_gather | solution.py:1097
  200.9 25.1 %feed.6 = (f32[1024,1024]{1,0:T(8,128)}, bf16[1024,3456]{1,0:T(8,128)(2,1)}, bf16[512,3456]{1,0:T(8,128)(2,1)}) custom-call(bf16[1024,1024]{1,0:T(8,128)(2,1)} %get-tuple-element.71.refs_0_.normed_hbm, bf16[1024,1024]{1,0:T(8,128)(2,1)} %get-tuple-element.72.refs_1_.low_hbm.low.refs_3_, bf16[1024,1024]{1,0:T(8,128)(2,1)} %get-tuple-element.73.refs_2_.normed_t_hbm.refs_1_, ...), custom_call_target="tpu_custom_call" | custom-call | flops 15703474176 | bytes 34471936 | tf_op jit(solution)/shard_map/feed/pallas_call | solution.py:649
  228.2 10.0 %feed_weights.5 = (bf16[256,3456]{1,0:T(8,128)(2,1)}, bf16[256,3456]{1,0:T(8,128)(2,1)}) custom-call(s32[5]{0:T(128)} %stack.29.place.refs_0_, bf16[1024,1024]{1,0:T(8,128)(2,1)} %get-tuple-element.73.refs_2_.normed_t_hbm.refs_1_, bf16[1024,1024]{1,0:T(8,128)(2,1)} %get-tuple-element.74.refs_3_.low_t_hbm.refs_2_, ...), custom_call_target="tpu_custom_call" | custom-call | flops 3623878656 | bytes 16252928 | tf_op jit(solution)/shard_map/feed_weights/pallas_call | solution.py:738
  238.3 10.6 %all-gather.10.cloned.1.call-done.refs_4_.refs_8_ = bf16[512,3456]{1,0:T(8,128)(2,1)} async-done(((bf16[128,3456]{1,0:T(8,128)(2,1)}), bf16[512,3456]{1,0:T(8,128)(2,1)}) %all-gather.10.cloned.1.call-update) | async-done | bytes 3538960 | tf_op jit(solution)/shard_map/all_gather | solution.py:1097
  250.3 10.3 %feed_weights.6 = (bf16[256,3456]{1,0:T(8,128)(2,1)}, bf16[256,3456]{1,0:T(8,128)(2,1)}) custom-call(s32[5]{0:T(128)} %stack.29.place.refs_0_, bf16[1024,1024]{1,0:T(8,128)(2,1)} %get-tuple-element.73.refs_2_.normed_t_hbm.refs_1_, bf16[1024,1024]{1,0:T(8,128)(2,1)} %get-tuple-element.74.refs_3_.low_t_hbm.refs_2_, ...), custom_call_target="tpu_custom_call" | custom-call | flops 3623878656 | bytes 16252928 | tf_op jit(solution)/shard_map/feed_weights/pallas_call | solution.py:738
  261.2 24.3 %feed.7 = (f32[1024,1024]{1,0:T(8,128)}, bf16[1024,3456]{1,0:T(8,128)(2,1)}, bf16[512,3456]{1,0:T(8,128)(2,1)}) custom-call(bf16[1024,1024]{1,0:T(8,128)(2,1)} %get-tuple-element.71.refs_0_.normed_hbm, bf16[1024,1024]{1,0:T(8,128)(2,1)} %get-tuple-element.72.refs_1_.low_hbm.low.refs_3_, bf16[1024,1024]{1,0:T(8,128)(2,1)} %get-tuple-element.73.refs_2_.normed_t_hbm.refs_1_, ...), custom_call_target="tpu_custom_call" | custom-call | flops 15703474176 | bytes 34471936 | tf_op jit(solution)/shard_map/feed/pallas_call | solution.py:649
  299.3 4.4 collective-permute-done.24
  309.5 10.5 %feed_weights.7 = (bf16[256,3456]{1,0:T(8,128)(2,1)}, bf16[256,3456]{1,0:T(8,128)(2,1)}) custom-call(s32[5]{0:T(128)} %stack.29.place.refs_0_, bf16[1024,1024]{1,0:T(8,128)(2,1)} %get-tuple-element.73.refs_2_.normed_t_hbm.refs_1_, bf16[1024,1024]{1,0:T(8,128)(2,1)} %get-tuple-element.74.refs_3_.low_t_hbm.refs_2_, ...), custom_call_target="tpu_custom_call" | custom-call | flops 3623878656 | bytes 16252928 | tf_op jit(solution)/shard_map/feed_weights/pallas_call | solution.py:738
  324.4 25.9 %mix_backward.1 = (bf16[1024,512]{1,0:T(8,128)(2,1)}, bf16[1024,512]{1,0:T(8,128)(2,1)}, bf16[1024,3072]{1,0:T(8,128)(2,1)}, bf16[1024,1024]{1,0:T(8,128)(2,1)}, f32[8,1024]{1,0:T(8,128)}) custom-call(s32[5]{0:T(128)} %stack.29.place.refs_0_, f32[1024,1024]{1,0:T(8,128)} %get-tuple-element.70.hidden.refs_1_.refs_0_, ...), custom_call_target="tpu_custom_call" | custom-call | flops 8589934592 | bytes 46137344 | tf_op jit(solution)/shard_map/mix_backward/pallas_call | solution.py:874
  355.1 9.8 %mix_weights.2 = bf16[512,4096]{1,0:T(8,128)(2,1)} custom-call(s32[5]{0:T(128)} %stack.29.place.refs_0_, bf16[1024,1024]{1,0:T(8,128)(2,1)} %get-tuple-element.97.refs_1_, bf16[1024,1024]{1,0:T(8,128)(2,1)} %get-tuple-element.107.refs_2_, bf16[1024,3072]{1,0:T(8,128)(2,1)} %get-tuple-element.108.refs_3_, bf16[1024,1024]{1,0:T(8,128)(2,1)} %get-tuple-element.109.refs_4_, ...), custom_call_target="tpu_custom_call" | custom-call | flops 4294967296 | bytes 14680064 | tf_op jit(solution)/shard_map/mix_weights/pallas_call | solution.py:962
  366.0 7.9 %collective-permute-done.31.theirs = bf16[1024,512]{1,0:T(8,128)(2,1)} collective-permute-done((bf16[1024,512]{1,0:T(8,128)(2,1)}, bf16[1024,512]{1,0:T(8,128)(2,1)}, u32[]{:S(2)}, u32[]{:S(2)}) %collective-permute-start.31) | collective-permute-done | bytes 1048608 | tf_op jit(solution)/shard_map/ppermute | solution.py:990
  381.7 7.4 %collective-permute-done.30.refs_7_ = bf16[128,3456]{1,0:T(8,128)(2,1)} collective-permute-done((bf16[128,3456]{1,0:T(8,128)(2,1)S(1)}, bf16[128,3456]{1,0:T(8,128)(2,1)}, u32[]{:S(2)}, u32[]{:S(2)}) %collective-permute-start.30) | collective-permute-done | bytes 884768 | tf_op jit(solution)/shard_map/ppermute | solution.py:1006
  389.1 10.9 %mix_weights.3 = (bf16[256,4096]{1,0:T(8,128)(2,1)}, bf16[256,4096]{1,0:T(8,128)(2,1)}) custom-call(s32[5]{0:T(128)} %stack.29.place.refs_0_, bf16[1024,1024]{1,0:T(8,128)(2,1)} %get-tuple-element.97.refs_1_, bf16[1024,1024]{1,0:T(8,128)(2,1)} %get-tuple-element.107.refs_2_, bf16[1024,3072]{1,0:T(8,128)(2,1)} %get-tuple-element.108.refs_3_, ...), custom_call_target="tpu_custom_call" | custom-call | flops 4294967296 | bytes 14680064 | tf_op jit(solution)/shard_map/mix_weights/pallas_call | solution.py:962
  404.7 17.7 %feed_output.1 = (bf16[1024,512]{1,0:T(8,128)(2,1)}, bf16[1024,512]{1,0:T(8,128)(2,1)}) custom-call(f32[1024,1024]{1,0:T(8,128)} %get-tuple-element.70.hidden.refs_1_.refs_0_, bf16[1024,3456]{1,0:T(8,128)(2,1)} %get-tuple-element.75.refs_3_.refs_1_, bf16[1024,3456]{1,0:T(8,128)(2,1)} %get-tuple-element.80.refs_3_.refs_2_, ...), custom_call_target="tpu_custom_call" | custom-call | flops 9663676416 | bytes 25165824 | tf_op jit(solution)/shard_map/feed_output/pallas_call | solution.py:692
  422.5 13.6 %collective-permute-done.35 = bf16[256,4096]{1,0:T(8,128)(2,1)} collective-permute-done((bf16[256,4096]{1,0:T(8,128)(2,1)}, bf16[256,4096]{1,0:T(8,128)(2,1)}, u32[]{:S(2)}, u32[]{:S(2)}) %collective-permute-start.35) | collective-permute-done | bytes 2097184 | tf_op jit(solution)/shard_map/ppermute | solution.py:1000
  439.5 4.7 collective-permute-done.34
  448.8 4.0 collective-permute-done.39
  456.4 15.3 %collective-permute-done.36.refs_1_ = bf16[128,3456]{1,0:T(8,128)(2,1)} collective-permute-done((bf16[128,3456]{1,0:T(8,128)(2,1)S(1)}, bf16[128,3456]{1,0:T(8,128)(2,1)}, u32[]{:S(2)}, u32[]{:S(2)}) %collective-permute-start.36) | collective-permute-done | bytes 884768 | tf_op jit(solution)/shard_map/ppermute | solution.py:994
  474.7 7.2 %collective-permute-done.41 = bf16[128,1024]{1,0:T(8,128)(2,1)S(1)} collective-permute-done((bf16[128,1024]{1,0:T(8,128)(2,1)S(1)}, bf16[128,1024]{1,0:T(8,128)(2,1)S(1)}, u32[]{:S(2)}, u32[]{:S(2)}) %collective-permute-start.41) | collective-permute-done | bytes 262176 | tf_op jit(solution)/shard_map/ppermute | solution.py:1006
  481.9 4.6 collective-permute-done.42
  495.5 6.2 %unpack.2 = (f32[2,512,1152]{2,1,0:T(8,128)}, f32[1152,512]{1,0:T(8,128)}) custom-call(s32[5]{0:T(128)} %stack.29.place.refs_0_, bf16[128,3456]{1,0:T(8,128)(2,1)} %copy-done.7, bf16[128,3456]{1,0:T(8,128)(2,1)} %collective-permute-done.36.refs_1_, bf16[128,3456]{1,0:T(8,128)(2,1)} %collective-permute-done.37.refs_2_, ...), custom_call_target="tpu_custom_call" | custom-call | tf_op jit(solution)/shard_map/unpack/pallas_call | solution.py:238
  (182 shorter events, 125.1 us)
Async XLA Ops:
  7.2 138.3 %all-gather.6.cloned.1.call-start = ((), (), s32[]{:S(2)}) async-start(), calls=%async_computation | async-start | bytes 4423680 | tf_op jit(solution)/shard_map/all_gather | solution.py:1087
  13.6 20.3 %collective-permute-start.1 = (bf16[144,1024]{1,0:T(8,128)(2,1)}, bf16[144,1024]{1,0:T(8,128)(2,1)S(1)}, u32[]{:S(2)}, u32[]{:S(2)}) collective-permute-start(bf16[144,1024]{1,0:T(8,128)(2,1)} %pack.4.refs_3_), channel_id=1, source_target_pairs={{0,2},{2,4},{4,6},{6,0},{1,3},{3,5},{5,7},{7,1},{8,10},{10,12},{12... | collective-permute-start | bytes 884744 | tf_op jit(solution)/shard_map/ppermute | solution.py:1006
  18.7 26.2 %collective-permute-start.3 = (bf16[144,1024]{1,0:T(8,128)(2,1)}, bf16[144,1024]{1,0:T(8,128)(2,1)S(1)}, u32[]{:S(2)}, u32[]{:S(2)}) collective-permute-start(bf16[144,1024]{1,0:T(8,128)(2,1)} %pack.4.refs_3_), channel_id=1, source_target_pairs={{0,4},{2,6},{4,0},{6,2},{1,5},{3,7},{5,1},{7,3},{8,12},{10,14},{12... | collective-permute-start | bytes 884744 | tf_op jit(solution)/shard_map/ppermute | solution.py:1006
  24.6 23.1 %collective-permute-start = (bf16[16,512]{1,0:T(8,128)(2,1)S(1)}, bf16[16,512]{1,0:T(8,128)(2,1)S(1)}, u32[]{:S(2)}, u32[]{:S(2)}) collective-permute-start(bf16[16,512]{1,0:T(8,128)(2,1)S(1)} %slice.127), channel_id=1, source_target_pairs={{0,2},{2,4},{4,6},{1,3},{3,5},{5,7},{8,10},{10,12},{12,14},{9,11},... | collective-permute-start | bytes 49160 | tf_op jit(solution)/shard_map/ppermute | solution.py:1068
  52.0 21.7 %collective-permute-start.4 = (bf16[2080,512]{1,0:T(8,128)(2,1)}, bf16[2080,512]{1,0:T(8,128)(2,1)}, u32[]{:S(2)}, u32[]{:S(2)}) collective-permute-start(bf16[2080,512]{1,0:T(8,128)(2,1)} %outgoing.1), channel_id=1, source_target_pairs={{0,1},{1,0},{2,3},{3,2},{4,5},{5,4},{6,7},{7,6},{8,9},{9,8},{10,11... | collective-permute-start | bytes 6389768 | tf_op jit(solution)/shard_map/ppermute | solution.py:990
  56.4 26.1 %collective-permute-start.6 = (bf16[432,1024]{1,0:T(8,128)(2,1)}, bf16[432,1024]{1,0:T(8,128)(2,1)}, u32[]{:S(2)}, u32[]{:S(2)}) collective-permute-start(bf16[432,1024]{1,0:T(8,128)(2,1)} %join_rows.1.refs_6_.refs_9_.refs_3_.refs_2_), channel_id=1, source_target_pairs={{0,16},{1,9},{8,24},{9,1},{16,0},{17,25},{24,8},{25,17},{2,18},{3,... | collective-permute-start | bytes 2654216 | tf_op jit(solution)/shard_map/ppermute | solution.py:1000
  57.9 24.5 %collective-permute-start.8 = (bf16[128,3456]{1,0:T(8,128)(2,1)}, bf16[128,3456]{1,0:T(8,128)(2,1)S(1)}, u32[]{:S(2)}, u32[]{:S(2)}) collective-permute-start(bf16[128,3456]{1,0:T(8,128)(2,1)} %pack.7), channel_id=1, source_target_pairs={{0,2},{2,4},{4,6},{6,0},{1,3},{3,5},{5,7},{7,1},{8,10},{10,12},{12... | collective-permute-start | bytes 2654216 | tf_op jit(solution)/shard_map/ppermute | solution.py:1006
  89.6 104.7 %all-gather.8.cloned.1.call-start = ((), (), s32[]{:S(2)}) async-start(), calls=%async_computation.1 | async-start | bytes 4423680 | tf_op jit(solution)/shard_map/all_gather | solution.py:1097
  89.7 31.1 %collective-permute-start.10 = (bf16[512,3456]{1,0:T(8,128)(2,1)}, bf16[512,3456]{1,0:T(8,128)(2,1)}, u32[]{:S(2)}, u32[]{:S(2)}) collective-permute-start(bf16[512,3456]{1,0:T(8,128)(2,1)} %pack.6.refs_4_.refs_5_), channel_id=1, source_target_pairs={{0,1},{1,0},{2,3},{3,2},{4,5},{5,4},{6,7},{7,6},{8,9},{9,8},{10,11... | collective-permute-start | bytes 10616840 | tf_op jit(solution)/shard_map/ppermute | solution.py:990
  92.9 52.8 %collective-permute-start.12 = (bf16[128,3456]{1,0:T(8,128)(2,1)}, bf16[128,3456]{1,0:T(8,128)(2,1)S(1)}, u32[]{:S(2)}, u32[]{:S(2)}) collective-permute-start(bf16[128,3456]{1,0:T(8,128)(2,1)} %pack.7), channel_id=1, source_target_pairs={{0,6},{2,0},{4,2},{6,4},{1,7},{3,1},{5,3},{7,5},{8,14},{10,8},{12,... | collective-permute-start | bytes 2654216 | tf_op jit(solution)/shard_map/ppermute | solution.py:1006
  146.6 102.2 %all-gather.10.cloned.1.call-start = ((), (), s32[]{:S(2)}) async-start(), calls=%async_computation.2 | async-start | bytes 4423680 | tf_op jit(solution)/shard_map/all_gather | solution.py:1097
  146.7 30.7 %collective-permute-start.13 = (bf16[512,3456]{1,0:T(8,128)(2,1)}, bf16[512,3456]{1,0:T(8,128)(2,1)}, u32[]{:S(2)}, u32[]{:S(2)}) collective-permute-start(bf16[512,3456]{1,0:T(8,128)(2,1)} %get-tuple-element.77), channel_id=1, source_target_pairs={{0,1},{1,0},{2,3},{3,2},{4,5},{5,4},{6,7},{7,6},{8,9},{9,8},{10,11... | collective-permute-start | bytes 10616840 | tf_op jit(solution)/shard_map/ppermute | solution.py:990
  147.1 47.2 %collective-permute-start.15 = (bf16[128,3456]{1,0:T(8,128)(2,1)}, bf16[128,3456]{1,0:T(8,128)(2,1)S(1)}, u32[]{:S(2)}, u32[]{:S(2)}) collective-permute-start(bf16[128,3456]{1,0:T(8,128)(2,1)} %pack.7), channel_id=1, source_target_pairs={{0,4},{2,6},{4,0},{6,2},{1,5},{3,7},{5,1},{7,3},{8,12},{10,14},{12... | collective-permute-start | bytes 2654216 | tf_op jit(solution)/shard_map/ppermute | solution.py:1006
  195.3 306.4 %all-gather.12.cloned.1.call-start = ((), (), s32[]{:S(2)}) async-start(), calls=%async_computation.3 | async-start | bytes 1081344 | tf_op jit(solution)/shard_map/all_gather | solution.py:1164
  195.3 32.9 %collective-permute-start.16 = (bf16[512,3456]{1,0:T(8,128)(2,1)}, bf16[512,3456]{1,0:T(8,128)(2,1)}, u32[]{:S(2)}, u32[]{:S(2)}) collective-permute-start(bf16[512,3456]{1,0:T(8,128)(2,1)} %get-tuple-element.83.refs_5_), channel_id=1, source_target_pairs={{0,1},{1,0},{2,3},{3,2},{4,5},{5,4},{6,7},{7,6},{8,9},{9,8},{10,11... | collective-permute-start | bytes 10616840 | tf_op jit(solution)/shard_map/ppermute | solution.py:990
  195.9 32.3 %collective-permute-start.17 = (bf16[256,3456]{1,0:T(8,128)(2,1)}, bf16[256,3456]{1,0:T(8,128)(2,1)}, u32[]{:S(2)}, u32[]{:S(2)}) collective-permute-start(bf16[256,3456]{1,0:T(8,128)(2,1)} %get-tuple-element.91), channel_id=1, source_target_pairs={{0,16},{1,9},{8,24},{9,1},{16,0},{17,25},{24,8},{25,17},{2,18},{3,... | collective-permute-start | bytes 5308424 | tf_op jit(solution)/shard_map/ppermute | solution.py:1000
  226.0 24.3 %collective-permute-start.19 = (bf16[512,3456]{1,0:T(8,128)(2,1)}, bf16[512,3456]{1,0:T(8,128)(2,1)}, u32[]{:S(2)}, u32[]{:S(2)}) collective-permute-start(bf16[512,3456]{1,0:T(8,128)(2,1)} %get-tuple-element.90.refs_5_), channel_id=1, source_target_pairs={{0,1},{1,0},{2,3},{3,2},{4,5},{5,4},{6,7},{7,6},{8,9},{9,8},{10,11... | collective-permute-start | bytes 10616840 | tf_op jit(solution)/shard_map/ppermute | solution.py:990
  248.9 40.0 %collective-permute-start.22 = (bf16[256,3456]{1,0:T(8,128)(2,1)}, bf16[256,3456]{1,0:T(8,128)(2,1)}, u32[]{:S(2)}, u32[]{:S(2)}) collective-permute-start(bf16[256,3456]{1,0:T(8,128)(2,1)} %get-tuple-element.104), channel_id=1, source_target_pairs={{0,16},{1,9},{8,24},{9,1},{16,0},{17,25},{24,8},{25,17},{2,18},{3,... | collective-permute-start | bytes 5308424 | tf_op jit(solution)/shard_map/ppermute | solution.py:1000
  260.6 35.6 %collective-permute-start.23 = (bf16[256,3456]{1,0:T(8,128)(2,1)}, bf16[256,3456]{1,0:T(8,128)(2,1)}, u32[]{:S(2)}, u32[]{:S(2)}) collective-permute-start(bf16[256,3456]{1,0:T(8,128)(2,1)} %get-tuple-element.105), channel_id=1, source_target_pairs={{0,16},{1,9},{8,24},{9,1},{16,0},{17,25},{24,8},{25,17},{2,18},{3,... | collective-permute-start | bytes 5308424 | tf_op jit(solution)/shard_map/ppermute | solution.py:1000
  285.5 23.9 %collective-permute-start.21 = (bf16[512,3456]{1,0:T(8,128)(2,1)}, bf16[512,3456]{1,0:T(8,128)(2,1)}, u32[]{:S(2)}, u32[]{:S(2)}) collective-permute-start(bf16[512,3456]{1,0:T(8,128)(2,1)} %get-tuple-element.103), channel_id=1, source_target_pairs={{0,1},{1,0},{2,3},{3,2},{4,5},{5,4},{6,7},{7,6},{8,9},{9,8},{10,11... | collective-permute-start | bytes 10616840 | tf_op jit(solution)/shard_map/ppermute | solution.py:990
  298.7 22.7 %collective-permute-start.25 = (bf16[128,3456]{1,0:T(8,128)(2,1)}, bf16[128,3456]{1,0:T(8,128)(2,1)}, u32[]{:S(2)}, u32[]{:S(2)}) collective-permute-start(bf16[128,3456]{1,0:T(8,128)(2,1)} %add_convert_fusion.8.refs_7_), channel_id=1, source_target_pairs={{0,8},{1,17},{8,0},{9,25},{16,24},{17,1},{24,16},{25,9},{2,10},{3,... | collective-permute-start | bytes 2654216 | tf_op jit(solution)/shard_map/ppermute | solution.py:994
  305.5 49.6 %collective-permute-start.26 = (bf16[128,3456]{1,0:T(8,128)(2,1)S(1)}, bf16[128,3456]{1,0:T(8,128)(2,1)}, u32[]{:S(2)}, u32[]{:S(2)}) collective-permute-start(bf16[128,3456]{1,0:T(8,128)(2,1)S(1)} %add_convert_fusion.7.refs_17_), channel_id=1, source_target_pairs={{0,6},{2,0},{4,2},{6,4},{1,7},{3,1},{5,3},{7,5},{8,14},{10,8},{12,... | collective-permute-start | bytes 2654216 | tf_op jit(solution)/shard_map/ppermute | solution.py:1006
  320.0 32.5 %collective-permute-start.27 = (bf16[256,3456]{1,0:T(8,128)(2,1)}, bf16[256,3456]{1,0:T(8,128)(2,1)}, u32[]{:S(2)}, u32[]{:S(2)}) collective-permute-start(bf16[256,3456]{1,0:T(8,128)(2,1)} %get-tuple-element.110), channel_id=1, source_target_pairs={{0,16},{1,9},{8,24},{9,1},{16,0},{17,25},{24,8},{25,17},{2,18},{3,... | collective-permute-start | bytes 5308424 | tf_op jit(solution)/shard_map/ppermute | solution.py:1000
  364.9 24.2 %collective-permute-start.28 = (bf16[512,4096]{1,0:T(8,128)(2,1)}, bf16[512,4096]{1,0:T(8,128)(2,1)}, u32[]{:S(2)}, u32[]{:S(2)}) collective-permute-start(bf16[512,4096]{1,0:T(8,128)(2,1)} %mix_weights.2), channel_id=1, source_target_pairs={{0,1},{1,0},{2,3},{3,2},{4,5},{5,4},{6,7},{7,6},{8,9},{9,8},{10,11... | collective-permute-start | bytes 12582920 | tf_op jit(solution)/shard_map/ppermute | solution.py:990
  366.0 23.2 %collective-permute-start.30 = (bf16[128,3456]{1,0:T(8,128)(2,1)S(1)}, bf16[128,3456]{1,0:T(8,128)(2,1)}, u32[]{:S(2)}, u32[]{:S(2)}) collective-permute-start(bf16[128,3456]{1,0:T(8,128)(2,1)S(1)} %copy-done.5), channel_id=1, source_target_pairs={{0,2},{2,4},{4,6},{6,0},{1,3},{3,5},{5,7},{7,1},{8,10},{10,12},{12... | collective-permute-start | bytes 2654216 | tf_op jit(solution)/shard_map/ppermute | solution.py:1006
  400.0 36.1 %collective-permute-start.35 = (bf16[256,4096]{1,0:T(8,128)(2,1)}, bf16[256,4096]{1,0:T(8,128)(2,1)}, u32[]{:S(2)}, u32[]{:S(2)}) collective-permute-start(bf16[256,4096]{1,0:T(8,128)(2,1)} %get-tuple-element.119), channel_id=1, source_target_pairs={{0,16},{1,9},{8,24},{9,1},{16,0},{17,25},{24,8},{25,17},{2,18},{3,... | collective-permute-start | bytes 6291464 | tf_op jit(solution)/shard_map/ppermute | solution.py:1000
  404.1 40.1 %collective-permute-start.33 = (bf16[128,3456]{1,0:T(8,128)(2,1)}, bf16[128,3456]{1,0:T(8,128)(2,1)}, u32[]{:S(2)}, u32[]{:S(2)}) collective-permute-start(bf16[128,3456]{1,0:T(8,128)(2,1)} %add_convert_fusion.3), channel_id=1, source_target_pairs={{0,8},{1,17},{8,0},{9,25},{16,24},{17,1},{24,16},{25,9},{2,10},{3,... | collective-permute-start | bytes 2654216 | tf_op jit(solution)/shard_map/ppermute | solution.py:994
  404.7 39.5 %collective-permute-start.34 = (bf16[128,3456]{1,0:T(8,128)(2,1)S(1)}, bf16[128,3456]{1,0:T(8,128)(2,1)}, u32[]{:S(2)}, u32[]{:S(2)}) collective-permute-start(bf16[128,3456]{1,0:T(8,128)(2,1)S(1)} %copy-done.8), channel_id=1, source_target_pairs={{0,4},{2,6},{4,0},{6,2},{1,5},{3,7},{5,1},{7,3},{8,12},{10,14},{12... | collective-permute-start | bytes 2654216 | tf_op jit(solution)/shard_map/ppermute | solution.py:1006
  422.4 64.5 %collective-permute-start.32 = (bf16[1024,512]{1,0:T(8,128)(2,1)}, bf16[1024,512]{1,0:T(8,128)(2,1)}, u32[]{:S(2)}, u32[]{:S(2)}) collective-permute-start(bf16[1024,512]{1,0:T(8,128)(2,1)} %get-tuple-element.117), channel_id=1, source_target_pairs={{0,1},{1,0},{2,3},{3,2},{4,5},{5,4},{6,7},{7,6},{8,9},{9,8},{10,11... | collective-permute-start | bytes 3145736 | tf_op jit(solution)/shard_map/ppermute | solution.py:990
  447.2 24.4 %collective-permute-start.36 = (bf16[128,3456]{1,0:T(8,128)(2,1)S(1)}, bf16[128,3456]{1,0:T(8,128)(2,1)}, u32[]{:S(2)}, u32[]{:S(2)}) collective-permute-start(bf16[128,3456]{1,0:T(8,128)(2,1)S(1)} %add_convert_fusion.2.refs_0_), channel_id=1, source_target_pairs={{0,8},{1,17},{8,0},{9,25},{16,24},{17,1},{24,16},{25,9},{2,10},{3,... | collective-permute-start | bytes 2654216 | tf_op jit(solution)/shard_map/ppermute | solution.py:994
  454.9 40.6 %collective-permute-start.37 = (bf16[128,3456]{1,0:T(8,128)(2,1)S(1)}, bf16[128,3456]{1,0:T(8,128)(2,1)}, u32[]{:S(2)}, u32[]{:S(2)}) collective-permute-start(bf16[128,3456]{1,0:T(8,128)(2,1)S(1)} %add_convert_fusion.2.refs_0_), channel_id=1, source_target_pairs={{0,16},{1,9},{8,24},{9,1},{16,0},{17,25},{24,8},{25,17},{2,18},{3,... | collective-permute-start | bytes 2654216 | tf_op jit(solution)/shard_map/ppermute | solution.py:1000
  471.6 23.9 %collective-permute-start.38 = (bf16[128,3456]{1,0:T(8,128)(2,1)}, bf16[128,3456]{1,0:T(8,128)(2,1)}, u32[]{:S(2)}, u32[]{:S(2)}) collective-permute-start(bf16[128,3456]{1,0:T(8,128)(2,1)} %collective-permute-done.36.refs_1_), channel_id=1, source_target_pairs={{0,16},{1,9},{8,24},{9,1},{16,0},{17,25},{24,8},{25,17},{2,18},{3,... | collective-permute-start | bytes 2654216 | tf_op jit(solution)/shard_map/ppermute | solution.py:1000
  (41 other events, 425.0 us)
Sparse Core Ops, SparseCore 0:
  89.7 47.3 all-gather.5
  146.8 47.5 all-gather.7
  196.8 52.0 all-gather.9
  404.2 64.5 all-gather.11

commit v5 on v3

--- a/solution.py
+++ b/solution.py
@@ -1185,7 +1185,7 @@
     output_back = join_tokens(own_out, other_out, place)
     gate_up_grad, down_grad = unpack(feed_sum, 2, place)
     in_grad, out_grad = unpack(mix_sum, 3, place)
-    every = after(every, gate_up_grad)
+    every = after(every, mix_sum[0])
     sums = jnp.sum(every.reshape(16, 2, *packed_sums.shape), axis=0)
     mine, other = sums[core], sums[1 - core]
     gain_grads = mine[:2, :half] + other[:2, half:]

time: 521 us -> 517 us (level)
  waiting for transfers between devices: 128 us -> 114 us
    ppermute x8, waiting for transfers between devices: 40.6 us -> 31.7 us  [across_first(): lax.ppermute(value, ('dp', 'col'), [(2 * p + c, 2 * (p ^ 1 << c) + c) for...]
  transfers between devices with their start and end apart: 50 -> 50, of which waited for: 20 -> 20; matrix products, arithmetic and copies ran while one was open for 7% -> 8% of each run, Pallas kernels for 48% -> 49%
where the time goes in v5:
time: 517 us; the launch traced here: 511 us
  Pallas kernels  285 us (55%)
  waiting for transfers between devices  114 us (22%)
  starting transfers between devices  47.7 us (9%)
  other arithmetic  30 us (6%)
  between operations  18.4 us (4%)
  local copies, waits for them, and re-layouts  16.2 us (3%)
    pallas_call x4, Pallas kernels, feed(): call(body, 'feed', (shape_of(count, width, dtype=f32), shape_of(count, la...  104 us
    pallas_call x4, Pallas kernels, feed_weights(): call(body, 'feed_weights', (shape_of(half // 2, lanes),) * 2, flops=6 * c...  40.2 us
    ppermute x8, waiting for transfers between devices, across_first(): lax.ppermute(value, ('dp', 'col'), [(2 * p + c, 2 * (p ^ 1 << c) + c) for...  31.7 us
    ppermute x12, waiting for transfers between devices, along_row(): lax.ppermute(value, 'row', [(i, (i + steps) % BLOCKS) for i in range(BLOC...  30.1 us
    pallas_call x1, Pallas kernels, mix_backward(): call(body, 'mix_backward', (shape_of(count, half), shape_of(count, half),...  25.9 us
    convert_element_type x11, other arithmetic, add(): return sum((part.astype(f32) for part in parts)).astype(bf16)  25.6 us
    pallas_call x1, Pallas kernels, mix_forward(): call(body, 'mix_forward', (flat, flat, flat, flat, wide, flat, flat, shap...  23.6 us
    pallas_call x2, Pallas kernels, mix_weights(): call(body, 'mix_weights', (shape_of(half // 2, 4 * width),) * 2 if more e...  20.7 us
  transfers between devices with their start and end apart: 50, of which 20 were waited for; matrix products, arithmetic and copies ran while one was open for 8% of the time, Pallas kernels for 49%

profile of v5, /device:TPU:0, one launch (start us, length us, event | category | flops | bytes accessed | tf_op | source)
XLA Modules:
  0.0 511.1 jit_solution(2233688126756523897)
XLA Ops:
  19.7 4.2 pack.5.refs_3_.refs_1_
  29.4 5.2 %pack.6.refs_4_.refs_5_ = bf16[512,3456]{1,0:T(8,128)(2,1)} custom-call(s32[5]{0:T(128)} %stack.29.place.refs_0_, bf16[2,512,1152]{2,1,0:T(8,128)(2,1)} %refs_1_.9, bf16[1152,512]{1,0:T(8,128)(2,1)} %refs_2_.7, bf16[512,1024]{1,0:T(8,128)(2,1)} %pack.5.refs_3_.refs_1_), custom_call_target="tpu_custom_call" | custom-call | tf_op jit(solution)/shard_map/pack/pallas_call | solution.py:160
  34.6 10.2 %collective-permute-done.3.refs_2_ = bf16[144,1024]{1,0:T(8,128)(2,1)S(1)} collective-permute-done((bf16[144,1024]{1,0:T(8,128)(2,1)}, bf16[144,1024]{1,0:T(8,128)(2,1)S(1)}, u32[]{:S(2)}, u32[]{:S(2)}) %collective-permute-start.3) | collective-permute-done | bytes 294944 | tf_op jit(solution)/shard_map/ppermute | solution.py:1005
  57.9 16.0 %collective-permute-done.5.refs_3_ = bf16[432,1024]{1,0:T(8,128)(2,1)} collective-permute-done((bf16[432,1024]{1,0:T(8,128)(2,1)S(1)}, bf16[432,1024]{1,0:T(8,128)(2,1)}, u32[]{:S(2)}, u32[]{:S(2)}) %collective-permute-start.5) | collective-permute-done | bytes 884768 | tf_op jit(solution)/shard_map/ppermute | solution.py:993
  77.2 7.5 %prepare.1 = (bf16[1040,1024]{1,0:T(8,128)(2,1)}, bf16[1024,1024]{1,0:T(8,128)(2,1)}, bf16[1024,1024]{1,0:T(8,128)(2,1)}, bf16[1024,1024]{1,0:T(8,128)(2,1)}) custom-call(s32[5]{0:T(128)} %stack.29.place.refs_0_, bf16[2048,512]{1,0:T(8,128)(2,1)} %refs_4_.3, bf16[2080,512]{1,0:T(8,128)(2,1)} %collective-permute-done.4.refs_2_.refs_5_.refs_7_.refs_4_, ...), custom_call_target="tpu_custom_call" | custom-call | bytes 16777216 | tf_op jit(solution)/shard_map/prepare/pallas_call | solution.py:314
  87.3 4.6 mix_assemble.1.refs_1_.refs_0_.refs_14_
  99.4 23.6 %mix_forward.1 = (bf16[1024,1024]{1,0:T(8,128)(2,1)}, bf16[1024,1024]{1,0:T(8,128)(2,1)}, bf16[1024,1024]{1,0:T(8,128)(2,1)}, bf16[1024,1024]{1,0:T(8,128)(2,1)}...) custom-call(s32[5]{0:T(128)} %stack.29.place.refs_0_, ...), custom_call_target="tpu_custom_call" | custom-call | flops 8589934592 | bytes 39845888 | tf_op jit(solution)/shard_map/mix_forward/pallas_call | solution.py:488
  123.0 25.5 %feed.4 = (f32[1024,1024]{1,0:T(8,128)}, bf16[1024,3456]{1,0:T(8,128)(2,1)}, bf16[512,3456]{1,0:T(8,128)(2,1)}) custom-call(bf16[1024,1024]{1,0:T(8,128)(2,1)} %get-tuple-element.71.refs_0_.normed_hbm, bf16[1024,1024]{1,0:T(8,128)(2,1)} %get-tuple-element.72.refs_1_.low_hbm.low.refs_3_, bf16[1024,1024]{1,0:T(8,128)(2,1)} %get-tuple-element.73.refs_2_.normed_t_hbm.refs_1_, ...), custom_call_target="tpu_custom_call" | custom-call | flops 15703474176 | bytes 34471936 | tf_op jit(solution)/shard_map/feed/pallas_call | solution.py:648
  150.2 5.0 collective-permute-done.11.other_hbm.refs_10_
  155.2 26.3 %feed.5 = (f32[1024,1024]{1,0:T(8,128)}, bf16[1024,3456]{1,0:T(8,128)(2,1)}, bf16[512,3456]{1,0:T(8,128)(2,1)}) custom-call(bf16[1024,1024]{1,0:T(8,128)(2,1)} %get-tuple-element.71.refs_0_.normed_hbm, bf16[1024,1024]{1,0:T(8,128)(2,1)} %get-tuple-element.72.refs_1_.low_hbm.low.refs_3_, bf16[1024,1024]{1,0:T(8,128)(2,1)} %get-tuple-element.73.refs_2_.normed_t_hbm.refs_1_, ...), custom_call_target="tpu_custom_call" | custom-call | flops 15703474176 | bytes 34471936 | tf_op jit(solution)/shard_map/feed/pallas_call | solution.py:648
  181.4 10.0 %feed_weights.4 = (bf16[256,3456]{1,0:T(8,128)(2,1)}, bf16[256,3456]{1,0:T(8,128)(2,1)}) custom-call(s32[5]{0:T(128)} %stack.29.place.refs_0_, bf16[1024,1024]{1,0:T(8,128)(2,1)} %get-tuple-element.73.refs_2_.normed_t_hbm.refs_1_, bf16[1024,1024]{1,0:T(8,128)(2,1)} %get-tuple-element.74.refs_3_.low_t_hbm.refs_2_, ...), custom_call_target="tpu_custom_call" | custom-call | flops 3623878656 | bytes 16252928 | tf_op jit(solution)/shard_map/feed_weights/pallas_call | solution.py:737
  191.5 5.9 %all-gather.8.cloned.1.call-done.refs_4_.refs_7_ = bf16[512,3456]{1,0:T(8,128)(2,1)} async-done(((bf16[128,3456]{1,0:T(8,128)(2,1)}), bf16[512,3456]{1,0:T(8,128)(2,1)}) %all-gather.8.cloned.1.call-update) | async-done | bytes 3538960 | tf_op jit(solution)/shard_map/all_gather | solution.py:1096
  204.0 26.4 %feed.6 = (f32[1024,1024]{1,0:T(8,128)}, bf16[1024,3456]{1,0:T(8,128)(2,1)}, bf16[512,3456]{1,0:T(8,128)(2,1)}) custom-call(bf16[1024,1024]{1,0:T(8,128)(2,1)} %get-tuple-element.71.refs_0_.normed_hbm, bf16[1024,1024]{1,0:T(8,128)(2,1)} %get-tuple-element.72.refs_1_.low_hbm.low.refs_3_, bf16[1024,1024]{1,0:T(8,128)(2,1)} %get-tuple-element.73.refs_2_.normed_t_hbm.refs_1_, ...), custom_call_target="tpu_custom_call" | custom-call | flops 15703474176 | bytes 34471936 | tf_op jit(solution)/shard_map/feed/pallas_call | solution.py:648
  231.3 10.1 %feed_weights.5 = (bf16[256,3456]{1,0:T(8,128)(2,1)}, bf16[256,3456]{1,0:T(8,128)(2,1)}) custom-call(s32[5]{0:T(128)} %stack.29.place.refs_0_, bf16[1024,1024]{1,0:T(8,128)(2,1)} %get-tuple-element.73.refs_2_.normed_t_hbm.refs_1_, bf16[1024,1024]{1,0:T(8,128)(2,1)} %get-tuple-element.74.refs_3_.low_t_hbm.refs_2_, ...), custom_call_target="tpu_custom_call" | custom-call | flops 3623878656 | bytes 16252928 | tf_op jit(solution)/shard_map/feed_weights/pallas_call | solution.py:737
  241.3 10.6 %all-gather.10.cloned.1.call-done.refs_4_.refs_8_ = bf16[512,3456]{1,0:T(8,128)(2,1)} async-done(((bf16[128,3456]{1,0:T(8,128)(2,1)}), bf16[512,3456]{1,0:T(8,128)(2,1)}) %all-gather.10.cloned.1.call-update) | async-done | bytes 3538960 | tf_op jit(solution)/shard_map/all_gather | solution.py:1096
  253.4 10.0 %feed_weights.6 = (bf16[256,3456]{1,0:T(8,128)(2,1)}, bf16[256,3456]{1,0:T(8,128)(2,1)}) custom-call(s32[5]{0:T(128)} %stack.29.place.refs_0_, bf16[1024,1024]{1,0:T(8,128)(2,1)} %get-tuple-element.73.refs_2_.normed_t_hbm.refs_1_, bf16[1024,1024]{1,0:T(8,128)(2,1)} %get-tuple-element.74.refs_3_.low_t_hbm.refs_2_, ...), custom_call_target="tpu_custom_call" | custom-call | flops 3623878656 | bytes 16252928 | tf_op jit(solution)/shard_map/feed_weights/pallas_call | solution.py:737
  264.0 25.6 %feed.7 = (f32[1024,1024]{1,0:T(8,128)}, bf16[1024,3456]{1,0:T(8,128)(2,1)}, bf16[512,3456]{1,0:T(8,128)(2,1)}) custom-call(bf16[1024,1024]{1,0:T(8,128)(2,1)} %get-tuple-element.71.refs_0_.normed_hbm, bf16[1024,1024]{1,0:T(8,128)(2,1)} %get-tuple-element.72.refs_1_.low_hbm.low.refs_3_, bf16[1024,1024]{1,0:T(8,128)(2,1)} %get-tuple-element.73.refs_2_.normed_t_hbm.refs_1_, ...), custom_call_target="tpu_custom_call" | custom-call | flops 15703474176 | bytes 34471936 | tf_op jit(solution)/shard_map/feed/pallas_call | solution.py:648
  303.5 4.4 collective-permute-done.24
  313.7 10.1 %feed_weights.7 = (bf16[256,3456]{1,0:T(8,128)(2,1)}, bf16[256,3456]{1,0:T(8,128)(2,1)}) custom-call(s32[5]{0:T(128)} %stack.29.place.refs_0_, bf16[1024,1024]{1,0:T(8,128)(2,1)} %get-tuple-element.73.refs_2_.normed_t_hbm.refs_1_, bf16[1024,1024]{1,0:T(8,128)(2,1)} %get-tuple-element.74.refs_3_.low_t_hbm.refs_2_, ...), custom_call_target="tpu_custom_call" | custom-call | flops 3623878656 | bytes 16252928 | tf_op jit(solution)/shard_map/feed_weights/pallas_call | solution.py:737
  328.2 25.9 %mix_backward.1 = (bf16[1024,512]{1,0:T(8,128)(2,1)}, bf16[1024,512]{1,0:T(8,128)(2,1)}, bf16[1024,3072]{1,0:T(8,128)(2,1)}, bf16[1024,1024]{1,0:T(8,128)(2,1)}, f32[8,1024]{1,0:T(8,128)}) custom-call(s32[5]{0:T(128)} %stack.29.place.refs_0_, f32[1024,1024]{1,0:T(8,128)} %get-tuple-element.70.hidden.refs_1_.refs_0_, ...), custom_call_target="tpu_custom_call" | custom-call | flops 8589934592 | bytes 46137344 | tf_op jit(solution)/shard_map/mix_backward/pallas_call | solution.py:873
  358.8 9.8 %mix_weights.2 = bf16[512,4096]{1,0:T(8,128)(2,1)} custom-call(s32[5]{0:T(128)} %stack.29.place.refs_0_, bf16[1024,1024]{1,0:T(8,128)(2,1)} %get-tuple-element.97.refs_1_, bf16[1024,1024]{1,0:T(8,128)(2,1)} %get-tuple-element.107.refs_2_, bf16[1024,3072]{1,0:T(8,128)(2,1)} %get-tuple-element.108.refs_3_, bf16[1024,1024]{1,0:T(8,128)(2,1)} %get-tuple-element.109.refs_4_, ...), custom_call_target="tpu_custom_call" | custom-call | flops 4294967296 | bytes 14680064 | tf_op jit(solution)/shard_map/mix_weights/pallas_call | solution.py:961
  369.7 7.9 %collective-permute-done.31.theirs = bf16[1024,512]{1,0:T(8,128)(2,1)} collective-permute-done((bf16[1024,512]{1,0:T(8,128)(2,1)}, bf16[1024,512]{1,0:T(8,128)(2,1)}, u32[]{:S(2)}, u32[]{:S(2)}) %collective-permute-start.31) | collective-permute-done | bytes 1048608 | tf_op jit(solution)/shard_map/ppermute | solution.py:989
  385.4 7.5 %collective-permute-done.30.refs_7_ = bf16[128,3456]{1,0:T(8,128)(2,1)} collective-permute-done((bf16[128,3456]{1,0:T(8,128)(2,1)S(1)}, bf16[128,3456]{1,0:T(8,128)(2,1)}, u32[]{:S(2)}, u32[]{:S(2)}) %collective-permute-start.30) | collective-permute-done | bytes 884768 | tf_op jit(solution)/shard_map/ppermute | solution.py:1005
  392.9 10.9 %mix_weights.3 = (bf16[256,4096]{1,0:T(8,128)(2,1)}, bf16[256,4096]{1,0:T(8,128)(2,1)}) custom-call(s32[5]{0:T(128)} %stack.29.place.refs_0_, bf16[1024,1024]{1,0:T(8,128)(2,1)} %get-tuple-element.97.refs_1_, bf16[1024,1024]{1,0:T(8,128)(2,1)} %get-tuple-element.107.refs_2_, bf16[1024,3072]{1,0:T(8,128)(2,1)} %get-tuple-element.108.refs_3_, ...), custom_call_target="tpu_custom_call" | custom-call | flops 4294967296 | bytes 14680064 | tf_op jit(solution)/shard_map/mix_weights/pallas_call | solution.py:961
  408.4 17.8 %feed_output.1 = (bf16[1024,512]{1,0:T(8,128)(2,1)}, bf16[1024,512]{1,0:T(8,128)(2,1)}) custom-call(f32[1024,1024]{1,0:T(8,128)} %get-tuple-element.70.hidden.refs_1_.refs_0_, bf16[1024,3456]{1,0:T(8,128)(2,1)} %get-tuple-element.75.refs_3_.refs_1_, bf16[1024,3456]{1,0:T(8,128)(2,1)} %get-tuple-element.80.refs_3_.refs_2_, ...), custom_call_target="tpu_custom_call" | custom-call | flops 9663676416 | bytes 25165824 | tf_op jit(solution)/shard_map/feed_output/pallas_call | solution.py:691
  426.3 13.5 %collective-permute-done.33 = bf16[256,4096]{1,0:T(8,128)(2,1)} collective-permute-done((bf16[256,4096]{1,0:T(8,128)(2,1)}, bf16[256,4096]{1,0:T(8,128)(2,1)}, u32[]{:S(2)}, u32[]{:S(2)}) %collective-permute-start.33) | collective-permute-done | bytes 2097184 | tf_op jit(solution)/shard_map/ppermute | solution.py:999
  443.2 4.7 collective-permute-done.42
  447.9 3.9 add_convert_fusion.2.refs_0_
  471.6 6.9 %collective-permute-done.37 = bf16[128,1024]{1,0:T(8,128)(2,1)S(1)} collective-permute-done((bf16[128,1024]{1,0:T(8,128)(2,1)}, bf16[128,1024]{1,0:T(8,128)(2,1)S(1)}, u32[]{:S(2)}, u32[]{:S(2)}) %collective-permute-start.37) | collective-permute-done | bytes 262176 | tf_op jit(solution)/shard_map/ppermute | solution.py:1005
  485.1 5.5 %collective-permute-done.38.refs_1_ = bf16[128,1024]{1,0:T(8,128)(2,1)S(1)} collective-permute-done((bf16[128,1024]{1,0:T(8,128)(2,1)S(1)}, bf16[128,1024]{1,0:T(8,128)(2,1)S(1)}, u32[]{:S(2)}, u32[]{:S(2)}) %collective-permute-start.38) | collective-permute-done | bytes 262176 | tf_op jit(solution)/shard_map/ppermute | solution.py:993
  493.0 6.1 %unpack.3 = (f32[2,512,1152]{2,1,0:T(8,128)}, f32[1152,512]{1,0:T(8,128)}) custom-call(s32[5]{0:T(128)} %stack.29.place.refs_0_, bf16[128,3456]{1,0:T(8,128)(2,1)} %add_convert_fusion.2.refs_0_, bf16[128,3456]{1,0:T(8,128)(2,1)} %collective-permute-done.43.refs_1_, bf16[128,3456]{1,0:T(8,128)(2,1)} %collective-permute-done.44.refs_2_, ...), custom_call_target="tpu_custom_call" | custom-call | tf_op jit(solution)/shard_map/unpack/pallas_call | solution.py:237
  500.4 3.9 unpack.2
  (186 shorter events, 127.3 us)
Async XLA Ops:
  7.2 141.3 %all-gather.6.cloned.1.call-start = ((), (), s32[]{:S(2)}) async-start(), calls=%async_computation | async-start | bytes 4423680 | tf_op jit(solution)/shard_map/all_gather | solution.py:1086
  13.6 21.0 %collective-permute-start.1 = (bf16[144,1024]{1,0:T(8,128)(2,1)}, bf16[144,1024]{1,0:T(8,128)(2,1)S(1)}, u32[]{:S(2)}, u32[]{:S(2)}) collective-permute-start(bf16[144,1024]{1,0:T(8,128)(2,1)} %pack.4.refs_3_), channel_id=1, source_target_pairs={{0,2},{2,4},{4,6},{6,0},{1,3},{3,5},{5,7},{7,1},{8,10},{10,12},{12... | collective-permute-start | bytes 884744 | tf_op jit(solution)/shard_map/ppermute | solution.py:1005
  18.7 26.2 %collective-permute-start.3 = (bf16[144,1024]{1,0:T(8,128)(2,1)}, bf16[144,1024]{1,0:T(8,128)(2,1)S(1)}, u32[]{:S(2)}, u32[]{:S(2)}) collective-permute-start(bf16[144,1024]{1,0:T(8,128)(2,1)} %pack.4.refs_3_), channel_id=1, source_target_pairs={{0,4},{2,6},{4,0},{6,2},{1,5},{3,7},{5,1},{7,3},{8,12},{10,14},{12... | collective-permute-start | bytes 884744 | tf_op jit(solution)/shard_map/ppermute | solution.py:1005
  25.2 22.5 %collective-permute-start = (bf16[16,512]{1,0:T(8,128)(2,1)}, bf16[16,512]{1,0:T(8,128)(2,1)S(1)}, u32[]{:S(2)}, u32[]{:S(2)}) collective-permute-start(bf16[16,512]{1,0:T(8,128)(2,1)} %slice.127), channel_id=1, source_target_pairs={{0,2},{2,4},{4,6},{1,3},{3,5},{5,7},{8,10},{10,12},{12,14},{9,11},... | collective-permute-start | bytes 49160 | tf_op jit(solution)/shard_map/ppermute | solution.py:1067
  52.0 23.9 %collective-permute-start.4 = (bf16[2080,512]{1,0:T(8,128)(2,1)}, bf16[2080,512]{1,0:T(8,128)(2,1)}, u32[]{:S(2)}, u32[]{:S(2)}) collective-permute-start(bf16[2080,512]{1,0:T(8,128)(2,1)} %outgoing.1), channel_id=1, source_target_pairs={{0,1},{1,0},{2,3},{3,2},{4,5},{5,4},{6,7},{7,6},{8,9},{9,8},{10,11... | collective-permute-start | bytes 6389768 | tf_op jit(solution)/shard_map/ppermute | solution.py:989
  52.0 21.9 %collective-permute-start.5 = (bf16[432,1024]{1,0:T(8,128)(2,1)S(1)}, bf16[432,1024]{1,0:T(8,128)(2,1)}, u32[]{:S(2)}, u32[]{:S(2)}) collective-permute-start(bf16[432,1024]{1,0:T(8,128)(2,1)S(1)} %copy-done.2), channel_id=1, source_target_pairs={{0,8},{1,17},{8,0},{9,25},{16,24},{17,1},{24,16},{25,9},{2,10},{3,... | collective-permute-start | bytes 2654216 | tf_op jit(solution)/shard_map/ppermute | solution.py:993
  53.5 31.2 %collective-permute-start.6 = (bf16[432,1024]{1,0:T(8,128)(2,1)S(1)}, bf16[432,1024]{1,0:T(8,128)(2,1)}, u32[]{:S(2)}, u32[]{:S(2)}) collective-permute-start(bf16[432,1024]{1,0:T(8,128)(2,1)S(1)} %copy-done.2), channel_id=1, source_target_pairs={{0,16},{1,9},{8,24},{9,1},{16,0},{17,25},{24,8},{25,17},{2,18},{3,... | collective-permute-start | bytes 2654216 | tf_op jit(solution)/shard_map/ppermute | solution.py:999
  57.9 26.8 %collective-permute-start.8 = (bf16[128,3456]{1,0:T(8,128)(2,1)}, bf16[128,3456]{1,0:T(8,128)(2,1)}, u32[]{:S(2)}, u32[]{:S(2)}) collective-permute-start(bf16[128,3456]{1,0:T(8,128)(2,1)} %pack.7), channel_id=1, source_target_pairs={{0,2},{2,4},{4,6},{6,0},{1,3},{3,5},{5,7},{7,1},{8,10},{10,12},{12... | collective-permute-start | bytes 2654216 | tf_op jit(solution)/shard_map/ppermute | solution.py:1005
  91.9 105.5 %all-gather.8.cloned.1.call-start = ((), (), s32[]{:S(2)}) async-start(), calls=%async_computation.1 | async-start | bytes 4423680 | tf_op jit(solution)/shard_map/all_gather | solution.py:1096
  91.9 31.0 %collective-permute-start.10 = (bf16[512,3456]{1,0:T(8,128)(2,1)}, bf16[512,3456]{1,0:T(8,128)(2,1)}, u32[]{:S(2)}, u32[]{:S(2)}) collective-permute-start(bf16[512,3456]{1,0:T(8,128)(2,1)} %pack.6.refs_4_.refs_5_), channel_id=1, source_target_pairs={{0,1},{1,0},{2,3},{3,2},{4,5},{5,4},{6,7},{7,6},{8,9},{9,8},{10,11... | collective-permute-start | bytes 10616840 | tf_op jit(solution)/shard_map/ppermute | solution.py:989
  95.2 53.6 %collective-permute-start.12 = (bf16[128,3456]{1,0:T(8,128)(2,1)}, bf16[128,3456]{1,0:T(8,128)(2,1)S(1)}, u32[]{:S(2)}, u32[]{:S(2)}) collective-permute-start(bf16[128,3456]{1,0:T(8,128)(2,1)} %pack.7), channel_id=1, source_target_pairs={{0,6},{2,0},{4,2},{6,4},{1,7},{3,1},{5,3},{7,5},{8,14},{10,8},{12,... | collective-permute-start | bytes 2654216 | tf_op jit(solution)/shard_map/ppermute | solution.py:1005
  149.7 102.2 %all-gather.10.cloned.1.call-start = ((), (), s32[]{:S(2)}) async-start(), calls=%async_computation.2 | async-start | bytes 4423680 | tf_op jit(solution)/shard_map/all_gather | solution.py:1096
  149.7 31.7 %collective-permute-start.13 = (bf16[512,3456]{1,0:T(8,128)(2,1)}, bf16[512,3456]{1,0:T(8,128)(2,1)}, u32[]{:S(2)}, u32[]{:S(2)}) collective-permute-start(bf16[512,3456]{1,0:T(8,128)(2,1)} %get-tuple-element.77), channel_id=1, source_target_pairs={{0,1},{1,0},{2,3},{3,2},{4,5},{5,4},{6,7},{7,6},{8,9},{9,8},{10,11... | collective-permute-start | bytes 10616840 | tf_op jit(solution)/shard_map/ppermute | solution.py:989
  150.2 47.2 %collective-permute-start.15 = (bf16[128,3456]{1,0:T(8,128)(2,1)}, bf16[128,3456]{1,0:T(8,128)(2,1)S(1)}, u32[]{:S(2)}, u32[]{:S(2)}) collective-permute-start(bf16[128,3456]{1,0:T(8,128)(2,1)} %pack.7), channel_id=1, source_target_pairs={{0,4},{2,6},{4,0},{6,2},{1,5},{3,7},{5,1},{7,3},{8,12},{10,14},{12... | collective-permute-start | bytes 2654216 | tf_op jit(solution)/shard_map/ppermute | solution.py:1005
  198.3 285.4 %all-gather.12.cloned.1.call-start = ((), (), s32[]{:S(2)}) async-start(), calls=%async_computation.3 | async-start | bytes 1081344 | tf_op jit(solution)/shard_map/all_gather | solution.py:1163
  198.4 32.9 %collective-permute-start.16 = (bf16[512,3456]{1,0:T(8,128)(2,1)}, bf16[512,3456]{1,0:T(8,128)(2,1)}, u32[]{:S(2)}, u32[]{:S(2)}) collective-permute-start(bf16[512,3456]{1,0:T(8,128)(2,1)} %get-tuple-element.83.refs_5_), channel_id=1, source_target_pairs={{0,1},{1,0},{2,3},{3,2},{4,5},{5,4},{6,7},{7,6},{8,9},{9,8},{10,11... | collective-permute-start | bytes 10616840 | tf_op jit(solution)/shard_map/ppermute | solution.py:989
  199.0 32.3 %collective-permute-start.17 = (bf16[256,3456]{1,0:T(8,128)(2,1)}, bf16[256,3456]{1,0:T(8,128)(2,1)}, u32[]{:S(2)}, u32[]{:S(2)}) collective-permute-start(bf16[256,3456]{1,0:T(8,128)(2,1)} %get-tuple-element.91), channel_id=1, source_target_pairs={{0,16},{1,9},{8,24},{9,1},{16,0},{17,25},{24,8},{25,17},{2,18},{3,... | collective-permute-start | bytes 5308424 | tf_op jit(solution)/shard_map/ppermute | solution.py:999
  230.4 23.0 %collective-permute-start.19 = (bf16[512,3456]{1,0:T(8,128)(2,1)}, bf16[512,3456]{1,0:T(8,128)(2,1)}, u32[]{:S(2)}, u32[]{:S(2)}) collective-permute-start(bf16[512,3456]{1,0:T(8,128)(2,1)} %get-tuple-element.90.refs_5_), channel_id=1, source_target_pairs={{0,1},{1,0},{2,3},{3,2},{4,5},{5,4},{6,7},{7,6},{8,9},{9,8},{10,11... | collective-permute-start | bytes 10616840 | tf_op jit(solution)/shard_map/ppermute | solution.py:989
  251.9 41.1 %collective-permute-start.22 = (bf16[256,3456]{1,0:T(8,128)(2,1)}, bf16[256,3456]{1,0:T(8,128)(2,1)}, u32[]{:S(2)}, u32[]{:S(2)}) collective-permute-start(bf16[256,3456]{1,0:T(8,128)(2,1)} %get-tuple-element.104), channel_id=1, source_target_pairs={{0,16},{1,9},{8,24},{9,1},{16,0},{17,25},{24,8},{25,17},{2,18},{3,... | collective-permute-start | bytes 5308424 | tf_op jit(solution)/shard_map/ppermute | solution.py:999
  263.4 37.0 %collective-permute-start.23 = (bf16[256,3456]{1,0:T(8,128)(2,1)}, bf16[256,3456]{1,0:T(8,128)(2,1)}, u32[]{:S(2)}, u32[]{:S(2)}) collective-permute-start(bf16[256,3456]{1,0:T(8,128)(2,1)} %get-tuple-element.105), channel_id=1, source_target_pairs={{0,16},{1,9},{8,24},{9,1},{16,0},{17,25},{24,8},{25,17},{2,18},{3,... | collective-permute-start | bytes 5308424 | tf_op jit(solution)/shard_map/ppermute | solution.py:999
  289.6 24.1 %collective-permute-start.21 = (bf16[512,3456]{1,0:T(8,128)(2,1)}, bf16[512,3456]{1,0:T(8,128)(2,1)}, u32[]{:S(2)}, u32[]{:S(2)}) collective-permute-start(bf16[512,3456]{1,0:T(8,128)(2,1)} %get-tuple-element.103), channel_id=1, source_target_pairs={{0,1},{1,0},{2,3},{3,2},{4,5},{5,4},{6,7},{7,6},{8,9},{9,8},{10,11... | collective-permute-start | bytes 10616840 | tf_op jit(solution)/shard_map/ppermute | solution.py:989
  303.0 22.3 %collective-permute-start.25 = (bf16[128,3456]{1,0:T(8,128)(2,1)}, bf16[128,3456]{1,0:T(8,128)(2,1)}, u32[]{:S(2)}, u32[]{:S(2)}) collective-permute-start(bf16[128,3456]{1,0:T(8,128)(2,1)} %add_convert_fusion.8.refs_7_), channel_id=1, source_target_pairs={{0,8},{1,17},{8,0},{9,25},{16,24},{17,1},{24,16},{25,9},{2,10},{3,... | collective-permute-start | bytes 2654216 | tf_op jit(solution)/shard_map/ppermute | solution.py:993
  309.7 49.1 %collective-permute-start.26 = (bf16[128,3456]{1,0:T(8,128)(2,1)S(1)}, bf16[128,3456]{1,0:T(8,128)(2,1)}, u32[]{:S(2)}, u32[]{:S(2)}) collective-permute-start(bf16[128,3456]{1,0:T(8,128)(2,1)S(1)} %add_convert_fusion.7.refs_17_), channel_id=1, source_target_pairs={{0,6},{2,0},{4,2},{6,4},{1,7},{3,1},{5,3},{7,5},{8,14},{10,8},{12,... | collective-permute-start | bytes 2654216 | tf_op jit(solution)/shard_map/ppermute | solution.py:1005
  323.8 32.5 %collective-permute-start.27 = (bf16[256,3456]{1,0:T(8,128)(2,1)}, bf16[256,3456]{1,0:T(8,128)(2,1)}, u32[]{:S(2)}, u32[]{:S(2)}) collective-permute-start(bf16[256,3456]{1,0:T(8,128)(2,1)} %get-tuple-element.110), channel_id=1, source_target_pairs={{0,16},{1,9},{8,24},{9,1},{16,0},{17,25},{24,8},{25,17},{2,18},{3,... | collective-permute-start | bytes 5308424 | tf_op jit(solution)/shard_map/ppermute | solution.py:999
  368.6 24.3 %collective-permute-start.28 = (bf16[512,4096]{1,0:T(8,128)(2,1)}, bf16[512,4096]{1,0:T(8,128)(2,1)}, u32[]{:S(2)}, u32[]{:S(2)}) collective-permute-start(bf16[512,4096]{1,0:T(8,128)(2,1)} %mix_weights.2), channel_id=1, source_target_pairs={{0,1},{1,0},{2,3},{3,2},{4,5},{5,4},{6,7},{7,6},{8,9},{9,8},{10,11... | collective-permute-start | bytes 12582920 | tf_op jit(solution)/shard_map/ppermute | solution.py:989
  369.7 23.2 %collective-permute-start.30 = (bf16[128,3456]{1,0:T(8,128)(2,1)S(1)}, bf16[128,3456]{1,0:T(8,128)(2,1)}, u32[]{:S(2)}, u32[]{:S(2)}) collective-permute-start(bf16[128,3456]{1,0:T(8,128)(2,1)S(1)} %copy-done.6), channel_id=1, source_target_pairs={{0,2},{2,4},{4,6},{6,0},{1,3},{3,5},{5,7},{7,1},{8,10},{10,12},{12... | collective-permute-start | bytes 2654216 | tf_op jit(solution)/shard_map/ppermute | solution.py:1005
  403.8 36.1 %collective-permute-start.33 = (bf16[256,4096]{1,0:T(8,128)(2,1)}, bf16[256,4096]{1,0:T(8,128)(2,1)}, u32[]{:S(2)}, u32[]{:S(2)}) collective-permute-start(bf16[256,4096]{1,0:T(8,128)(2,1)} %get-tuple-element.118), channel_id=1, source_target_pairs={{0,16},{1,9},{8,24},{9,1},{16,0},{17,25},{24,8},{25,17},{2,18},{3,... | collective-permute-start | bytes 6291464 | tf_op jit(solution)/shard_map/ppermute | solution.py:999
  407.8 40.1 %collective-permute-start.41 = (bf16[128,3456]{1,0:T(8,128)(2,1)}, bf16[128,3456]{1,0:T(8,128)(2,1)}, u32[]{:S(2)}, u32[]{:S(2)}) collective-permute-start(bf16[128,3456]{1,0:T(8,128)(2,1)} %add_convert_fusion.3), channel_id=1, source_target_pairs={{0,8},{1,17},{8,0},{9,25},{16,24},{17,1},{24,16},{25,9},{2,10},{3,... | collective-permute-start | bytes 2654216 | tf_op jit(solution)/shard_map/ppermute | solution.py:993
  408.4 39.5 %collective-permute-start.42 = (bf16[128,3456]{1,0:T(8,128)(2,1)S(1)}, bf16[128,3456]{1,0:T(8,128)(2,1)}, u32[]{:S(2)}, u32[]{:S(2)}) collective-permute-start(bf16[128,3456]{1,0:T(8,128)(2,1)S(1)} %copy-done.7), channel_id=1, source_target_pairs={{0,4},{2,6},{4,0},{6,2},{1,5},{3,7},{5,1},{7,3},{8,12},{10,14},{12... | collective-permute-start | bytes 2654216 | tf_op jit(solution)/shard_map/ppermute | solution.py:1005
  426.2 36.7 %collective-permute-start.32 = (bf16[1024,512]{1,0:T(8,128)(2,1)}, bf16[1024,512]{1,0:T(8,128)(2,1)}, u32[]{:S(2)}, u32[]{:S(2)}) collective-permute-start(bf16[1024,512]{1,0:T(8,128)(2,1)} %get-tuple-element.117), channel_id=1, source_target_pairs={{0,1},{1,0},{2,3},{3,2},{4,5},{5,4},{6,7},{7,6},{8,9},{9,8},{10,11... | collective-permute-start | bytes 3145736 | tf_op jit(solution)/shard_map/ppermute | solution.py:989
  466.5 26.4 %collective-permute-start.44 = (bf16[128,3456]{1,0:T(8,128)(2,1)}, bf16[128,3456]{1,0:T(8,128)(2,1)}, u32[]{:S(2)}, u32[]{:S(2)}) collective-permute-start(bf16[128,3456]{1,0:T(8,128)(2,1)} %add_convert_fusion.2.refs_0_), channel_id=1, source_target_pairs={{0,16},{1,9},{8,24},{9,1},{16,0},{17,25},{24,8},{25,17},{2,18},{3,... | collective-permute-start | bytes 2654216 | tf_op jit(solution)/shard_map/ppermute | solution.py:999
  469.6 23.4 %collective-permute-start.45 = (bf16[128,3456]{1,0:T(8,128)(2,1)}, bf16[128,3456]{1,0:T(8,128)(2,1)}, u32[]{:S(2)}, u32[]{:S(2)}) collective-permute-start(bf16[128,3456]{1,0:T(8,128)(2,1)} %collective-permute-done.43.refs_1_), channel_id=1, source_target_pairs={{0,16},{1,9},{8,24},{9,1},{16,0},{17,25},{24,8},{25,17},{2,18},{3,... | collective-permute-start | bytes 2654216 | tf_op jit(solution)/shard_map/ppermute | solution.py:999
  (43 other events, 456.0 us)
Sparse Core Ops, SparseCore 0:
  92.0 47.3 all-gather.5
  149.8 47.5 all-gather.7
  199.8 52.0 all-gather.9
  407.9 72.6 all-gather.11
